TPU v7x, 128 devices: a whole 4x4x4 slice. The times are simulated.
128 devices in a mesh: row: 16 (over y, z), col: 8 (over x, core).
Axes of the slice: x: 4, y: 4, z: 4, core: 2. Of those that a mesh axis runs over, the one named last changes fastest.
Arguments:
- coords: float32 [4, 3, 8, 16384], P(None, None, None, ('row', 'col')), may hold values from -6 to 6
- chrom_lengths: int32 [46], replicated, may hold values from 1 to 8192, 131072 in all
- band_counts: int32 [4, 8, 128, 32], P(None, None, ('row', 'col')), may hold values from 16 to 111
- inter_pairs: int32 [4, 4096, 2], replicated, may hold values from 0 to 1023, as said below
- inter_counts: int32 [4, 4096], replicated, may hold values from 16 to 111
Outputs:
- grad: float32 [4, 3, 8, 16384], P(None, None, None, ('row', 'col'))
Inputs may be any that keep to these rules, and one draw needn't show every extreme that they name: `inter_pairs`: every entry names two blocks of the structure. for every g in 0 to 15 and h in 0 to 7, at most 64 entries of one structure have (I mod 128) div 8 = g and J mod 8 = h, and one such (g, h) has exactly 64; the same holds with the roles of I and J exchanged.
All inputs are finite; a program needn't handle non-finite values.
Results may differ from a plain program's by a relative error of at most 0.0003.
Values sent between devices are 32-bit elements; how exact they have to be, the bound alone decides.
A program may use at most 64 MiB of HBM per device.

v0:
```python
import jax
import jax.numpy as jnp
from jax import lax
from jax.sharding import PartitionSpec as P

LIST_CAP = 64


CONTACT_SHIFT = 3.0
CONTACT_SLOPE = 0.5
BACKGROUND = 0.5


def chromosome(beads, chrom_ends):
    return jnp.sum((chrom_ends <= beads[..., None]).astype(jnp.int32), axis=-1)


def pair_tiles(
    first_points,
    second_points,
    left_chrom,
    right_chrom,
    first_bead,
    second_bead,
    relation,
    tile_valid,
    tile_counts,
):
    block_size = first_points.shape[3]
    difference = first_points[:, :, :, :, None] - second_points[:, :, :, None, :]
    distance = jnp.sum(difference * difference, axis=1)
    chance = jax.nn.sigmoid(CONTACT_SHIFT - CONTACT_SLOPE * distance)
    same_chrom = left_chrom[:, :, :, None] == right_chrom[:, :, None, :]
    pair_order = jnp.sign(second_bead[:, :, None, :] - first_bead[:, :, :, None])
    wanted = relation[:, :, None, None]
    pair_mask = jnp.where(
        wanted == 0, jnp.logical_not(same_chrom), same_chrom & (pair_order == wanted)
    )
    masked = chance * (pair_mask.astype(jnp.float32) * tile_valid[:, :, None, None])
    expect = BACKGROUND + jnp.sum(masked, axis=(2, 3)) / block_size
    weight = 1.0 - tile_counts.astype(jnp.float32) / expect
    factor = (
        -2.0 * CONTACT_SLOPE / block_size * (masked * (1.0 - chance)) * weight[:, :, None, None]
    )
    pair_force = factor[:, None] * difference
    return (jnp.sum(pair_force, axis=4), -jnp.sum(pair_force, axis=3))


def on_device(coords, chrom_lengths, band_counts, inter_pairs, inter_counts):
    row_count = lax.axis_size("row")
    column_count = lax.axis_size("col")
    groups = row_count * column_count
    row_here = lax.axis_index("row")
    column_here = lax.axis_index("col")
    structures, _, sweeps, block_size = coords.shape
    band_reach = band_counts.shape[3] - 1
    column_steps = band_reach // column_count + 1
    chrom_ends = jnp.cumsum(chrom_lengths)
    beads_in = jnp.arange(block_size, dtype=jnp.int32)
    local_points = coords[:, :, None]
    local_counts = jnp.transpose(band_counts, (0, 2, 1, 3))
    row_points, row_counts = (
        lax.all_gather(local_points, "col", axis=2, tiled=True),
        lax.all_gather(local_counts, "col", axis=1, tiled=True),
    )
    column_points = lax.all_gather(local_points, "row", axis=2, tiled=True)
    row_flat = row_points.reshape(structures, 3, column_count * sweeps, block_size)
    column_flat = column_points.reshape(structures, 3, row_count * sweeps, block_size)
    column_slot = jnp.repeat(jnp.arange(column_count, dtype=jnp.int32), column_steps)
    step_slot = jnp.tile(jnp.arange(column_steps, dtype=jnp.int32), column_count)
    tile_total = column_slot.shape[0]
    up_gap = (column_here - column_slot) % column_count + step_slot * column_count
    up_pos = row_here * column_count + column_slot + up_gap
    up_shift = up_pos // groups
    up_row = up_pos % groups // column_count
    targets = jnp.arange(row_count * sweeps, dtype=jnp.int32)
    upward = jnp.ones((1, tile_total), jnp.int32)

    def sweep(column_total, sweep_turn):
        base_block = sweep_turn * groups + row_here * column_count + column_slot
        first_bead = base_block[:, None] * block_size + beads_in[None, :]
        left_chrom = chromosome(first_bead, chrom_ends)
        here_points = lax.dynamic_index_in_dim(row_points, sweep_turn, 3, keepdims=False)
        first_points = jnp.take(here_points, column_slot, axis=2)
        here_counts = lax.dynamic_index_in_dim(row_counts, sweep_turn, 2, keepdims=False)
        up_turn = sweep_turn + up_shift
        up_valid = (up_gap <= band_reach) & (up_turn < sweeps)
        up_index = up_row * sweeps + jnp.minimum(up_turn, sweeps - 1)
        second_points = jnp.take(column_flat, up_index, axis=2)
        second_bead = first_bead + up_gap[:, None] * block_size
        right_chrom = chromosome(second_bead, chrom_ends)
        tile_counts = here_counts[:, column_slot, jnp.minimum(up_gap, band_reach)]
        row_gain, column_gain = pair_tiles(
            first_points,
            second_points,
            left_chrom[None],
            right_chrom[None],
            first_bead[None],
            second_bead[None],
            upward,
            up_valid.astype(jnp.float32)[None],
            tile_counts,
        )
        rows_now = row_gain.reshape(structures, 3, column_count, column_steps, block_size).sum(3)
        placement = ((targets[None, :] == up_index[:, None]) & up_valid[:, None]).astype(
            jnp.float32
        )
        column_total = column_total + jnp.einsum(
            "sctb,tu->scub", column_gain, placement, precision=lax.Precision.HIGHEST
        )
        return (column_total, rows_now)

    column_total = jnp.zeros((structures, 3, row_count * sweeps, block_size), jnp.float32)
    column_total, rows_stack = lax.scan(sweep, column_total, jnp.arange(sweeps, dtype=jnp.int32))
    row_total = jnp.transpose(rows_stack, (1, 2, 3, 0, 4))
    first_blocks = inter_pairs[:, :, 0]
    second_blocks = inter_pairs[:, :, 1]
    entry_total = inter_pairs.shape[1]
    row_slots = jnp.arange(column_count * sweeps, dtype=jnp.int32)
    owned_tiles = (first_blocks % groups // column_count == row_here) & (
        second_blocks % column_count == column_here
    )
    entry_score = jnp.where(
        owned_tiles, entry_total - jnp.arange(entry_total, dtype=jnp.int32)[None, :], -1
    )
    top_score, picked = lax.top_k(entry_score, LIST_CAP)
    tile_valid = (top_score >= 0).astype(jnp.float32)
    first_block = jnp.take_along_axis(first_blocks, picked, axis=1)
    second_block = jnp.take_along_axis(second_blocks, picked, axis=1)
    tile_counts = jnp.take_along_axis(inter_counts, picked, axis=1)
    first_index = first_block % column_count * sweeps + first_block // groups
    second_index = second_block % groups // column_count * sweeps + second_block // groups
    first_points = jax.vmap(lambda points, indices: jnp.take(points, indices, axis=1))(
        row_flat, first_index
    )
    second_points = jax.vmap(lambda points, indices: jnp.take(points, indices, axis=1))(
        column_flat, second_index
    )
    first_bead = first_block[:, :, None] * block_size + beads_in
    second_bead = second_block[:, :, None] * block_size + beads_in
    row_gain, column_gain = pair_tiles(
        first_points,
        second_points,
        chromosome(first_bead, chrom_ends),
        chromosome(second_bead, chrom_ends),
        first_bead,
        second_bead,
        jnp.zeros_like(picked),
        tile_valid,
        tile_counts,
    )
    row_place = (row_slots[None, None, :] == first_index[:, :, None]).astype(jnp.float32)
    column_place = (targets[None, None, :] == second_index[:, :, None]).astype(jnp.float32)
    row_gain, column_gain, row_place, column_place = (
        row_gain,
        column_gain,
        row_place,
        column_place,
    )
    row_extra = jnp.einsum("sctb,stu->scub", row_gain, row_place, precision=lax.Precision.HIGHEST)
    column_total = column_total + jnp.einsum(
        "sctb,stu->scub", column_gain, column_place, precision=lax.Precision.HIGHEST
    )
    row_total = row_total + row_extra.reshape(structures, 3, column_count, sweeps, block_size)
    owned_rows = lax.psum_scatter(row_total, "col", scatter_dimension=2, tiled=True)
    result = owned_rows + lax.psum_scatter(
        column_total.reshape(structures, 3, row_count, sweeps, block_size),
        "row",
        scatter_dimension=2,
        tiled=True,
    )
    return result[:, :, 0]


def solution(mesh):
    placed = (
        P(None, None, None, ("row", "col")),
        P(),
        P(None, None, ("row", "col"), None),
        P(),
        P(),
    )
    return jax.shard_map(
        on_device,
        mesh=mesh,
        in_specs=placed,
        out_specs=P(None, None, None, ("row", "col")),
        check_vma=False,
    )
```

profile of v0, /device:TPU:1, one launch (start us, length us, event | category | flops | bytes accessed | tf_op | source)
XLA Modules:
  0.0 696.6 jit_solution(18318625419140526425)
XLA Ops:
  10.1 14.8 %all-gather = f32[4,3,64,128]{3,1,2,0:T(4,128)S(1)} all-gather(f32[4,3,8,128]{3,1,2,0:T(4,128)S(1)} %copy.68), channel_id=2, replica_groups=mesh['row'=16,'col'=8] {'col'}, dimensions={2}, use_global_device_ids=true | all-gather | bytes 442368 | tf_op jit(solution)/shard_map/all_gather | solution.py:63
  24.9 21.4 %all-gather.1 = f32[4,3,128,128]{3,1,2,0:T(4,128)S(1)} all-gather(f32[4,3,8,128]{3,1,2,0:T(4,128)S(1)} %copy.68), channel_id=3, replica_groups=mesh['row'=16,'col'=8] {'row'}, dimensions={2}, use_global_device_ids=true | all-gather | bytes 835584 | tf_op jit(solution)/shard_map/all_gather | solution.py:66
  47.2 19.6 %all-gather.2 = s32[4,64,1,32]{3,1,0,2:T(8,128)} all-gather(s32[4,8,1,32]{3,1,0,2:T(8,128)} %bitcast.127), channel_id=4, replica_groups=mesh['row'=16,'col'=8] {'col'}, dimensions={1}, use_global_device_ids=true | all-gather | bytes 36864 | tf_op jit(solution)/shard_map/all_gather | solution.py:64
  69.2 421.9 %while.19 = (s32[]{:T(128)}, f32[4,3,128,128]{3,2,1,0:T(8,128)S(1)}, f32[8,4,3,8,128]{4,0,2,1,3:T(8,128)}, s32[8]{0:T(128)S(1)}, f32[4,3,8,8,128]{4,0,2,1,3:T(4,...) while((s32[]{:T(128)}, ...), condition=%wide.region_9.10_spmd.clone.clone.clone.clone, body=%wide.region_1.9_spmd.clone.clone.clone.clone.sunk | while | flops 155764096 | bytes 54283132 | solution.py:114
  80.3 11.6 %fusion.89 = f32[4,32,128,128]{3,2,1,0:T(8,128)} fusion(f32[4,3,32,128]{3,2,1,0:T(8,128)S(1)} %copy.107, f32[4,3,32,128]{3,2,1,0:T(8,128)S(1)} %copy.108), kind=kLoop, calls=%fused_computation.17.clone.1 | loop fusion | flops 16777216 | bytes 8781824 | tf_op jit(solution)/shard_map/while/body/eval_jaxpr/reduce_sum | solution.py:31
  91.9 5.4 multiply_reduce_fusion.2
  97.4 5.0 multiply_multiply_fusion.3
  102.4 15.9 %fusion.90 = (f32[4,3,32,128]{3,2,1,0:T(8,128)S(1)}, f32[4,3,32,128]{3,2,1,0:T(8,128)S(1)}) fusion(f32[4,32,128,128]{3,2,1,0:T(8,128)S(1)} %multiply_multiply_fusion.3, f32[4,3,32,128]{3,2,1,0:T(8,128)S(1)} %copy.107, f32[4,3,32,128]{3,2,1,0:T(8,128)S(1)} %copy.108), kind=kLoop, calls=%fused_computation.15.clone.1 | loop fusion | flops 25067520 | bytes 9175040 | tf_op jit(solution)/shard_map/while/body/eval_jaxpr/reduce_sum | solution.py:46
  118.5 2.8 dynamic_update_slice.12
  133.0 11.6 %fusion.89 = f32[4,32,128,128]{3,2,1,0:T(8,128)} fusion(f32[4,3,32,128]{3,2,1,0:T(8,128)S(1)} %copy.107, f32[4,3,32,128]{3,2,1,0:T(8,128)S(1)} %copy.108), kind=kLoop, calls=%fused_computation.17.clone.1 | loop fusion | flops 16777216 | bytes 8781824 | tf_op jit(solution)/shard_map/while/body/eval_jaxpr/reduce_sum | solution.py:31
  144.6 5.4 multiply_reduce_fusion.2
  150.1 5.0 multiply_multiply_fusion.3
  155.1 15.9 %fusion.90 = (f32[4,3,32,128]{3,2,1,0:T(8,128)S(1)}, f32[4,3,32,128]{3,2,1,0:T(8,128)S(1)}) fusion(f32[4,32,128,128]{3,2,1,0:T(8,128)S(1)} %multiply_multiply_fusion.3, f32[4,3,32,128]{3,2,1,0:T(8,128)S(1)} %copy.107, f32[4,3,32,128]{3,2,1,0:T(8,128)S(1)} %copy.108), kind=kLoop, calls=%fused_computation.15.clone.1 | loop fusion | flops 25067520 | bytes 9175040 | tf_op jit(solution)/shard_map/while/body/eval_jaxpr/reduce_sum | solution.py:46
  171.2 2.8 dynamic_update_slice.12
  185.8 11.6 %fusion.89 = f32[4,32,128,128]{3,2,1,0:T(8,128)} fusion(f32[4,3,32,128]{3,2,1,0:T(8,128)S(1)} %copy.107, f32[4,3,32,128]{3,2,1,0:T(8,128)S(1)} %copy.108), kind=kLoop, calls=%fused_computation.17.clone.1 | loop fusion | flops 16777216 | bytes 8781824 | tf_op jit(solution)/shard_map/while/body/eval_jaxpr/reduce_sum | solution.py:31
  197.4 5.4 multiply_reduce_fusion.2
  202.8 5.0 multiply_multiply_fusion.3
  207.9 15.9 %fusion.90 = (f32[4,3,32,128]{3,2,1,0:T(8,128)S(1)}, f32[4,3,32,128]{3,2,1,0:T(8,128)S(1)}) fusion(f32[4,32,128,128]{3,2,1,0:T(8,128)S(1)} %multiply_multiply_fusion.3, f32[4,3,32,128]{3,2,1,0:T(8,128)S(1)} %copy.107, f32[4,3,32,128]{3,2,1,0:T(8,128)S(1)} %copy.108), kind=kLoop, calls=%fused_computation.15.clone.1 | loop fusion | flops 25067520 | bytes 9175040 | tf_op jit(solution)/shard_map/while/body/eval_jaxpr/reduce_sum | solution.py:46
  223.9 2.8 dynamic_update_slice.12
  238.5 11.6 %fusion.89 = f32[4,32,128,128]{3,2,1,0:T(8,128)} fusion(f32[4,3,32,128]{3,2,1,0:T(8,128)S(1)} %copy.107, f32[4,3,32,128]{3,2,1,0:T(8,128)S(1)} %copy.108), kind=kLoop, calls=%fused_computation.17.clone.1 | loop fusion | flops 16777216 | bytes 8781824 | tf_op jit(solution)/shard_map/while/body/eval_jaxpr/reduce_sum | solution.py:31
  250.1 5.4 multiply_reduce_fusion.2
  255.6 5.0 multiply_multiply_fusion.3
  260.6 15.9 %fusion.90 = (f32[4,3,32,128]{3,2,1,0:T(8,128)S(1)}, f32[4,3,32,128]{3,2,1,0:T(8,128)S(1)}) fusion(f32[4,32,128,128]{3,2,1,0:T(8,128)S(1)} %multiply_multiply_fusion.3, f32[4,3,32,128]{3,2,1,0:T(8,128)S(1)} %copy.107, f32[4,3,32,128]{3,2,1,0:T(8,128)S(1)} %copy.108), kind=kLoop, calls=%fused_computation.15.clone.1 | loop fusion | flops 25067520 | bytes 9175040 | tf_op jit(solution)/shard_map/while/body/eval_jaxpr/reduce_sum | solution.py:46
  291.3 11.6 %fusion.89 = f32[4,32,128,128]{3,2,1,0:T(8,128)} fusion(f32[4,3,32,128]{3,2,1,0:T(8,128)S(1)} %copy.107, f32[4,3,32,128]{3,2,1,0:T(8,128)S(1)} %copy.108), kind=kLoop, calls=%fused_computation.17.clone.1 | loop fusion | flops 16777216 | bytes 8781824 | tf_op jit(solution)/shard_map/while/body/eval_jaxpr/reduce_sum | solution.py:31
  302.9 5.4 multiply_reduce_fusion.2
  308.3 5.0 multiply_multiply_fusion.3
  313.4 15.9 %fusion.90 = (f32[4,3,32,128]{3,2,1,0:T(8,128)S(1)}, f32[4,3,32,128]{3,2,1,0:T(8,128)S(1)}) fusion(f32[4,32,128,128]{3,2,1,0:T(8,128)S(1)} %multiply_multiply_fusion.3, f32[4,3,32,128]{3,2,1,0:T(8,128)S(1)} %copy.107, f32[4,3,32,128]{3,2,1,0:T(8,128)S(1)} %copy.108), kind=kLoop, calls=%fused_computation.15.clone.1 | loop fusion | flops 25067520 | bytes 9175040 | tf_op jit(solution)/shard_map/while/body/eval_jaxpr/reduce_sum | solution.py:46
  329.4 2.8 dynamic_update_slice.12
  344.0 11.6 %fusion.89 = f32[4,32,128,128]{3,2,1,0:T(8,128)} fusion(f32[4,3,32,128]{3,2,1,0:T(8,128)S(1)} %copy.107, f32[4,3,32,128]{3,2,1,0:T(8,128)S(1)} %copy.108), kind=kLoop, calls=%fused_computation.17.clone.1 | loop fusion | flops 16777216 | bytes 8781824 | tf_op jit(solution)/shard_map/while/body/eval_jaxpr/reduce_sum | solution.py:31
  355.6 5.4 multiply_reduce_fusion.2
  361.1 5.0 multiply_multiply_fusion.3
  366.1 15.9 %fusion.90 = (f32[4,3,32,128]{3,2,1,0:T(8,128)S(1)}, f32[4,3,32,128]{3,2,1,0:T(8,128)S(1)}) fusion(f32[4,32,128,128]{3,2,1,0:T(8,128)S(1)} %multiply_multiply_fusion.3, f32[4,3,32,128]{3,2,1,0:T(8,128)S(1)} %copy.107, f32[4,3,32,128]{3,2,1,0:T(8,128)S(1)} %copy.108), kind=kLoop, calls=%fused_computation.15.clone.1 | loop fusion | flops 25067520 | bytes 9175040 | tf_op jit(solution)/shard_map/while/body/eval_jaxpr/reduce_sum | solution.py:46
  396.7 11.6 %fusion.89 = f32[4,32,128,128]{3,2,1,0:T(8,128)} fusion(f32[4,3,32,128]{3,2,1,0:T(8,128)S(1)} %copy.107, f32[4,3,32,128]{3,2,1,0:T(8,128)S(1)} %copy.108), kind=kLoop, calls=%fused_computation.17.clone.1 | loop fusion | flops 16777216 | bytes 8781824 | tf_op jit(solution)/shard_map/while/body/eval_jaxpr/reduce_sum | solution.py:31
  408.3 5.4 multiply_reduce_fusion.2
  413.8 5.0 multiply_multiply_fusion.3
  418.8 15.9 %fusion.90 = (f32[4,3,32,128]{3,2,1,0:T(8,128)S(1)}, f32[4,3,32,128]{3,2,1,0:T(8,128)S(1)}) fusion(f32[4,32,128,128]{3,2,1,0:T(8,128)S(1)} %multiply_multiply_fusion.3, f32[4,3,32,128]{3,2,1,0:T(8,128)S(1)} %copy.107, f32[4,3,32,128]{3,2,1,0:T(8,128)S(1)} %copy.108), kind=kLoop, calls=%fused_computation.15.clone.1 | loop fusion | flops 25067520 | bytes 9175040 | tf_op jit(solution)/shard_map/while/body/eval_jaxpr/reduce_sum | solution.py:46
  434.9 2.8 dynamic_update_slice.12
  449.5 11.6 %fusion.89 = f32[4,32,128,128]{3,2,1,0:T(8,128)} fusion(f32[4,3,32,128]{3,2,1,0:T(8,128)S(1)} %copy.107, f32[4,3,32,128]{3,2,1,0:T(8,128)S(1)} %copy.108), kind=kLoop, calls=%fused_computation.17.clone.1 | loop fusion | flops 16777216 | bytes 8781824 | tf_op jit(solution)/shard_map/while/body/eval_jaxpr/reduce_sum | solution.py:31
  461.1 5.4 multiply_reduce_fusion.2
  466.5 5.0 multiply_multiply_fusion.3
  471.6 15.9 %fusion.90 = (f32[4,3,32,128]{3,2,1,0:T(8,128)S(1)}, f32[4,3,32,128]{3,2,1,0:T(8,128)S(1)}) fusion(f32[4,32,128,128]{3,2,1,0:T(8,128)S(1)} %multiply_multiply_fusion.3, f32[4,3,32,128]{3,2,1,0:T(8,128)S(1)} %copy.107, f32[4,3,32,128]{3,2,1,0:T(8,128)S(1)} %copy.108), kind=kLoop, calls=%fused_computation.15.clone.1 | loop fusion | flops 25067520 | bytes 9175040 | tf_op jit(solution)/shard_map/while/body/eval_jaxpr/reduce_sum | solution.py:46
  487.6 2.8 dynamic_update_slice.12
  508.1 22.3 %fusion.35 = f32[4,64,128,128]{3,2,1,0:T(8,128)} fusion(f32[4,3,64,128]{3,2,1,0:T(8,128)S(1)} %copy.78, f32[4,3,64,128]{3,2,1,0:T(8,128)S(1)} %copy.77), kind=kLoop, calls=%fused_computation.83 | loop fusion | flops 33554432 | bytes 17563648 | tf_op jit(solution)/shard_map/reduce_sum | solution.py:31
  530.4 10.6 %fusion.36 = f32[4,64]{1,0:T(4,128)S(1)} fusion(f32[4,64]{1,0:T(4,128)S(1)} %fusion.64, s32[4,64,128]{2,1,0:T(8,128)S(1)} %get-tuple-element.420, s32[4,64,128]{2,1,0:T(8,128)S(1)} %get-tuple-element.419, f32[4,64,128,128]{3,2,1,0:T(8,128)} %fusion.35), kind=kLoop, calls=%fused_computation.86 | loop fusion | flops 37748480 | bytes 17041408 | tf_op jit(solution)/shard_map/reduce_sum | solution.py:40
  541.2 9.7 %multiply_multiply_fusion.1 = f32[4,64,128,128]{3,2,1,0:T(8,128)S(1)} fusion(f32[4,64]{1,0:T(4,128)S(1)} %subtract_multiply_fusion.5, f32[4,64]{1,0:T(4,128)S(1)} %fusion.64, s32[4,64,128]{2,1,0:T(8,128)} %copy-done.6, s32[4,64,128]{2,1,0:T(8,128)} %copy-done.5, f32[4,64,128,128]{3,2,1,0:T(8,128)S(1)} %copy-done.1), kind=kLoop, calls=%fused_computation.84 | loop fusion | flops 46137344 | bytes 33818624 | tf_op jit(solution)/shard_map/mul | solution.py:43
  550.9 33.4 %fusion.33 = (f32[4,3,64,128]{3,2,1,0:T(8,128)}, f32[4,3,64,128]{3,2,1,0:T(8,128)S(1)}) fusion(f32[4,64,128,128]{3,2,1,0:T(8,128)S(1)} %multiply_multiply_fusion.1, f32[4,3,64,128]{3,2,1,0:T(8,128)} %copy-done.4, f32[4,3,64,128]{3,2,1,0:T(8,128)} %copy-done.3), kind=kLoop, calls=%fused_computation.81 | loop fusion | flops 50135040 | bytes 18350080 | tf_op jit(solution)/shard_map/reduce_sum | solution.py:46
  588.5 23.4 %reduce-scatter.5.cloned.1.call-done = f32[4,3,1,8,128]{4,3,1,0,2:T(8,128)} async-done(((f32[4,3,8,8,128]{4,3,1,0,2:T(8,128)}), f32[4,3,1,8,128]{4,3,1,0,2:T(8,128)}) %reduce-scatter.5.cloned.1.call-update) | async-done | bytes 49168 | tf_op jit(solution)/shard_map/reduce_scatter | solution.py:165
  611.9 76.7 %reduce-scatter.7.cloned.1.call-done = f32[4,3,1,8,128]{4,3,1,0,2:T(8,128)} async-done(((f32[4,3,16,8,128]{4,3,1,0,2:T(8,128)}), f32[4,3,1,8,128]{4,3,1,0,2:T(8,128)}) %reduce-scatter.7.cloned.1.call-update) | async-done | bytes 49168
  (326 shorter events, 109.8 us)
Async XLA Ops:
  6.5 492.1 %copy-start = (s32[4,4096]{1,0:T(4,128)S(1)}, s32[4,4096]{1,0:T(4,128)}, u32[]{:S(2)}) copy-start(s32[4,4096]{1,0:T(4,128)} %param.13) | copy-start | bytes 196612
  6.5 484.7 %top_k.31.cloned.1.call-start = ((), (), s32[]{:S(2)}) async-start(), calls=%async_computation.4 | async-start | bytes 393248 | tf_op jit(solution)/shard_map/top_k | solution.py:126
  9.2 602.7 %reduce-scatter.5.cloned.1.call-start = ((), (), s32[]{:S(2)}) async-start(), calls=%async_computation.2 | async-start | bytes 442368 | tf_op jit(solution)/shard_map/reduce_scatter | solution.py:165
  491.2 49.9 %copy-start.2 = (f32[4,3,128,128]{3,2,1,0:T(8,128)}, f32[4,3,128,128]{3,2,1,0:T(8,128)S(1)}, u32[]{:S(2)}) copy-start(f32[4,3,128,128]{3,2,1,0:T(8,128)S(1)} %get-tuple-element.220) | copy-start | bytes 2359300
  504.1 37.0 %copy-start.3 = (f32[4,3,64,128]{3,2,1,0:T(8,128)}, f32[4,3,64,128]{3,2,1,0:T(8,128)S(1)}, u32[]{:S(2)}) copy-start(f32[4,3,64,128]{3,2,1,0:T(8,128)S(1)} %copy.77) | copy-start | bytes 1179652
  505.8 35.3 %copy-start.4 = (f32[4,3,64,128]{3,2,1,0:T(8,128)}, f32[4,3,64,128]{3,2,1,0:T(8,128)S(1)}, u32[]{:S(2)}) copy-start(f32[4,3,64,128]{3,2,1,0:T(8,128)S(1)} %copy.78) | copy-start | bytes 1179652
  508.1 33.0 %copy-start.5 = (s32[4,64,128]{2,1,0:T(8,128)}, s32[4,64,128]{2,1,0:T(8,128)S(1)}, u32[]{:S(2)}) copy-start(s32[4,64,128]{2,1,0:T(8,128)S(1)} %get-tuple-element.419) | copy-start | bytes 393220
  508.1 33.0 %copy-start.6 = (s32[4,64,128]{2,1,0:T(8,128)}, s32[4,64,128]{2,1,0:T(8,128)S(1)}, u32[]{:S(2)}) copy-start(s32[4,64,128]{2,1,0:T(8,128)S(1)} %get-tuple-element.420) | copy-start | bytes 393220
  530.4 10.8 %copy-start.1 = (f32[4,64,128,128]{3,2,1,0:T(8,128)S(1)}, f32[4,64,128,128]{3,2,1,0:T(8,128)}, u32[]{:S(2)}) copy-start(f32[4,64,128,128]{3,2,1,0:T(8,128)} %fusion.35) | copy-start | bytes 50331652
  550.9 33.8 %copy-start.7 = (f32[8,4,3,8,128]{4,0,2,1,3:T(8,128)S(1)}, f32[8,4,3,8,128]{4,0,2,1,3:T(8,128)}, u32[]{:S(2)}) copy-start(f32[8,4,3,8,128]{4,0,2,1,3:T(8,128)} %get-tuple-element.217) | copy-start | bytes 1179652
  585.5 103.0 %reduce-scatter.7.cloned.1.call-start = ((), (), s32[]{:S(2)}) async-start(), calls=%async_computation.3 | async-start | bytes 835584
Sparse Core Ops, SparseCore 0:
  9.8 7.2 top_k.33.cloned.1.call-done
  585.7 26.1 reduce-scatter.4
  615.0 73.4 reduce-scatter.6
  (1 shorter events, 0.0 us)
where the time goes:
time: 700 us; the launch traced here: 697 us
  other arithmetic  409 us (58%)
  waiting for transfers between devices  100 us (14%)
  local copies, waits for them, and re-layouts  89.2 us (13%)
  blocking collectives  55.8 us (8%)
  loops' own time  21.3 us (3%)
  between operations  13.4 us (2%)
  matrix products  8.08 us (1%)
    reduce_sum x9, other arithmetic, pair_tiles(): return (jnp.sum(pair_force, axis=4), -jnp.sum(pair_force, axis=3))  160 us
    reduce_sum x9, other arithmetic, pair_tiles(): distance = jnp.sum(difference * difference, axis=1)  115 us
    unnamed x3, waiting for transfers between devices  76.8 us
    reduce_sum x9, other arithmetic, pair_tiles(): expect = BACKGROUND + jnp.sum(masked, axis=(2, 3)) / block_size  54.2 us
    mul x18, other arithmetic, pair_tiles(): -2.0 * CONTACT_SLOPE / block_size * (masked * (1.0 - chance))  50 us
    reduce_scatter x1, waiting for transfers between devices, on_device(): lax.psum_scatter(row_total, 'col', scatter_dimension=2, tiled=True)  23.4 us
    dynamic_update_slice x16, local copies, waits for them, and re-layouts, on_device(): lax.scan(sweep, column_total, jnp.arange(sweeps, dtype=jnp.int32))  22.6 us
    all_gather x1, blocking collectives, on_device(): column_points = lax.all_gather(local_points, 'row', axis=2, tiled=True)  21.4 us
  transfers between devices with their start and end apart: 2, of which 2 were waited for; matrix products, arithmetic and copies ran while one was open for 0% of the time, Pallas kernels for 0%

commit v1 on v0

v1 whole, which is shorter than its diff:
```python
import functools

import jax
import jax.numpy as jnp
from jax import lax
from jax.experimental import pallas as pl
from jax.experimental.pallas import tpu as pltpu
from jax.sharding import PartitionSpec as P

MESH = pl.DeviceIdType.MESH
ROWS, COLS = 16, 8
S, U, BEADS = 4, 8, 128
CAP = 64
LABELS = 48
NR, NC = COLS * U, ROWS * U
PAD = 4
BIG = 64.0
F32, BF16, I32 = jnp.float32, jnp.bfloat16, jnp.int32
ANY = pl.BlockSpec(memory_space=pl.ANY)
VMEM = pl.BlockSpec(memory_space=pltpu.VMEM)
SMEM = pl.BlockSpec(memory_space=pltpu.SMEM)
NT = (((1,), (1,)), ((), ()))


def iota(shape, axis):
    return lax.broadcasted_iota(I32, shape, axis)


def chrom_bounds(lens_ref):
    lens = jnp.broadcast_to(lens_ref[...], (LABELS, lens_ref.shape[1]))
    sub, lane = iota(lens.shape, 0), iota(lens.shape, 1)
    ends = jnp.sum(jnp.where(lane <= sub, lens, 0), axis=1, keepdims=True)
    starts = jnp.sum(jnp.where(lane < sub, lens, 0), axis=1, keepdims=True)
    return starts, ends


def list_kernel(me_ref, lens_ref, first_ref, second_ref, count_ref, out_ref):
    row, col = me_ref[0], me_ref[1]
    first, second, counts = first_ref[...], second_ref[...], count_ref[...]
    mine = (((first & 127) >> 3) == row) & ((second & 7) == col)
    mask = mine.astype(F32).astype(BF16)
    a, b = iota((128, 128), 0), iota((128, 128), 1)
    upper = (a <= b).astype(F32).astype(BF16)
    within = jnp.dot(mask, upper, preferred_element_type=F32)
    total = jnp.dot(mask, jnp.ones((128, 128), BF16), preferred_element_type=F32)
    lower = ((b < a) & ((a >> 5) == (b >> 5))).astype(F32).astype(BF16)
    offset = jnp.dot(lower, total.astype(BF16), preferred_element_type=F32)
    place = jnp.where(mine, (offset + within).astype(I32) - 1, -1)
    row_at = (first & 7) * U + (first >> 7)
    values = [row_at, second >> 3, counts, mine.astype(I32)]
    values = [v.astype(F32) for v in values]
    slots = iota((CAP, 128), 0)
    for s in range(S):
        acc = jnp.zeros((16, CAP), F32)
        for t in range(32):
            e = s * 32 + t
            hot = (place[e:e + 1] == slots).astype(F32).astype(BF16)
            rows = [v[e:e + 1] for v in values] + [jnp.zeros((12, 128), F32)]
            rows = jnp.concatenate(rows, axis=0).astype(BF16)
            acc = acc + lax.dot_general(rows, hot, NT, preferred_element_type=F32)
        out_ref[s * 8:s * 8 + 8, 0:CAP] = acc[0:8].astype(I32)
        amount = jnp.sum(acc[3:4], axis=1, keepdims=True).astype(I32)
        out_ref[s * 8 + 4:s * 8 + 5, :] = jnp.broadcast_to(amount, (1, 128))
    starts, ends = chrom_bounds(lens_ref)
    lane = iota((1, 128), 1)
    block = (lane & 7) * 128 + row * 8 + ((lane >> 3) & 7)
    last = jnp.broadcast_to(block * 128 + 127, (LABELS, 128))
    stop = jnp.min(jnp.where(ends > last, ends, 1 << 20), axis=0, keepdims=True)
    gap = (col - ((lane >> 3) & 7)) & 7
    far = jnp.minimum(jnp.minimum((stop - 1) >> 7, block + 31), 1023)
    width = ((far - block - gap) >> 3) + 1
    out_ref[32:40, :] = jnp.broadcast_to(jnp.clip(width, 0, 4), (8, 128))


def gather_kernel(coords, counts, rows, cols, tallies, send, recv):
    r, c = lax.axis_index("row"), lax.axis_index("col")
    barrier = pltpu.get_barrier_semaphore()
    for d in range(1, COLS):
        pl.semaphore_signal(barrier, 1, device_id=(r, lax.rem(c + d, COLS)), device_id_type=MESH)
    for d in range(1, ROWS):
        pl.semaphore_signal(barrier, 1, device_id=(lax.rem(r + d, ROWS), c), device_id_type=MESH)
    pl.semaphore_wait(barrier, COLS + ROWS - 2)
    copies = []
    for d in range(1, ROWS):
        copies.append(pltpu.make_async_remote_copy(
            coords, cols.at[r], send.at[d], recv.at[d],
            device_id=(lax.rem(r + d, ROWS), c), device_id_type=MESH))
    for d in range(1, COLS):
        peer = (r, lax.rem(c + d, COLS))
        copies.append(pltpu.make_async_remote_copy(
            coords, rows.at[c], send.at[ROWS + d], recv.at[ROWS + d],
            device_id=peer, device_id_type=MESH))
        copies.append(pltpu.make_async_remote_copy(
            counts, tallies.at[c], send.at[ROWS + COLS + d], recv.at[ROWS + COLS + d],
            device_id=peer, device_id_type=MESH))
    for copy in copies:
        copy.start()
    for copy in copies:
        copy.wait()


def scatter_kernel(rows, cols, out, land, own, send, recv, local):
    r, c = lax.axis_index("row"), lax.axis_index("col")
    first = pltpu.make_async_copy(rows.at[c], own.at[0], local.at[0])
    second = pltpu.make_async_copy(cols.at[r], own.at[1], local.at[1])
    first.start()
    second.start()
    barrier = pltpu.get_barrier_semaphore()
    for d in range(1, COLS):
        pl.semaphore_signal(barrier, 1, device_id=(r, lax.rem(c + d, COLS)), device_id_type=MESH)
    for d in range(1, ROWS):
        pl.semaphore_signal(barrier, 1, device_id=(lax.rem(r + d, ROWS), c), device_id_type=MESH)
    pl.semaphore_wait(barrier, COLS + ROWS - 2)
    copies = []
    for d in range(1, ROWS):
        to = lax.rem(r + d, ROWS)
        copies.append(pltpu.make_async_remote_copy(
            cols.at[to], land.at[d - 1], send.at[d], recv.at[d],
            device_id=(to, c), device_id_type=MESH))
    for d in range(1, COLS):
        to = lax.rem(c + d, COLS)
        copies.append(pltpu.make_async_remote_copy(
            rows.at[to], land.at[ROWS - 2 + d], send.at[ROWS + d], recv.at[ROWS + d],
            device_id=(r, to), device_id_type=MESH))
    for copy in copies:
        copy.start()
    first.wait()
    second.wait()
    for copy in copies:
        copy.wait()
    for s in range(S):
        total = own[0, s] + own[1, s]
        for d in range(ROWS + COLS - 2):
            total = total + land[d, s]
        out[s] = total


def split3(x):
    a = x.astype(BF16).astype(F32)
    b = (x - a).astype(BF16).astype(F32)
    return a, b, (x - a) - b


def points_of(x, y, z):
    c = 0.75 - 0.25 * (x * x + y * y + z * z)
    return split3(x), split3(y), split3(z), split3(c)


def pair_kernel(me_ref, list_ref, tally_ref, count_ref, lens_ref, coords_ref, rows_ref, cols_ref,
                prow_ref, pcol_ref,
                tile_ref, left_ref, lrow_ref, right_ref, same_ref, differ_ref,
                sum_ref, num_ref, gcol_ref, grow_ref, lsum_ref, lnum_ref, lgcol_ref, lgrow_ref,
                arow_ref, acol_ref):
    r, c = me_ref[0], me_ref[1]
    rows_ref[c] = coords_ref[...]
    cols_ref[r] = coords_ref[...]
    starts, ends = chrom_bounds(lens_ref)
    starts = jnp.broadcast_to(starts, (LABELS, BEADS))
    ends = jnp.broadcast_to(ends, (LABELS, BEADS))
    lanes = iota((LABELS, BEADS), 1)
    eye = (iota((128, 128), 0) == iota((128, 128), 1)).astype(F32).astype(BF16)
    one = jnp.ones((8, 128), F32)
    nil = jnp.zeros((8, 128), F32)
    for v in range(2):
        for u in range(U):
            for q in range(3):
                tile_ref[v, u, 8 * q:8 * q + 8] = nil

    def hot_of(block):
        bead = lanes + block * BEADS
        return (bead >= starts) & (bead < ends)

    @pl.loop(0, COLS)
    def _(k):
        for s in range(S):
            x, y, z = rows_ref[k, s, 0], rows_ref[k, s, 1], rows_ref[k, s, 2]
            parts = points_of(x, y, z)
            v = s % 2
            for q in range(3):
                for w in range(4):
                    value = parts[w][q]
                    tile_ref[v, :, 8 * q + w, :] = 0.5 * value if w < 3 else value
            tile_ref[v, :, 4, :] = one
            for u in range(U):
                tiles = [tile_ref[v, u, 8 * q:8 * q + 8] for q in range(3)]
                hot = jnp.where(hot_of(u * 128 + r * 8 + k), 1.0, 0.0)
                full = jnp.concatenate(
                    [tiles[i] for i in (0, 0, 1, 0, 2, 1)] + [hot, jnp.zeros((32, 128), F32)], axis=0)
                flipped = lax.dot_general(eye, full.astype(BF16), NT, preferred_element_type=F32)
                left_ref[s * NR + k * U + u] = flipped.astype(BF16)
                lrow_ref[s * NR + k * U + u] = jnp.concatenate(tiles[:2], axis=0).astype(BF16)

    tile_ref[0, :, 3, :] = one
    tile_ref[1, :, 3, :] = one
    for v in range(2):
        tile_ref[v, :, 11, :] = nil
        tile_ref[v, :, 19, :] = nil

    @pl.loop(0, ROWS)
    def _(k):
        for s in range(S):
            x, y, z = cols_ref[k, s, 0], cols_ref[k, s, 1], cols_ref[k, s, 2]
            parts = points_of(x, y, z)
            v = s % 2
            for q in range(3):
                for w in range(4):
                    tile_ref[v, :, 8 * q + (w if w < 3 else 4), :] = parts[w][q]
            for u in range(U):
                tiles = [tile_ref[v, u, 8 * q:8 * q + 8] for q in range(3)]
                full = jnp.concatenate([tiles[i] for i in (0, 1, 0, 2, 0, 1)], axis=0)
                right_ref[s, u * ROWS + k] = full.astype(BF16)
        for u in range(U):
            hot = hot_of((u * ROWS + k) * 8 + c)
            same_ref[u * ROWS + k] = jnp.where(hot, 0.0, -BIG).astype(BF16)
            differ_ref[u * ROWS + k] = jnp.where(hot, -BIG, 0.0).astype(BF16)
    for p in range(PAD):
        same_ref[NC + p] = jnp.full((LABELS, BEADS), -BIG, BF16)
        for s in range(S):
            right_ref[s, NC + p] = jnp.zeros((LABELS, BEADS), BF16)

    @pl.loop(0, NC + PAD)
    def _(i):
        for s in range(S):
            acol_ref[s, i] = nil

    @pl.loop(0, NR)
    def _(i):
        for s in range(S):
            arow_ref[s, i] = nil

    triangle = iota((128, 128), 0) < iota((128, 128), 1)

    def chances(left, blocks, labels, diagonal=False):
        right = [jnp.concatenate([b, l], axis=0) for b, l in zip(blocks, labels)]
        right = jnp.concatenate(right, axis=1)
        z = jnp.dot(left[:, :2 * LABELS], right, preferred_element_type=F32)
        t = jnp.tanh(z)
        if diagonal:
            t = jnp.concatenate([jnp.where(triangle, t[:, :128], -1.0), t[:, 128:]], axis=1)
        return jnp.sum(t, axis=0, keepdims=True), (1.0 - t * t).astype(BF16)

    def pull(g, near, blocks):
        o = jnp.dot(near, g, preferred_element_type=F32)
        rows = []
        for j, b in enumerate(blocks):
            p = lax.dot_general(b[0:16], g[:, j * 128:j * 128 + 128], NT, preferred_element_type=F32)
            rows.append(p[0:8] + p[8:16])
        return o[0:8] + o[8:16], jnp.concatenate(rows, axis=1)

    def window(k, u, width, diagonal):
        at = k * U + u
        start = u * ROWS + r + jnp.where(k > c, 1, 0)
        gap = (c - k) & 7
        labels = [same_ref[start + m] for m in range(width)]
        held = None
        for s in range(S + 1):
            if s < S:
                blocks = [right_ref[s, start + m] for m in range(width)]
                sums, g = chances(left_ref[s * NR + at], blocks, labels, diagonal)
            if held is not None:
                q = at * S + s - 1
                o, p = pull(held[1], lrow_ref[(s - 1) * NR + at], held[2])
                gcol_ref[q, :, 0:width * 128] = o
                grow_ref[q, :, 0:width * 128] = p
                for m in range(width):
                    sum_ref[m, pl.ds(q, 1), :] = held[0][:, m * 128:m * 128 + 128]
                if width < 4:
                    gcol_ref[q, :, width * 128:] = jnp.zeros((8, 512 - width * 128), F32)
                    grow_ref[q, :, width * 128:] = jnp.zeros((8, 512 - width * 128), F32)
                    for m in range(width, 4):
                        sum_ref[m, pl.ds(q, 1), :] = jnp.zeros((1, 128), F32)
                        num_ref[m, pl.ds(q, 1), :] = jnp.zeros((1, 128), F32)
            held = (sums, g, blocks)
        for s in range(S):
            q = at * S + s
            for m in range(width):
                line, lane = s * 2 + (u >> 2), (u & 3) * 32 + gap + 8 * m
                n = count_ref[line, lane] if diagonal else tally_ref[k, line, lane]
                num_ref[m, pl.ds(q, 1), :] = jnp.full((1, 128), n, I32).astype(F32)

    @pl.loop(0, U)
    def _(u):
        window(c, u, 4, True)

    @pl.loop(0, U)
    def _(u):
        @pl.loop(1, COLS)
        def _(d):
            k = (c + d) & 7
            width = list_ref[32, k * U + u]

            @pl.when(width > 2)
            def _():
                window(k, u, 4, False)

            @pl.when((width > 0) & (width <= 2))
            def _():
                window(k, u, 2, False)

    most = jnp.maximum(jnp.maximum(list_ref[4, 0], list_ref[12, 0]),
                       jnp.maximum(list_ref[20, 0], list_ref[28, 0]))

    @pl.loop(0, (most + 1) >> 1)
    def _(half):
        held = None
        for turn in range(2 * S + 1):
            if turn < 2 * S:
                s, slot = turn % S, half * 2 + turn // S
                i, j = list_ref[s * 8, slot], list_ref[s * 8 + 1, slot]
                block = right_ref[s, j]
                sums, g = chances(left_ref[s * NR + i], [block], [differ_ref[j]])
                lnum_ref[0, pl.ds(s * CAP + slot, 1), :] = jnp.full(
                    (1, 128), list_ref[s * 8 + 2, slot], I32).astype(F32)
            if held is not None:
                o, p = pull(held[1], lrow_ref[held[3]], [held[2]])
                lgcol_ref[held[4]] = o
                lgrow_ref[held[4]] = p
                lsum_ref[0, pl.ds(held[4], 1), :] = held[0]
            held = (sums, g, block, s * NR + i, s * CAP + slot)

    def weights(sums_ref, nums_ref, lo, width):
        for m in range(width):
            at = (m, pl.ds(lo, 8), slice(None))
            total = jnp.sum(sums_ref[at], axis=1, keepdims=True)
            expect = 0.5 + (0.5 * (16384.0 + total)) / 128.0
            nums_ref[at] = 1.0 - nums_ref[at] / jnp.broadcast_to(expect, (8, 128))

    @pl.loop(0, NR * S // 8)
    def _(i):
        weights(sum_ref, num_ref, pl.multiple_of(i * 8, 8), 4)

    @pl.loop(0, CAP * S // 8)
    def _(i):
        weights(lsum_ref, lnum_ref, pl.multiple_of(i * 8, 8), 1)

    @pl.loop(0, U)
    def _(u):
        @pl.loop(0, COLS)
        def _(k):
            at = k * U + u
            start = u * ROWS + r + jnp.where(k > c, 1, 0)

            @pl.when((k == c) | (list_ref[32, at] > 0))
            def _():
                for s in range(S):
                    q = at * S + s
                    total = nil
                    for m in range(4):
                        lane = slice(m * 128, m * 128 + 128)
                        w = jnp.broadcast_to(num_ref[m, pl.ds(q, 1), :], (8, 128))
                        total = total + w * grow_ref[q, :, lane]
                        acol_ref[s, start + m] += w * gcol_ref[q, :, lane]
                    arow_ref[s, at] = total

    for s in range(S):
        @pl.loop(0, list_ref[s * 8 + 4, 0])
        def _(slot):
            i, j = list_ref[s * 8, slot], list_ref[s * 8 + 1, slot]
            q = s * CAP + slot
            w = jnp.broadcast_to(lnum_ref[0, pl.ds(q, 1), :], (8, 128))
            arow_ref[s, i] += w * lgrow_ref[q]
            acol_ref[s, j] += w * lgcol_ref[q]

    @pl.loop(0, COLS)
    def _(k):
        for s in range(S):
            here = pl.ds(k * U, U)
            mass = arow_ref[s, here, 3, :]
            for w in range(3):
                pulled = rows_ref[k, s, w] * mass - arow_ref[s, here, w, :]
                prow_ref[k, s, w] = pulled * (-1.0 / 512.0)

    @pl.loop(0, ROWS)
    def _(k):
        for s in range(S):
            here = pl.ds(k, U, stride=ROWS)
            mass = acol_ref[s, here, 4, :]
            for w in range(3):
                pulled = cols_ref[k, s, w] * mass - 2.0 * acol_ref[s, here, w, :]
                pcol_ref[k, s, w] = pulled * (-1.0 / 512.0)


def on_device(coords, chrom_lengths, band_counts, inter_pairs, inter_counts):
    shard = coords.shape
    me = jnp.stack([lax.axis_index("row"), lax.axis_index("col")]).astype(I32)
    lens = chrom_lengths.reshape(1, -1)
    counts = band_counts.reshape(8, 128)
    listing = pl.pallas_call(
        list_kernel,
        out_shape=jax.ShapeDtypeStruct((40, 128), I32),
        in_specs=[SMEM] + [VMEM] * 4, out_specs=VMEM, name="listing",
    )(me, lens, inter_pairs[:, :, 0].reshape(128, 128), inter_pairs[:, :, 1].reshape(128, 128),
      inter_counts.reshape(128, 128))
    rows, cols, tallies = pl.pallas_call(
        gather_kernel,
        out_shape=[jax.ShapeDtypeStruct((COLS,) + shard, F32), jax.ShapeDtypeStruct((ROWS,) + shard, F32),
                   jax.ShapeDtypeStruct((COLS, 8, 128), I32)],
        in_specs=[ANY] * 2, out_specs=[ANY] * 3,
        scratch_shapes=[pltpu.SemaphoreType.DMA((ROWS + 2 * COLS,))] * 2,
        compiler_params=pltpu.CompilerParams(collective_id=0, has_side_effects=True),
        name="gather",
    )(coords, counts)
    prow, pcol = pl.pallas_call(
        pair_kernel,
        out_shape=[jax.ShapeDtypeStruct((COLS,) + shard, F32), jax.ShapeDtypeStruct((ROWS,) + shard, F32)],
        in_specs=[SMEM] * 4 + [VMEM] * 4, out_specs=[VMEM] * 2,
        scratch_shapes=[
            pltpu.VMEM((2, U, 24, BEADS), F32),
            pltpu.VMEM((S * NR, BEADS, 128), BF16),
            pltpu.VMEM((S * NR, 16, BEADS), BF16),
            pltpu.VMEM((S, NC + PAD, LABELS, BEADS), BF16),
            pltpu.VMEM((NC + PAD, LABELS, BEADS), BF16),
            pltpu.VMEM((NC, LABELS, BEADS), BF16),
            pltpu.VMEM((4, NR * S, 128), F32),
            pltpu.VMEM((4, NR * S, 128), F32),
            pltpu.VMEM((NR * S, 8, 512), F32),
            pltpu.VMEM((NR * S, 8, 512), F32),
            pltpu.VMEM((1, CAP * S, 128), F32),
            pltpu.VMEM((1, CAP * S, 128), F32),
            pltpu.VMEM((CAP * S, 8, 128), F32),
            pltpu.VMEM((CAP * S, 8, 128), F32),
            pltpu.VMEM((S, NR, 8, BEADS), F32),
            pltpu.VMEM((S, NC + PAD, 8, BEADS), F32),
        ],
        compiler_params=pltpu.CompilerParams(vmem_limit_bytes=60 << 20),
        name="pairs",
    )(me, listing, tallies, counts, lens, coords, rows, cols)
    return pl.pallas_call(
        scatter_kernel,
        out_shape=jax.ShapeDtypeStruct(shard, F32),
        in_specs=[ANY] * 2, out_specs=VMEM,
        scratch_shapes=[
            pltpu.VMEM((ROWS + COLS - 2,) + shard, F32),
            pltpu.VMEM((2,) + shard, F32),
            pltpu.SemaphoreType.DMA((ROWS + COLS,)),
            pltpu.SemaphoreType.DMA((ROWS + COLS,)),
            pltpu.SemaphoreType.DMA((2,)),
        ],
        compiler_params=pltpu.CompilerParams(collective_id=1, has_side_effects=True),
        name="scatter",
    )(prow, pcol)


def solution(mesh):
    placed = (P(None, None, None, ("row", "col")), P(), P(None, None, ("row", "col"), None), P(), P())
    return jax.shard_map(on_device, mesh=mesh, in_specs=placed,
                         out_specs=P(None, None, None, ("row", "col")), check_vma=False)
```

time: 700 us -> 134 us (0.19)
  other arithmetic: 409 us -> 2.05 us
  Pallas kernels: 0 us -> 128 us
  waiting for transfers between devices: 100 us -> 0 us
  local copies, waits for them, and re-layouts: 89.2 us -> 4.02 us
  blocking collectives: 55.8 us -> 0 us
  loops' own time: 21.3 us -> 0 us
  between operations: 13.4 us -> 0.03 us
  matrix products: 8.08 us -> 0 us
    reduce_sum x44 -> x0, other arithmetic: 335 us -> none  [the longest x9 160 us: pair_tiles(): return (jnp.sum(pair_force, axis=4), -jnp.sum(pair_force, axis=3))]
    pallas_call x0 -> x4, Pallas kernels: none -> 128 us  [the longest x1 75.7 us: on_device(): pl.pallas_call(pair_kernel, out_shape=[jax.ShapeDtypeStruct((COLS,) + sha...]
    unnamed x3 -> x0, waiting for transfers between devices: 76.8 us -> none
    mul x43 -> x0, other arithmetic: 59.6 us -> none  [the longest x18 50 us: pair_tiles(): -2.0 * CONTACT_SLOPE / block_size * (masked * (1.0 - chance))]
    all_gather x3 -> x0, blocking collectives: 55.8 us -> none  [the longest x1 21.4 us: on_device(): column_points = lax.all_gather(local_points, 'row', axis=2, tiled=True)]
    gather x35 -> x0, local copies, waits for them, and re-layouts: 36.6 us -> none  [the longest x8 14.6 us: sweep(): second_points = jnp.take(column_flat, up_index, axis=2)]
    reduce_scatter x1 -> x0, waiting for transfers between devices: 23.4 us -> none  [on_device(): lax.psum_scatter(row_total, 'col', scatter_dimension=2, tiled=True)]
    dynamic_update_slice x16 -> x0, local copies, waits for them, and re-layouts: 22.6 us -> none  [on_device(): lax.scan(sweep, column_total, jnp.arange(sweeps, dtype=jnp.int32))]
  transfers between devices with their start and end apart: 2 -> 0, of which waited for: 2 -> 0; matrix products, arithmetic and copies ran while one was open for 0% -> 0% of each run, Pallas kernels for 0% -> 0%
where the time goes in v1:
time: 134 us
  Pallas kernels  128 us (96%)
  local copies, waits for them, and re-layouts  4.02 us (3%)
  other arithmetic  2.05 us (2%)
    pallas_call x1, Pallas kernels, on_device(): pl.pallas_call(pair_kernel, out_shape=[jax.ShapeDtypeStruct((COLS,) + sha...  75.7 us
    pallas_call x1, Pallas kernels, on_device(): pl.pallas_call(scatter_kernel, out_shape=jax.ShapeDtypeStruct(shard, F32)...  30.7 us
    pallas_call x1, Pallas kernels, on_device(): pl.pallas_call(gather_kernel, out_shape=[jax.ShapeDtypeStruct((COLS,) + s...  18.1 us
    pallas_call x1, Pallas kernels, on_device(): pl.pallas_call(list_kernel, out_shape=jax.ShapeDtypeStruct((40, 128), I32...  3.08 us

profile of v1, /device:TPU:1, one launch (start us, length us, event | category | flops | bytes accessed | tf_op | source)
XLA Modules:
  0.0 133.7 jit_solution(158483942437715993)
XLA Ops:
  0.0 0.0 copy-start.1
  0.0 0.0 copy-start
  0.0 0.6 pad_add_fusion.me_ref
  0.7 0.5 broadcast.3
  1.2 1.4 %reduce.3 = s32[4,8,32]{2,1,0:T(8,128)S(1)} reduce(s32[4,8,1,32]{3,2,1,0:T(1,128)} %param.7, s32[]{:T(128)} %broadcast.3), dimensions={2}, to_apply=%param.7.reduce_sub_computation.3 | reduce | bytes 8196 | tf_op args[2]
  2.6 0.7 reshape.11.counts.count_ref
  3.2 0.0 copy-done.1
  3.2 0.7 reshape.10.count_ref
  3.9 0.0 copy-done
  3.9 0.7 fusion
  4.7 3.1 %listing.1.list_ref = s32[40,128]{1,0:T(8,128)} custom-call(s32[2]{0:T(128)} %pad_add_fusion.me_ref, s32[1,46]{1,0:T(1,128)} %bitcast.7, s32[128,128]{1,0:T(8,128)} %bitcast.6, s32[128,128]{1,0:T(8,128)} %bitcast.5, s32[128,128]{1,0:T(8,128)} %reshape.10.count_ref), custom_call_target="tpu_custom_call" | custom-call | tf_op jit(solution)/shard_map/listing/pallas_call | solution.py:388
  7.7 18.1 %gather.1 = (f32[8,4,3,8,128]{4,3,2,1,0:T(8,128)}, f32[16,4,3,8,128]{4,3,2,1,0:T(8,128)}, s32[8,8,128]{2,1,0:T(8,128)}) custom-call(f32[4,3,8,128]{3,2,1,0:T(8,128)} %coords_ref.1, s32[8,128]{1,0:T(8,128)} %reshape.11.counts.count_ref), custom_call_target="tpu_custom_call" | custom-call | tf_op jit(solution)/shard_map/gather/pallas_call | solution.py:394
  25.9 75.7 %pairs.1 = (f32[8,4,3,8,128]{4,3,2,1,0:T(8,128)}, f32[16,4,3,8,128]{4,3,2,1,0:T(8,128)}) custom-call(s32[2]{0:T(128)} %pad_add_fusion.me_ref, s32[40,128]{1,0:T(8,128)} %listing.1.list_ref, s32[8,8,128]{2,1,0:T(8,128)} %get-tuple-element.10.tally_ref, s32[8,128]{1,0:T(8,128)} %reshape.11.counts.count_ref, s32[1,46]{1,0:T(1,128)} %bitcast.8, ...), custom_call_target="tpu_custom_call" | custom-call | tf_op jit(solution)/shard_map/pairs/pallas_call | solution.py:403
  101.6 30.7 %scatter.1 = f32[4,3,8,128]{3,2,1,0:T(8,128)} custom-call(f32[8,4,3,8,128]{4,3,2,1,0:T(8,128)} %get-tuple-element.13.rows, f32[16,4,3,8,128]{4,3,2,1,0:T(8,128)} %get-tuple-element.14.cols), custom_call_target="tpu_custom_call" | custom-call | tf_op jit(solution)/shard_map/scatter/pallas_call | solution.py:428
  132.3 1.4 %copy.7 = f32[4,3,8,128]{3,2,1,0:T(8,128)} copy(f32[4,3,8,128]{3,2,1,0:T(8,128)} %scatter.1) | data formatting | bytes 98304
Async XLA Ops:
  0.0 3.2 %copy-start.1 = (s32[4,4096]{1,0:T(4,128)S(1)}, s32[4,4096]{1,0:T(4,128)}, u32[]{:S(2)}) copy-start(s32[4,4096]{1,0:T(4,128)} %param.9) | copy-start | bytes 196612
  0.0 3.9 %copy-start = (s32[4,4096,2]{1,2,0:T(2,128)S(1)}, s32[4,4096,2]{1,2,0:T(2,128)}, u32[]{:S(2)}) copy-start(s32[4,4096,2]{1,2,0:T(2,128)} %param.8) | copy-start | bytes 393220

commit v2 on v1

v2 whole, which is shorter than its diff:
```python
import functools

import jax
import jax.numpy as jnp
from jax import lax
from jax.experimental import pallas as pl
from jax.experimental.pallas import tpu as pltpu
from jax.sharding import PartitionSpec as P

MESH = pl.DeviceIdType.MESH
ROWS, COLS = 16, 8
S, U, BEADS = 4, 8, 128
CAP = 64
LABELS = 48
NR, NC = COLS * U, ROWS * U
PAD = 4
WIDE = 4
BIG = 64.0
F32, BF16, I32 = jnp.float32, jnp.bfloat16, jnp.int32
ANY = pl.BlockSpec(memory_space=pl.ANY)
VMEM = pl.BlockSpec(memory_space=pltpu.VMEM)
SMEM = pl.BlockSpec(memory_space=pltpu.SMEM)
NT = (((1,), (1,)), ((), ()))


def iota(shape, axis):
    return lax.broadcasted_iota(I32, shape, axis)


def chrom_bounds(lens_ref):
    lens = jnp.broadcast_to(lens_ref[...], (LABELS, lens_ref.shape[1]))
    sub, lane = iota(lens.shape, 0), iota(lens.shape, 1)
    ends = jnp.sum(jnp.where(lane <= sub, lens, 0), axis=1, keepdims=True)
    starts = jnp.sum(jnp.where(lane < sub, lens, 0), axis=1, keepdims=True)
    return starts, ends


def list_kernel(me_ref, lens_ref, first_ref, second_ref, count_ref, out_ref):
    row, col = me_ref[0], me_ref[1]
    first, second, counts = first_ref[...], second_ref[...], count_ref[...]
    mine = (((first & 127) >> 3) == row) & ((second & 7) == col)
    mask = mine.astype(F32).astype(BF16)
    a, b = iota((128, 128), 0), iota((128, 128), 1)
    upper = (a <= b).astype(F32).astype(BF16)
    within = jnp.dot(mask, upper, preferred_element_type=F32)
    total = jnp.dot(mask, jnp.ones((128, 128), BF16), preferred_element_type=F32)
    lower = ((b < a) & ((a >> 5) == (b >> 5))).astype(F32).astype(BF16)
    offset = jnp.dot(lower, total.astype(BF16), preferred_element_type=F32)
    place = jnp.where(mine, (offset + within).astype(I32) - 1, -1)
    row_at = (first & 7) * U + (first >> 7)
    values = [row_at, second >> 3, counts, mine.astype(I32)]
    values = [v.astype(F32) for v in values]
    slots = iota((CAP, 128), 0)
    for s in range(S):
        acc = jnp.zeros((16, CAP), F32)
        for t in range(32):
            e = s * 32 + t
            hot = (place[e:e + 1] == slots).astype(F32).astype(BF16)
            rows = [v[e:e + 1] for v in values] + [jnp.zeros((12, 128), F32)]
            rows = jnp.concatenate(rows, axis=0).astype(BF16)
            acc = acc + lax.dot_general(rows, hot, NT, preferred_element_type=F32)
        spare = jnp.where(iota((8, CAP), 0) == 1, NC * (1.0 - acc[3:4]), 0.0)
        out_ref[s * 8:s * 8 + 8, 0:CAP] = (acc[0:8] + spare).astype(I32)
        amount = jnp.sum(acc[3:4], axis=1, keepdims=True).astype(I32)
        out_ref[s * 8 + 4:s * 8 + 5, :] = jnp.broadcast_to(amount, (1, 128))
    starts, ends = chrom_bounds(lens_ref)
    lane = iota((1, 128), 1)
    block = (lane & 7) * 128 + row * 8 + ((lane >> 3) & 7)
    last = jnp.broadcast_to(block * 128 + 127, (LABELS, 128))
    stop = jnp.min(jnp.where(ends > last, ends, 1 << 20), axis=0, keepdims=True)
    gap = (col - ((lane >> 3) & 7)) & 7
    far = jnp.minimum(jnp.minimum((stop - 1) >> 7, block + 31), 1023)
    width = ((far - block - gap) >> 3) + 1
    out_ref[32:40, :] = jnp.broadcast_to(jnp.clip(width, 0, 4), (8, 128))


def gather_kernel(coords, counts, rows, cols, tallies, send, recv, local):
    r, c = lax.axis_index("row"), lax.axis_index("col")
    kept = [pltpu.make_async_copy(coords, rows.at[c], local.at[0]),
            pltpu.make_async_copy(coords, cols.at[r], local.at[1]),
            pltpu.make_async_copy(counts, tallies.at[c], local.at[2])]
    for copy in kept:
        copy.start()
    barrier = pltpu.get_barrier_semaphore()
    for d in range(1, COLS):
        pl.semaphore_signal(barrier, 1, device_id=(r, lax.rem(c + d, COLS)), device_id_type=MESH)
    for d in range(1, ROWS):
        pl.semaphore_signal(barrier, 1, device_id=(lax.rem(r + d, ROWS), c), device_id_type=MESH)
    pl.semaphore_wait(barrier, COLS + ROWS - 2)
    copies = []
    for d in range(1, ROWS):
        copies.append(pltpu.make_async_remote_copy(
            coords, cols.at[r], send.at[d], recv.at[d],
            device_id=(lax.rem(r + d, ROWS), c), device_id_type=MESH))
    for d in range(1, COLS):
        peer = (r, lax.rem(c + d, COLS))
        copies.append(pltpu.make_async_remote_copy(
            coords, rows.at[c], send.at[ROWS + d], recv.at[ROWS + d],
            device_id=peer, device_id_type=MESH))
        copies.append(pltpu.make_async_remote_copy(
            counts, tallies.at[c], send.at[ROWS + COLS + d], recv.at[ROWS + COLS + d],
            device_id=peer, device_id_type=MESH))
    for copy in copies:
        copy.start()
    for copy in kept + copies:
        copy.wait()


def scatter_kernel(rows, cols, out, land, own, send, recv, local):
    r, c = lax.axis_index("row"), lax.axis_index("col")
    first = pltpu.make_async_copy(rows.at[c], own.at[0], local.at[0])
    second = pltpu.make_async_copy(cols.at[r], own.at[1], local.at[1])
    first.start()
    second.start()
    barrier = pltpu.get_barrier_semaphore()
    for d in range(1, COLS):
        pl.semaphore_signal(barrier, 1, device_id=(r, lax.rem(c + d, COLS)), device_id_type=MESH)
    for d in range(1, ROWS):
        pl.semaphore_signal(barrier, 1, device_id=(lax.rem(r + d, ROWS), c), device_id_type=MESH)
    pl.semaphore_wait(barrier, COLS + ROWS - 2)
    copies = []
    for d in range(1, ROWS):
        to = lax.rem(r + d, ROWS)
        copies.append(pltpu.make_async_remote_copy(
            cols.at[to], land.at[d - 1], send.at[d], recv.at[d],
            device_id=(to, c), device_id_type=MESH))
    for d in range(1, COLS):
        to = lax.rem(c + d, COLS)
        copies.append(pltpu.make_async_remote_copy(
            rows.at[to], land.at[ROWS - 2 + d], send.at[ROWS + d], recv.at[ROWS + d],
            device_id=(r, to), device_id_type=MESH))
    for copy in copies:
        copy.start()
    first.wait()
    second.wait()
    for copy in copies:
        copy.wait()
    for s in range(S):
        total = own[0, s] + own[1, s]
        for d in range(ROWS + COLS - 2):
            total = total + land[d, s]
        out[s] = total


def split3(x):
    a = x.astype(BF16).astype(F32)
    b = (x - a).astype(BF16).astype(F32)
    return a, b, (x - a) - b


def points_of(x, y, z):
    c = 0.75 - 0.25 * (x * x + y * y + z * z)
    return split3(x), split3(y), split3(z), split3(c)


def pair_kernel(me_ref, list_ref, tally_ref, lens_ref, rows_ref, cols_ref,
                prow_ref, pcol_ref,
                unit_ref, tile_ref, left_ref, lrow_ref, right_ref, same_ref, differ_ref,
                sum_ref, num_ref, gcol_ref, grow_ref, lsum_ref, lnum_ref, lgcol_ref, lgrow_ref,
                arow_ref, acol_ref):
    r, c = me_ref[0], me_ref[1]
    starts, ends = chrom_bounds(lens_ref)
    starts = jnp.broadcast_to(starts, (LABELS, BEADS))
    ends = jnp.broadcast_to(ends, (LABELS, BEADS))
    lanes = iota((LABELS, BEADS), 1)
    eye = (iota((128, 128), 0) == iota((128, 128), 1)).astype(F32).astype(BF16)
    one = jnp.ones((8, 128), F32)
    nil = jnp.zeros((8, 128), F32)
    for v in range(S):
        for u in range(U):
            for q in range(3):
                tile_ref[v, u, 8 * q:8 * q + 8] = nil

    def hot_of(block):
        bead = lanes + block * BEADS
        return (bead >= starts) & (bead < ends)

    for v in range(S):
        tile_ref[v, :, 4, :] = one

    @pl.loop(0, COLS)
    def _(k):
        for s in range(S):
            x, y, z = rows_ref[k, s, 0], rows_ref[k, s, 1], rows_ref[k, s, 2]
            parts = points_of(x, y, z)
            for q in range(3):
                for w in range(4):
                    value = parts[w][q]
                    tile_ref[s, :, 8 * q + w, :] = 0.5 * value if w < 3 else value
        for u in range(0, U, 2):
            hots = [jnp.where(hot_of((u + i) * 128 + r * 8 + k), 1.0, 0.0).astype(BF16) for i in range(2)]
            for s in range(S):
                fulls = []
                for i in range(2):
                    tiles = [tile_ref[s, u + i, 8 * q:8 * q + 8] for q in range(3)]
                    full = jnp.concatenate([tiles[j] for j in (0, 0, 1, 0, 2, 1)], axis=0).astype(BF16)
                    fulls += [full, hots[i], jnp.zeros((32, 128), BF16)]
                    lrow_ref[s * NR + k * U + u + i] = jnp.concatenate(tiles[:2], axis=0).astype(BF16)
                flipped = lax.dot_general(eye, jnp.concatenate(fulls, axis=0), NT, preferred_element_type=F32)
                for i in range(2):
                    left_ref[s * NR + k * U + u + i] = flipped[:, i * 128:i * 128 + 128].astype(BF16)

    for v in range(S):
        tile_ref[v, :, 3, :] = one
        tile_ref[v, :, 11, :] = nil
        tile_ref[v, :, 19, :] = nil

    @pl.loop(0, ROWS)
    def _(k):
        for s in range(S):
            x, y, z = cols_ref[k, s, 0], cols_ref[k, s, 1], cols_ref[k, s, 2]
            parts = points_of(x, y, z)
            for q in range(3):
                for w in range(4):
                    tile_ref[s, :, 8 * q + (w if w < 3 else 4), :] = parts[w][q]
        for s in range(S):
            for u in range(U):
                tiles = [tile_ref[s, u, 8 * q:8 * q + 8] for q in range(3)]
                full = jnp.concatenate([tiles[i] for i in (0, 1, 0, 2, 0, 1)], axis=0)
                right_ref[s, u * ROWS + k] = full.astype(BF16)
        for u in range(U):
            hot = hot_of((u * ROWS + k) * 8 + c)
            same_ref[u * ROWS + k] = jnp.where(hot, 0.0, -BIG).astype(BF16)
            differ_ref[u * ROWS + k] = jnp.where(hot, -BIG, 0.0).astype(BF16)
    for p in range(PAD):
        same_ref[NC + p] = jnp.full((LABELS, BEADS), -BIG, BF16)
        for s in range(S):
            right_ref[s, NC + p] = jnp.zeros((LABELS, BEADS), BF16)
    differ_ref[NC] = jnp.full((LABELS, BEADS), -BIG, BF16)

    @pl.loop(0, (NC + PAD) // 4)
    def _(i):
        for s in range(S):
            for j in range(4):
                acol_ref[s, i * 4 + j] = nil

    @pl.loop(0, NR // 4)
    def _(i):
        for s in range(S):
            for j in range(4):
                arow_ref[s, i * 4 + j] = nil

    def collect(i, filled):
        k = i >> 3
        width = list_ref[32, i]
        unit_ref[filled] = i * 2
        filled = filled + jnp.where((width > 0) & (k != c), 1, 0)
        unit_ref[filled] = i * 2 + 1
        return filled + jnp.where(width > 2, 1, 0)

    units = lax.fori_loop(0, NR, collect, jnp.int32(0))
    unit_ref[units] = unit_ref[jnp.maximum(units - 1, 0)]
    triangle = iota((128, 128), 0) < iota((128, 128), 1)
    empty = jnp.zeros((16, 128), BF16)

    def chances(left, blocks, labels, diagonal=False):
        right = [jnp.concatenate([b, l], axis=0) for b, l in zip(blocks, labels)]
        right = jnp.concatenate(right, axis=1)
        return jnp.dot(left[:, :2 * LABELS], right, preferred_element_type=F32)

    def finish(z, diagonal=False):
        t = jnp.tanh(z)
        if diagonal:
            t = jnp.concatenate([jnp.where(triangle, t[:, :128], -1.0), t[:, 128:]], axis=1)
        return jnp.sum(t, axis=0, keepdims=True), (1.0 - t * t).astype(BF16)

    def pull(g, near, far):
        o = jnp.dot(near, g, preferred_element_type=F32)
        spread = jnp.concatenate([jnp.concatenate([far[0], empty], axis=1),
                                  jnp.concatenate([empty, far[1]], axis=1)], axis=0)
        p = lax.dot_general(spread, g, NT, preferred_element_type=F32)
        return o[0:8] + o[8:16], p[0:8] + p[8:16], p[16:24] + p[24:32]

    def window_pull(g, sums, at, start, out):
        o, p0, p1 = pull(g, lrow_ref[at], [right_ref[at >> 6, start + m, 0:16] for m in range(2)])
        gcol_ref[out] = o
        grow_ref[out, :, 0:128] = p0
        grow_ref[out, :, 128:256] = p1
        for m in range(2):
            sum_ref[m, pl.ds(out, 1), :] = sums[:, m * 128:m * 128 + 128]

    def locate(unit):
        at = unit >> 1
        k, u = at >> 3, at & 7
        start = u * ROWS + r + jnp.where(k > c, 1, 0) + 2 * (unit & 1)
        gap = ((c - k) & 7) + 16 * (unit & 1)
        return at, start, k, u >> 2, (u & 3) * 32 + gap

    def run(unit_at, count, diagonal):
        def drain(held):
            for entry in held:
                window_pull(*entry)

        def body(it, held):
            for q in range(2):
                unit = unit_at(it * 2 + q)
                here, begin, k, line, lane = locate(unit)
                labels = [same_ref[begin + m] for m in range(2)]
                for s0 in range(0, S, WIDE):
                    group = range(s0, s0 + WIDE)
                    zs = [chances(left_ref[s * NR + here], [right_ref[s, begin + m] for m in range(2)], labels)
                          for s in group]
                    drain(held)
                    done = [finish(z, diagonal) for z in zs]
                    held = [(done[i][1], done[i][0], s * NR + here, begin, unit * S + s)
                            for i, s in enumerate(group)]
                for s in range(S):
                    for m in range(2):
                        n = tally_ref[k, s * 2 + line, lane + 8 * m]
                        num_ref[m, pl.ds(unit * S + s, 1), :] = jnp.full((1, 128), n, I32).astype(F32)
            return held

        first = [(jnp.zeros((128, 256), BF16), jnp.zeros((1, 256), F32),
                  jnp.int32(0), jnp.int32(0), jnp.int32(NR * S * 2 + i)) for i in range(WIDE)]
        drain(lax.fori_loop(0, count, body, first))

    run(lambda i: (c * U + i) * 2, U // 2, True)
    run(lambda i: unit_ref[i], (units + 1) >> 1, False)

    most = jnp.maximum(jnp.maximum(list_ref[4, 0], list_ref[12, 0]),
                       jnp.maximum(list_ref[20, 0], list_ref[28, 0]))

    def listed_pull(g, sums, places):
        near = jnp.concatenate([lrow_ref[p[0]] for p in places], axis=0)
        o = jnp.dot(near, jnp.concatenate(g, axis=1), preferred_element_type=F32)
        far = jnp.concatenate([right_ref[p[0] >> 6, p[1], 0:16] for p in places], axis=0)
        w = lax.dot_general(far, jnp.concatenate(g, axis=0), NT, preferred_element_type=F32)
        for m, p in enumerate(places):
            lane = slice(m * 128, m * 128 + 128)
            lgcol_ref[p[2]] = o[m * 16:m * 16 + 8, lane] + o[m * 16 + 8:m * 16 + 16, lane]
            lgrow_ref[p[2]] = w[m * 16:m * 16 + 8, lane] + w[m * 16 + 8:m * 16 + 16, lane]
            lsum_ref[0, pl.ds(p[2], 1), :] = sums[m]

    def listed_body(it, carry):
        g, sums, places = carry
        for turn in range(2):
            slot = it * 2 + turn
            for s0 in range(0, S, 2):
                zs, now = [], []
                for s in (s0, s0 + 1):
                    i, j = list_ref[s * 8, slot], list_ref[s * 8 + 1, slot]
                    zs.append(chances(left_ref[s * NR + i], [right_ref[s, j]], [differ_ref[j]]))
                    now.append((s * NR + i, j, s * CAP + slot))
                    lnum_ref[0, pl.ds(s * CAP + slot, 1), :] = jnp.full(
                        (1, 128), list_ref[s * 8 + 2, slot], I32).astype(F32)
                listed_pull(g, sums, places)
                done = [finish(z) for z in zs]
                sums, g, places = [d[0] for d in done], [d[1] for d in done], now
        return g, sums, places

    idle = (jnp.int32(0), jnp.int32(0))
    first = ([jnp.zeros((128, 128), BF16)] * 2, [jnp.zeros((1, 128), F32)] * 2,
             [idle + (jnp.int32(CAP * S),), idle + (jnp.int32(CAP * S + 1),)])
    listed_pull(*lax.fori_loop(0, (most + 1) >> 1, listed_body, first))

    def weights(sums_ref, nums_ref, lo, width):
        for m in range(width):
            at = (m, pl.ds(lo, 8), slice(None))
            total = jnp.sum(sums_ref[at], axis=1, keepdims=True)
            expect = 0.5 + (0.5 * (16384.0 + total)) / 128.0
            nums_ref[at] = 1.0 - nums_ref[at] / jnp.broadcast_to(expect, (8, 128))

    @pl.loop(0, NR * S * 2 // 32)
    def _(i):
        for j in range(4):
            weights(sum_ref, num_ref, pl.multiple_of(i * 32 + j * 8, 8), 2)

    @pl.loop(0, CAP * S // 32)
    def _(i):
        for j in range(4):
            weights(lsum_ref, lnum_ref, pl.multiple_of(i * 32 + j * 8, 8), 1)

    def deposit(unit):
        at, start = locate(unit)[:2]
        held = []
        for s in range(S):
            out = unit * S + s
            w = [jnp.broadcast_to(num_ref[m, pl.ds(out, 1), :], (8, 128)) for m in range(2)]
            row = arow_ref[s, at] + (w[0] * grow_ref[out, :, 0:128] + w[1] * grow_ref[out, :, 128:256])
            col = [acol_ref[s, start + m] + w[m] * gcol_ref[out, :, m * 128:m * 128 + 128] for m in range(2)]
            held.append((row, col))
        for s in range(S):
            arow_ref[s, at] = held[s][0]
            for m in range(2):
                acol_ref[s, start + m] = held[s][1][m]

    @pl.loop(0, U)
    def _(u):
        deposit((c * U + u) * 2)

    @pl.loop(0, units)
    def _(i):
        deposit(unit_ref[i])

    @pl.loop(0, most)
    def _(slot):
        held = []
        for s in range(S):
            i, j, q = list_ref[s * 8, slot], list_ref[s * 8 + 1, slot], s * CAP + slot
            w = jnp.broadcast_to(lnum_ref[0, pl.ds(q, 1), :], (8, 128))
            held.append((i, j, arow_ref[s, i] + w * lgrow_ref[q], acol_ref[s, j] + w * lgcol_ref[q]))
        for s in range(S):
            i, j, row, col = held[s]
            arow_ref[s, i] = row
            acol_ref[s, j] = col

    @pl.loop(0, COLS)
    def _(k):
        for s in range(S):
            here = pl.ds(k * U, U)
            mass = arow_ref[s, here, 3, :]
            for w in range(3):
                pulled = rows_ref[k, s, w] * mass - arow_ref[s, here, w, :]
                prow_ref[k, s, w] = pulled * (-1.0 / 512.0)

    @pl.loop(0, ROWS)
    def _(k):
        for s in range(S):
            here = pl.ds(k, U, stride=ROWS)
            mass = acol_ref[s, here, 4, :]
            for w in range(3):
                pulled = cols_ref[k, s, w] * mass - 2.0 * acol_ref[s, here, w, :]
                pcol_ref[k, s, w] = pulled * (-1.0 / 512.0)


def pairs_call(me, listing, tallies, lens, rows, cols):
    shard = rows.shape[1:]
    return pl.pallas_call(
        pair_kernel,
        out_shape=[jax.ShapeDtypeStruct((COLS,) + shard, F32), jax.ShapeDtypeStruct((ROWS,) + shard, F32)],
        in_specs=[SMEM] * 3 + [VMEM] * 3, out_specs=[VMEM] * 2,
        scratch_shapes=[
            pltpu.SMEM((2 * NR + 2,), I32),
            pltpu.VMEM((S, U, 24, BEADS), F32),
            pltpu.VMEM((S * NR, BEADS, 128), BF16),
            pltpu.VMEM((S * NR, 16, BEADS), BF16),
            pltpu.VMEM((S, NC + PAD, LABELS, BEADS), BF16),
            pltpu.VMEM((NC + PAD, LABELS, BEADS), BF16),
            pltpu.VMEM((NC + 1, LABELS, BEADS), BF16),
            pltpu.VMEM((2, NR * S * 2 + 8, 128), F32),
            pltpu.VMEM((2, NR * S * 2 + 8, 128), F32),
            pltpu.VMEM((NR * S * 2 + 4, 8, 256), F32),
            pltpu.VMEM((NR * S * 2 + 4, 8, 256), F32),
            pltpu.VMEM((1, CAP * S + 8, 128), F32),
            pltpu.VMEM((1, CAP * S + 8, 128), F32),
            pltpu.VMEM((CAP * S + 2, 8, 128), F32),
            pltpu.VMEM((CAP * S + 2, 8, 128), F32),
            pltpu.VMEM((S, NR, 8, BEADS), F32),
            pltpu.VMEM((S, NC + PAD, 8, BEADS), F32),
        ],
        compiler_params=pltpu.CompilerParams(vmem_limit_bytes=60 << 20),
        name="pairs",
    )(me, listing, tallies, lens, rows, cols)


def on_device(coords, chrom_lengths, band_counts, inter_pairs, inter_counts):
    shard = coords.shape
    me = jnp.stack([lax.axis_index("row"), lax.axis_index("col")]).astype(I32)
    lens = chrom_lengths.reshape(1, -1)
    counts = band_counts.reshape(8, 128)
    listing = pl.pallas_call(
        list_kernel,
        out_shape=jax.ShapeDtypeStruct((40, 128), I32),
        in_specs=[SMEM] + [VMEM] * 4, out_specs=VMEM, name="listing",
    )(me, lens, inter_pairs[:, :, 0].reshape(128, 128), inter_pairs[:, :, 1].reshape(128, 128),
      inter_counts.reshape(128, 128))
    rows, cols, tallies = pl.pallas_call(
        gather_kernel,
        out_shape=[jax.ShapeDtypeStruct((COLS,) + shard, F32), jax.ShapeDtypeStruct((ROWS,) + shard, F32),
                   jax.ShapeDtypeStruct((COLS, 8, 128), I32)],
        in_specs=[ANY] * 2, out_specs=[ANY] * 3,
        scratch_shapes=[pltpu.SemaphoreType.DMA((ROWS + 2 * COLS,))] * 2 + [pltpu.SemaphoreType.DMA((3,))],
        compiler_params=pltpu.CompilerParams(collective_id=0, has_side_effects=True),
        name="gather",
    )(coords, counts)
    prow, pcol = pairs_call(me, listing, tallies, lens, rows, cols)
    return pl.pallas_call(
        scatter_kernel,
        out_shape=jax.ShapeDtypeStruct(shard, F32),
        in_specs=[ANY] * 2, out_specs=VMEM,
        scratch_shapes=[
            pltpu.VMEM((ROWS + COLS - 2,) + shard, F32),
            pltpu.VMEM((2,) + shard, F32),
            pltpu.SemaphoreType.DMA((ROWS + COLS,)),
            pltpu.SemaphoreType.DMA((ROWS + COLS,)),
            pltpu.SemaphoreType.DMA((2,)),
        ],
        compiler_params=pltpu.CompilerParams(collective_id=1, has_side_effects=True),
        name="scatter",
    )(prow, pcol)


def solution(mesh):
    placed = (P(None, None, None, ("row", "col")), P(), P(None, None, ("row", "col"), None), P(), P())
    return jax.shard_map(on_device, mesh=mesh, in_specs=placed,
                         out_specs=P(None, None, None, ("row", "col")), check_vma=False)
```

time: 134 us -> 101 us (0.75)
  Pallas kernels: 128 us -> 93.9 us
    pallas_call x1, Pallas kernels: 75.7 us -> 50 us  [pairs_call(): pl.pallas_call(pair_kernel, out_shape=[jax.ShapeDtypeStruct((COLS,) + sha...]
    pallas_call x1, Pallas kernels: 30.7 us -> 22.6 us  [on_device(): pl.pallas_call(scatter_kernel, out_shape=jax.ShapeDtypeStruct(shard, F32)...]
where the time goes in v2:
time: 101 us; the launch traced here: 99.9 us
  Pallas kernels  93.9 us (93%)
  local copies, waits for them, and re-layouts  4.01 us (4%)
  other arithmetic  1.98 us (2%)
    pallas_call x1, Pallas kernels, pairs_call(): pl.pallas_call(pair_kernel, out_shape=[jax.ShapeDtypeStruct((COLS,) + sha...  50 us
    pallas_call x1, Pallas kernels, on_device(): pl.pallas_call(scatter_kernel, out_shape=jax.ShapeDtypeStruct(shard, F32)...  22.6 us
    pallas_call x1, Pallas kernels, on_device(): pl.pallas_call(gather_kernel, out_shape=[jax.ShapeDtypeStruct((COLS,) + s...  18.2 us
    pallas_call x1, Pallas kernels, on_device(): pl.pallas_call(list_kernel, out_shape=jax.ShapeDtypeStruct((40, 128), I32...  3.08 us

profile of v2, /device:TPU:1, one launch (start us, length us, event | category | flops | bytes accessed | tf_op | source)
XLA Modules:
  0.0 99.9 jit_solution(5513736784192164859)
XLA Ops:
  0.0 0.0 copy-start.1
  0.0 0.0 copy-start
  0.0 0.6 pad_add_fusion.me_ref
  0.6 0.5 broadcast.3
  1.1 1.4 %reduce.3 = s32[4,8,32]{2,1,0:T(8,128)S(1)} reduce(s32[4,8,1,32]{3,2,1,0:T(1,128)} %param.7, s32[]{:T(128)} %broadcast.3), dimensions={2}, to_apply=%param.7.reduce_sub_computation.3 | reduce | bytes 8196 | tf_op args[2]
  2.5 0.7 reshape.11.counts
  3.2 0.0 copy-done.1
  3.2 0.7 reshape.10.count_ref
  3.8 0.0 copy-done
  3.8 0.7 fusion
  4.6 3.1 %listing.1.list_ref = s32[40,128]{1,0:T(8,128)} custom-call(s32[2]{0:T(128)} %pad_add_fusion.me_ref, s32[1,46]{1,0:T(1,128)} %bitcast.7, s32[128,128]{1,0:T(8,128)} %bitcast.6, s32[128,128]{1,0:T(8,128)} %bitcast.5, s32[128,128]{1,0:T(8,128)} %reshape.10.count_ref), custom_call_target="tpu_custom_call" | custom-call | tf_op jit(solution)/shard_map/listing/pallas_call | solution.py:461
  7.7 18.2 %gather.1 = (f32[8,4,3,8,128]{4,3,2,1,0:T(8,128)}, f32[16,4,3,8,128]{4,3,2,1,0:T(8,128)}, s32[8,8,128]{2,1,0:T(8,128)}) custom-call(f32[4,3,8,128]{3,2,1,0:T(8,128)} %coords.1, s32[8,128]{1,0:T(8,128)} %reshape.11.counts), custom_call_target="tpu_custom_call" | custom-call | tf_op jit(solution)/shard_map/gather/pallas_call | solution.py:467
  25.8 50.0 %pairs.1 = (f32[8,4,3,8,128]{4,3,2,1,0:T(8,128)}, f32[16,4,3,8,128]{4,3,2,1,0:T(8,128)}) custom-call(s32[2]{0:T(128)} %pad_add_fusion.me_ref, s32[40,128]{1,0:T(8,128)} %listing.1.list_ref, s32[8,8,128]{2,1,0:T(8,128)} %get-tuple-element.10.tally_ref, s32[1,46]{1,0:T(1,128)} %bitcast.8, f32[8,4,3,8,128]{4,3,2,1,0:T(8,128)} %get-tuple-element.11.rows_ref, ...), custom_call_target="tpu_custom_call" | custom-call | tf_op jit(solution)/shard_map/pairs/pallas_call | solution.py:428
  75.9 22.6 %scatter.1 = f32[4,3,8,128]{3,2,1,0:T(8,128)} custom-call(f32[8,4,3,8,128]{4,3,2,1,0:T(8,128)} %get-tuple-element.13.rows, f32[16,4,3,8,128]{4,3,2,1,0:T(8,128)} %get-tuple-element.14.cols), custom_call_target="tpu_custom_call" | custom-call | tf_op jit(solution)/shard_map/scatter/pallas_call | solution.py:477
  98.5 1.4 %copy.7 = f32[4,3,8,128]{3,2,1,0:T(8,128)} copy(f32[4,3,8,128]{3,2,1,0:T(8,128)} %scatter.1) | data formatting | bytes 98304
Async XLA Ops:
  0.0 3.2 %copy-start.1 = (s32[4,4096]{1,0:T(4,128)S(1)}, s32[4,4096]{1,0:T(4,128)}, u32[]{:S(2)}) copy-start(s32[4,4096]{1,0:T(4,128)} %param.9) | copy-start | bytes 196612
  0.0 3.8 %copy-start = (s32[4,4096,2]{1,2,0:T(2,128)S(1)}, s32[4,4096,2]{1,2,0:T(2,128)}, u32[]{:S(2)}) copy-start(s32[4,4096,2]{1,2,0:T(2,128)} %param.8) | copy-start | bytes 393220

commit v3 on v2

--- a/solution.py
+++ b/solution.py
@@ -8,7 +8,7 @@
 from jax.sharding import PartitionSpec as P
 
 MESH = pl.DeviceIdType.MESH
-ROWS, COLS = 16, 8
+ROWS, COLS, SIDE = 16, 8, 4
 S, U, BEADS = 4, 8, 128
 CAP = 64
 LABELS = 48
@@ -35,9 +35,14 @@
     return starts, ends
 
 
-def list_kernel(me_ref, lens_ref, first_ref, second_ref, count_ref, out_ref):
-    row, col = me_ref[0], me_ref[1]
-    first, second, counts = first_ref[...], second_ref[...], count_ref[...]
+def make_list(row, col, lens_ref, pairs_ref, count_ref, stage_ref, out_ref):
+    for s in range(S):
+        for t in range(32):
+            e, lane = s * 32 + t, slice(t * 128, t * 128 + 128)
+            stage_ref[0, e:e + 1, :] = pairs_ref[s, 0:1, lane]
+            stage_ref[1, e:e + 1, :] = pairs_ref[s, 1:2, lane]
+            stage_ref[2, e:e + 1, :] = count_ref[s:s + 1, lane]
+    first, second, counts = stage_ref[0], stage_ref[1], stage_ref[2]
     mine = (((first & 127) >> 3) == row) & ((second & 7) == col)
     mask = mine.astype(F32).astype(BF16)
     a, b = iota((128, 128), 0), iota((128, 128), 1)
@@ -48,17 +53,19 @@
     offset = jnp.dot(lower, total.astype(BF16), preferred_element_type=F32)
     place = jnp.where(mine, (offset + within).astype(I32) - 1, -1)
     row_at = (first & 7) * U + (first >> 7)
-    values = [row_at, second >> 3, counts, mine.astype(I32)]
-    values = [v.astype(F32) for v in values]
+    for i, v in enumerate([row_at, second >> 3, counts, mine.astype(I32), place]):
+        stage_ref[i] = v
     slots = iota((CAP, 128), 0)
+    pad = jnp.zeros((12, 128), F32)
     for s in range(S):
-        acc = jnp.zeros((16, CAP), F32)
-        for t in range(32):
+        def gather_slots(t, acc):
             e = s * 32 + t
-            hot = (place[e:e + 1] == slots).astype(F32).astype(BF16)
-            rows = [v[e:e + 1] for v in values] + [jnp.zeros((12, 128), F32)]
-            rows = jnp.concatenate(rows, axis=0).astype(BF16)
-            acc = acc + lax.dot_general(rows, hot, NT, preferred_element_type=F32)
+            hot = (stage_ref[4, pl.ds(e, 1), :] == slots).astype(F32).astype(BF16)
+            rows = [stage_ref[i, pl.ds(e, 1), :].astype(F32) for i in range(4)]
+            rows = jnp.concatenate(rows + [pad], axis=0).astype(BF16)
+            return acc + lax.dot_general(rows, hot, NT, preferred_element_type=F32)
+
+        acc = lax.fori_loop(0, 32, gather_slots, jnp.zeros((16, CAP), F32))
         spare = jnp.where(iota((8, CAP), 0) == 1, NC * (1.0 - acc[3:4]), 0.0)
         out_ref[s * 8:s * 8 + 8, 0:CAP] = (acc[0:8] + spare).astype(I32)
         amount = jnp.sum(acc[3:4], axis=1, keepdims=True).astype(I32)
@@ -70,76 +77,149 @@
     stop = jnp.min(jnp.where(ends > last, ends, 1 << 20), axis=0, keepdims=True)
     gap = (col - ((lane >> 3) & 7)) & 7
     far = jnp.minimum(jnp.minimum((stop - 1) >> 7, block + 31), 1023)
-    width = ((far - block - gap) >> 3) + 1
-    out_ref[32:40, :] = jnp.broadcast_to(jnp.clip(width, 0, 4), (8, 128))
-
-
-def gather_kernel(coords, counts, rows, cols, tallies, send, recv, local):
+    width = jnp.clip(((far - block - gap) >> 3) + 1, 0, 4)
+    out_ref[32:33, :] = width
+    out_ref[33:34, :] = jnp.full((1, 128), row, I32)
+    out_ref[34:35, :] = jnp.full((1, 128), col, I32)
+    out_ref[35:40, :] = jnp.zeros((5, 128), I32)
+
+
+def greet(r, c):
+    y, z = r // SIDE, lax.rem(r, SIDE)
+    peers = [(r, lax.rem(c + d, COLS)) for d in range(1, COLS)]
+    peers += [(lax.rem(y + d, SIDE) * SIDE + z, c) for d in range(1, SIDE)]
+    peers += [(y * SIDE + lax.rem(z + d, SIDE), c) for d in range(1, SIDE)]
+    barrier = pltpu.get_barrier_semaphore()
+    for peer in peers:
+        pl.semaphore_signal(barrier, 1, device_id=peer, device_id_type=MESH)
+    pl.semaphore_wait(barrier, len(peers))
+
+
+def gather_kernel(coords, counts, lens_ref, pairs, inter, rows, cols, tallies, list_ref,
+                  pairs_ref, inter_ref, stage_ref, send, recv, local):
     r, c = lax.axis_index("row"), lax.axis_index("col")
+    y, z = r // SIDE, lax.rem(r, SIDE)
+    taken = [pltpu.make_async_copy(pairs, pairs_ref, local.at[3]),
+             pltpu.make_async_copy(inter, inter_ref, local.at[4])]
     kept = [pltpu.make_async_copy(coords, rows.at[c], local.at[0]),
             pltpu.make_async_copy(coords, cols.at[r], local.at[1]),
             pltpu.make_async_copy(counts, tallies.at[c], local.at[2])]
+    for copy in taken + kept:
+        copy.start()
+    greet(r, c)
+    half = (pl.ds(0, S // 2), pl.ds(S // 2, S // 2))
+
+    def along(axis, d):
+        return (lax.rem(y + d, SIDE) * SIDE + z, c) if axis == 0 else (y * SIDE + lax.rem(z + d, SIDE), c)
+
+    def relay(h, step, d):
+        back = (lax.rem(y + SIDE - step, SIDE) * SIDE + z) if h == 0 else y * SIDE + lax.rem(z + SIDE - step, SIDE)
+        source = coords.at[half[h]] if step == 0 else cols.at[back, half[h]]
+        n = (h * SIDE + step) * SIDE + d
+        return pltpu.make_async_remote_copy(
+            source, cols.at[back, half[h]], send.at[n], recv.at[n],
+            device_id=along(1 - h, d), device_id_type=MESH)
+
+    early, base = [], 2 * SIDE * SIDE
+    for d in (1, 3, 2):
+        for h in range(2):
+            n = base + h * SIDE + d
+            early.append((h, d, pltpu.make_async_remote_copy(
+                coords.at[half[h]], cols.at[r, half[h]], send.at[n], recv.at[n],
+                device_id=along(h, d), device_id_type=MESH)))
+    base += 2 * SIDE
+    across = []
+    for d in range(1, COLS):
+        peer = (r, lax.rem(c + d, COLS))
+        across.append(pltpu.make_async_remote_copy(
+            coords, rows.at[c], send.at[base + d], recv.at[base + d], device_id=peer, device_id_type=MESH))
+        across.append(pltpu.make_async_remote_copy(
+            counts, tallies.at[c], send.at[base + COLS + d], recv.at[base + COLS + d],
+            device_id=peer, device_id_type=MESH))
+    for _, _, copy in early:
+        copy.start()
+    late = [relay(h, 0, d) for d in (1, 3, 2) for h in range(2)]
+    for copy in late + across:
+        copy.start()
+    for h, step, copy in early:
+        copy.wait_recv()
+        passed = [relay(h, step, d) for d in (1, 3, 2)]
+        for forward in passed:
+            forward.start()
+        late += passed
+    for copy in taken:
+        copy.wait()
+    make_list(r, c, lens_ref, pairs_ref, inter_ref, stage_ref, list_ref)
+    for _, _, copy in early:
+        copy.wait_send()
+    for copy in kept + across + late:
+        copy.wait()
+
+
+def scatter_kernel(rows, cols, out, land_a, land_b, sum_a, sum_b, last_a, last_b, land, own, send, recv, local):
+    r, c = lax.axis_index("row"), lax.axis_index("col")
+    y, z = r // SIDE, lax.rem(r, SIDE)
+    a, b = pl.ds(0, S // 2), pl.ds(S // 2, S // 2)
+    kept = [pltpu.make_async_copy(rows.at[c], own, local.at[0]),
+            pltpu.make_async_copy(cols.at[:, z, a], sum_a, local.at[1]),
+            pltpu.make_async_copy(cols.at[y, :, b], sum_b, local.at[2])]
     for copy in kept:
         copy.start()
-    barrier = pltpu.get_barrier_semaphore()
-    for d in range(1, COLS):
-        pl.semaphore_signal(barrier, 1, device_id=(r, lax.rem(c + d, COLS)), device_id_type=MESH)
-    for d in range(1, ROWS):
-        pl.semaphore_signal(barrier, 1, device_id=(lax.rem(r + d, ROWS), c), device_id_type=MESH)
-    pl.semaphore_wait(barrier, COLS + ROWS - 2)
-    copies = []
-    for d in range(1, ROWS):
-        copies.append(pltpu.make_async_remote_copy(
-            coords, cols.at[r], send.at[d], recv.at[d],
-            device_id=(lax.rem(r + d, ROWS), c), device_id_type=MESH))
-    for d in range(1, COLS):
-        peer = (r, lax.rem(c + d, COLS))
-        copies.append(pltpu.make_async_remote_copy(
-            coords, rows.at[c], send.at[ROWS + d], recv.at[ROWS + d],
-            device_id=peer, device_id_type=MESH))
-        copies.append(pltpu.make_async_remote_copy(
-            counts, tallies.at[c], send.at[ROWS + COLS + d], recv.at[ROWS + COLS + d],
-            device_id=peer, device_id_type=MESH))
-    for copy in copies:
-        copy.start()
-    for copy in kept + copies:
-        copy.wait()
-
-
-def scatter_kernel(rows, cols, out, land, own, send, recv, local):
-    r, c = lax.axis_index("row"), lax.axis_index("col")
-    first = pltpu.make_async_copy(rows.at[c], own.at[0], local.at[0])
-    second = pltpu.make_async_copy(cols.at[r], own.at[1], local.at[1])
-    first.start()
-    second.start()
-    barrier = pltpu.get_barrier_semaphore()
-    for d in range(1, COLS):
-        pl.semaphore_signal(barrier, 1, device_id=(r, lax.rem(c + d, COLS)), device_id_type=MESH)
-    for d in range(1, ROWS):
-        pl.semaphore_signal(barrier, 1, device_id=(lax.rem(r + d, ROWS), c), device_id_type=MESH)
-    pl.semaphore_wait(barrier, COLS + ROWS - 2)
-    copies = []
-    for d in range(1, ROWS):
-        to = lax.rem(r + d, ROWS)
-        copies.append(pltpu.make_async_remote_copy(
-            cols.at[to], land.at[d - 1], send.at[d], recv.at[d],
-            device_id=(to, c), device_id_type=MESH))
+    greet(r, c)
+    first_a, first_b, across = [], [], []
+    for d in (1, 3, 2):
+        to = lax.rem(z + d, SIDE)
+        first_a.append(pltpu.make_async_remote_copy(
+            cols.at[:, to, a], land_a.at[d - 1], send.at[d], recv.at[d],
+            device_id=(y * SIDE + to, c), device_id_type=MESH))
+        to = lax.rem(y + d, SIDE)
+        first_b.append(pltpu.make_async_remote_copy(
+            cols.at[to, :, b], land_b.at[d - 1], send.at[SIDE + d], recv.at[SIDE + d],
+            device_id=(to * SIDE + z, c), device_id_type=MESH))
     for d in range(1, COLS):
         to = lax.rem(c + d, COLS)
-        copies.append(pltpu.make_async_remote_copy(
-            rows.at[to], land.at[ROWS - 2 + d], send.at[ROWS + d], recv.at[ROWS + d],
+        n = 4 * SIDE + d
+        across.append(pltpu.make_async_remote_copy(
+            rows.at[to], land.at[d - 1], send.at[n], recv.at[n],
             device_id=(r, to), device_id_type=MESH))
-    for copy in copies:
+    for one, two in zip(first_a, first_b):
+        one.start()
+        two.start()
+    for copy in across:
         copy.start()
-    first.wait()
-    second.wait()
-    for copy in copies:
-        copy.wait()
+    second = []
+    for turn, (first, total, landed, last) in enumerate(
+            [(first_a, sum_a, land_a, last_a), (first_b, sum_b, land_b, last_b)]):
+        kept[1 + turn].wait()
+        for copy in first:
+            copy.wait_recv()
+        for i in range(SIDE):
+            for s in range(S // 2):
+                total[i, s] = (total[i, s] + landed[0, i, s]) + (landed[1, i, s] + landed[2, i, s])
+        for d in (1, 3, 2):
+            here = y if turn == 0 else z
+            to = lax.rem(here + d, SIDE)
+            n = (2 + turn) * SIDE + d
+            peer = (to * SIDE + z, c) if turn == 0 else (y * SIDE + to, c)
+            copy = pltpu.make_async_remote_copy(
+                total.at[to], last.at[d - 1], send.at[n], recv.at[n], device_id=peer, device_id_type=MESH)
+            copy.start()
+            second.append(copy)
+    kept[0].wait()
+    for copy in across:
+        copy.wait_recv()
     for s in range(S):
-        total = own[0, s] + own[1, s]
-        for d in range(ROWS + COLS - 2):
+        total = own[s]
+        for d in range(COLS - 1):
             total = total + land[d, s]
         out[s] = total
+    for copy in second:
+        copy.wait_recv()
+    for s in range(S // 2):
+        out[s] = out[s] + (sum_a[y, s] + last_a[0, s]) + (last_a[1, s] + last_a[2, s])
+        out[s + S // 2] = out[s + S // 2] + (sum_b[z, s] + last_b[0, s]) + (last_b[1, s] + last_b[2, s])
+    for copy in first_a + first_b + across + second:
+        copy.wait_send()
 
 
 def split3(x):
@@ -153,12 +233,12 @@
     return split3(x), split3(y), split3(z), split3(c)
 
 
-def pair_kernel(me_ref, list_ref, tally_ref, lens_ref, rows_ref, cols_ref,
+def pair_kernel(list_ref, tally_ref, lens_ref, rows_ref, cols_ref,
                 prow_ref, pcol_ref,
                 unit_ref, tile_ref, left_ref, lrow_ref, right_ref, same_ref, differ_ref,
                 sum_ref, num_ref, gcol_ref, grow_ref, lsum_ref, lnum_ref, lgcol_ref, lgrow_ref,
                 arow_ref, acol_ref):
-    r, c = me_ref[0], me_ref[1]
+    r, c = list_ref[33, 0], list_ref[34, 0]
     starts, ends = chrom_bounds(lens_ref)
     starts = jnp.broadcast_to(starts, (LABELS, BEADS))
     ends = jnp.broadcast_to(ends, (LABELS, BEADS))
@@ -284,7 +364,7 @@
         k, u = at >> 3, at & 7
         start = u * ROWS + r + jnp.where(k > c, 1, 0) + 2 * (unit & 1)
         gap = ((c - k) & 7) + 16 * (unit & 1)
-        return at, start, k, u >> 2, (u & 3) * 32 + gap
+        return at, start, k, u, gap
 
     def run(unit_at, count, diagonal):
         def drain(held):
@@ -294,7 +374,7 @@
         def body(it, held):
             for q in range(2):
                 unit = unit_at(it * 2 + q)
-                here, begin, k, line, lane = locate(unit)
+                here, begin, k, u, gap = locate(unit)
                 labels = [same_ref[begin + m] for m in range(2)]
                 for s0 in range(0, S, WIDE):
                     group = range(s0, s0 + WIDE)
@@ -306,7 +386,7 @@
                             for i, s in enumerate(group)]
                 for s in range(S):
                     for m in range(2):
-                        n = tally_ref[k, s * 2 + line, lane + 8 * m]
+                        n = tally_ref[k, s, u, 0, gap + 8 * m]
                         num_ref[m, pl.ds(unit * S + s, 1), :] = jnp.full((1, 128), n, I32).astype(F32)
             return held
 
@@ -423,12 +503,12 @@
                 pcol_ref[k, s, w] = pulled * (-1.0 / 512.0)
 
 
-def pairs_call(me, listing, tallies, lens, rows, cols):
+def pairs_call(listing, tallies, lens, rows, cols):
     shard = rows.shape[1:]
     return pl.pallas_call(
         pair_kernel,
         out_shape=[jax.ShapeDtypeStruct((COLS,) + shard, F32), jax.ShapeDtypeStruct((ROWS,) + shard, F32)],
-        in_specs=[SMEM] * 3 + [VMEM] * 3, out_specs=[VMEM] * 2,
+        in_specs=[SMEM] * 2 + [VMEM] * 3, out_specs=[VMEM] * 2,
         scratch_shapes=[
             pltpu.SMEM((2 * NR + 2,), I32),
             pltpu.VMEM((S, U, 24, BEADS), F32),
@@ -450,44 +530,52 @@
         ],
         compiler_params=pltpu.CompilerParams(vmem_limit_bytes=60 << 20),
         name="pairs",
-    )(me, listing, tallies, lens, rows, cols)
+    )(listing, tallies, lens, rows, cols)
 
 
 def on_device(coords, chrom_lengths, band_counts, inter_pairs, inter_counts):
     shard = coords.shape
-    me = jnp.stack([lax.axis_index("row"), lax.axis_index("col")]).astype(I32)
     lens = chrom_lengths.reshape(1, -1)
-    counts = band_counts.reshape(8, 128)
-    listing = pl.pallas_call(
-        list_kernel,
-        out_shape=jax.ShapeDtypeStruct((40, 128), I32),
-        in_specs=[SMEM] + [VMEM] * 4, out_specs=VMEM, name="listing",
-    )(me, lens, inter_pairs[:, :, 0].reshape(128, 128), inter_pairs[:, :, 1].reshape(128, 128),
-      inter_counts.reshape(128, 128))
-    rows, cols, tallies = pl.pallas_call(
+    flipped = jnp.transpose(inter_pairs, (0, 2, 1))
+    rows, cols, tallies, listing = pl.pallas_call(
         gather_kernel,
         out_shape=[jax.ShapeDtypeStruct((COLS,) + shard, F32), jax.ShapeDtypeStruct((ROWS,) + shard, F32),
-                   jax.ShapeDtypeStruct((COLS, 8, 128), I32)],
-        in_specs=[ANY] * 2, out_specs=[ANY] * 3,
-        scratch_shapes=[pltpu.SemaphoreType.DMA((ROWS + 2 * COLS,))] * 2 + [pltpu.SemaphoreType.DMA((3,))],
+                   jax.ShapeDtypeStruct((COLS,) + band_counts.shape, I32),
+                   jax.ShapeDtypeStruct((40, 128), I32)],
+        in_specs=[ANY] * 2 + [VMEM] + [ANY] * 2, out_specs=[ANY] * 3 + [VMEM],
+        scratch_shapes=[
+            pltpu.VMEM(flipped.shape, I32),
+            pltpu.VMEM(inter_counts.shape, I32),
+            pltpu.VMEM((5, 128, 128), I32),
+            pltpu.SemaphoreType.DMA((2 * SIDE * SIDE + 2 * SIDE + 2 * COLS,)),
+            pltpu.SemaphoreType.DMA((2 * SIDE * SIDE + 2 * SIDE + 2 * COLS,)),
+            pltpu.SemaphoreType.DMA((5,)),
+        ],
         compiler_params=pltpu.CompilerParams(collective_id=0, has_side_effects=True),
         name="gather",
-    )(coords, counts)
-    prow, pcol = pairs_call(me, listing, tallies, lens, rows, cols)
+    )(coords, band_counts, lens, flipped, inter_counts)
+    prow, pcol = pairs_call(listing, tallies, lens, rows, cols)
+    part = shard[1:]
     return pl.pallas_call(
         scatter_kernel,
         out_shape=jax.ShapeDtypeStruct(shard, F32),
         in_specs=[ANY] * 2, out_specs=VMEM,
         scratch_shapes=[
-            pltpu.VMEM((ROWS + COLS - 2,) + shard, F32),
-            pltpu.VMEM((2,) + shard, F32),
-            pltpu.SemaphoreType.DMA((ROWS + COLS,)),
-            pltpu.SemaphoreType.DMA((ROWS + COLS,)),
-            pltpu.SemaphoreType.DMA((2,)),
+            pltpu.VMEM((SIDE - 1, SIDE, S // 2) + part, F32),
+            pltpu.VMEM((SIDE - 1, SIDE, S // 2) + part, F32),
+            pltpu.VMEM((SIDE, S // 2) + part, F32),
+            pltpu.VMEM((SIDE, S // 2) + part, F32),
+            pltpu.VMEM((SIDE - 1, S // 2) + part, F32),
+            pltpu.VMEM((SIDE - 1, S // 2) + part, F32),
+            pltpu.VMEM((COLS - 1,) + shard, F32),
+            pltpu.VMEM(shard, F32),
+            pltpu.SemaphoreType.DMA((4 * SIDE + COLS,)),
+            pltpu.SemaphoreType.DMA((4 * SIDE + COLS,)),
+            pltpu.SemaphoreType.DMA((3,)),
         ],
         compiler_params=pltpu.CompilerParams(collective_id=1, has_side_effects=True),
         name="scatter",
-    )(prow, pcol)
+    )(prow, pcol.reshape((SIDE, SIDE) + shard))
 
 
 def solution(mesh):

time: 101 us -> 108 us (1.069); the launches traced: 99.9 us -> 106 us
  Pallas kernels: 93.9 us -> 104 us
  local copies, waits for them, and re-layouts: 4.01 us -> 1.42 us
  other arithmetic: 1.98 us -> 0 us
    pallas_call x1, Pallas kernels: 18.2 us -> 30.2 us  [on_device(): pl.pallas_call(gather_kernel, out_shape=[jax.ShapeDtypeStruct((COLS,) + s...]
    pallas_call x1 -> x0, Pallas kernels: 3.08 us -> none  [on_device(): pl.pallas_call(list_kernel, out_shape=jax.ShapeDtypeStruct((40, 128), I32...]
    unnamed x1 -> x0, other arithmetic: 1.41 us -> none
    reshape x2 -> x0, local copies, waits for them, and re-layouts: 1.33 us -> none  [the longest x1 0.67 us: on_device(): inter_counts.reshape(128, 128)]
where the time goes in v3:
time: 108 us; the launch traced here: 106 us
  Pallas kernels  104 us (96%)
  local copies, waits for them, and re-layouts  1.42 us (1%)
    pallas_call x1, Pallas kernels, pairs_call(): pl.pallas_call(pair_kernel, out_shape=[jax.ShapeDtypeStruct((COLS,) + sha...  51 us
    pallas_call x1, Pallas kernels, on_device(): pl.pallas_call(gather_kernel, out_shape=[jax.ShapeDtypeStruct((COLS,) + s...  30.2 us
    pallas_call x1, Pallas kernels, on_device(): pl.pallas_call(scatter_kernel, out_shape=jax.ShapeDtypeStruct(shard, F32)...  22.9 us

profile of v3, /device:TPU:1, one launch (start us, length us, event | category | flops | bytes accessed | tf_op | source)
XLA Modules:
  0.0 105.6 jit_solution(3323598998914603385)
XLA Ops:
  0.0 30.2 %gather.1 = (f32[8,4,3,8,128]{4,3,2,1,0:T(8,128)}, f32[16,4,3,8,128]{4,3,2,1,0:T(8,128)}, s32[8,4,8,1,32]{4,3,2,1,0:T(1,128)}, s32[40,128]{1,0:T(8,128)}) custom-call(f32[4,3,8,128]{3,2,1,0:T(8,128)} %coords.1, s32[4,8,1,32]{3,2,1,0:T(1,128)} %counts.1, s32[1,46]{1,0:T(1,128)} %bitcast.5, s32[4,2,4096]{2,1,0:T(2,128)} %bitcast.4, s32[4,4096]{1,0:T(4,128)} %inter.1), custom_call_target="tpu_custom_call" | custom-call | tf_op jit(solution)/shard_map/gather/pallas_call | solution.py:540
  30.2 51.0 %pairs.1 = (f32[8,4,3,8,128]{4,3,2,1,0:T(8,128)}, f32[16,4,3,8,128]{4,3,2,1,0:T(8,128)}) custom-call(s32[40,128]{1,0:T(8,128)} %get-tuple-element.11.list_ref, s32[8,4,8,1,32]{4,3,2,1,0:T(1,128)} %get-tuple-element.12.tally_ref, s32[1,46]{1,0:T(1,128)} %bitcast.6, f32[8,4,3,8,128]{4,3,2,1,0:T(8,128)} %get-tuple-element.13.rows_ref, ...), custom_call_target="tpu_custom_call" | custom-call | tf_op jit(solution)/shard_map/pairs/pallas_call | solution.py:508
  81.3 22.9 %scatter.1 = f32[4,3,8,128]{3,2,1,0:T(8,128)} custom-call(f32[8,4,3,8,128]{4,3,2,1,0:T(8,128)} %get-tuple-element.15.rows, f32[4,4,4,3,8,128]{5,4,3,2,1,0:T(8,128)} %bitcast.3), custom_call_target="tpu_custom_call" | custom-call | tf_op jit(solution)/shard_map/scatter/pallas_call | solution.py:559
  104.2 1.4 %copy.7 = f32[4,3,8,128]{3,2,1,0:T(8,128)} copy(f32[4,3,8,128]{3,2,1,0:T(8,128)} %scatter.1) | data formatting | bytes 98304

commit v4 on v0

v4 whole, which is shorter than its diff:
```python
import jax
import jax.numpy as jnp
from jax import lax
from jax.experimental import pallas as pl
from jax.experimental.pallas import tpu as pltpu
from jax.sharding import PartitionSpec as P

MESH = pl.DeviceIdType.MESH
ROWS, COLS, SIDE = 16, 8, 4
U, BEADS = 8, 128
CAP = 256
LABELS = 48
NR, NC = SIDE * COLS * U, ROWS * U
UNITS = 2 * NR
PAD = 4
WIDE = 4
BIG = 64.0
F32, BF16, I32 = jnp.float32, jnp.bfloat16, jnp.int32
ANY = pl.BlockSpec(memory_space=pl.ANY)
VMEM = pl.BlockSpec(memory_space=pltpu.VMEM)
SMEM = pl.BlockSpec(memory_space=pltpu.SMEM)
NT = (((1,), (1,)), ((), ()))
LISTED, TOTALS, WIDTHS, PLACE, TALLY, UNIT, LINES = 0, 16, 17, 19, 24, 88, 96


def iota(shape, axis):
    return lax.broadcasted_iota(I32, shape, axis)


def flag(x):
    return x.astype(F32).astype(BF16)


def chrom_bounds(lens_ref):
    lens = jnp.broadcast_to(lens_ref[...], (LABELS, lens_ref.shape[1]))
    sub, lane = iota(lens.shape, 0), iota(lens.shape, 1)
    ends = jnp.sum(jnp.where(lane <= sub, lens, 0), axis=1, keepdims=True)
    starts = jnp.sum(jnp.where(lane < sub, lens, 0), axis=1, keepdims=True)
    return starts, ends


def compact(mine, values, slots):
    count = mine.shape[0]
    a, b = iota((128, 128), 0), iota((128, 128), 1)
    within = jnp.dot(flag(mine), flag(a <= b), preferred_element_type=F32)
    total = jnp.dot(flag(mine), jnp.ones((128, 128), BF16), preferred_element_type=F32)
    lower = flag(iota((count, count), 1) < iota((count, count), 0))
    offset = jnp.dot(lower, total.astype(BF16), preferred_element_type=F32)
    place = jnp.where(mine, (offset + within).astype(I32) - 1, -1)
    values = [v.astype(F32) for v in values] + [mine.astype(F32)]
    slot = iota((slots, 128), 0)
    pad = jnp.zeros((16 - len(values), 128), F32)
    acc = jnp.zeros((16, slots), F32)
    for lo in range(0, count, 8):
        span = range(lo, min(lo + 8, count))
        hot = jnp.concatenate([flag(place[e:e + 1] == slot) for e in span], axis=1)
        rows = [jnp.concatenate([v[e:e + 1] for v in values] + [pad], axis=0) for e in span]
        acc = acc + lax.dot_general(jnp.concatenate(rows, axis=1).astype(BF16), hot, NT,
                                    preferred_element_type=F32)
    return acc[0:8]


def make_list(y, z, c, lens_ref, pairs_ref, count_ref, stage_ref, out_ref):
    for t in range(32):
        lane = slice(t * 128, t * 128 + 128)
        stage_ref[0, t:t + 1, :] = pairs_ref[0:1, lane]
        stage_ref[1, t:t + 1, :] = pairs_ref[1:2, lane]
        block = count_ref[:, lane]
        stage_ref[2, t:t + 1, :] = jnp.sum(jnp.where(iota(block.shape, 0) == y, block, 0), axis=0, keepdims=True)
    first, second, counts = stage_ref[0], stage_ref[1], stage_ref[2]
    mine = (((first >> 3) & 3) == z) & ((second & 7) == c)
    at = (first & 7) * 32 + ((first >> 5) & 3) * 8 + (first >> 7)
    acc = compact(mine, [at, second >> 3, counts], CAP)
    spare = jnp.where(iota((8, CAP), 0) == 1, NC * (1.0 - acc[3:4]), 0.0)
    found = (acc + spare).astype(I32)
    out_ref[LISTED:LISTED + 8, :] = found[:, 0:128]
    out_ref[LISTED + 8:LISTED + 16, :] = found[:, 128:256]

    starts, ends = chrom_bounds(lens_ref)
    widths = []
    for i in range(2):
        at = iota((1, 128), 1) + i * 128
        k = at >> 5
        block = (at & 7) * 128 + (((at >> 3) & 3) * 4 + z) * 8 + k
        last = jnp.broadcast_to(block * 128 + 127, (LABELS, 128))
        stop = jnp.min(jnp.where(ends > last, ends, 1 << 20), axis=0, keepdims=True)
        far = jnp.minimum(jnp.minimum((stop - 1) >> 7, block + 31), 1023)
        widths.append(((far - block - ((c - k) & 7)) >> 3) + 1)
    width = jnp.concatenate(widths + widths, axis=0)
    entry = iota((4, 128), 0) * 128 + iota((4, 128), 1)
    near = (entry < NR) & (width > 0) & (((entry >> 5) & 7) != c)
    live = near | ((entry >= NR) & (width > 2))
    acc = compact(live, [entry >> 2, entry & 3], UNITS)
    units = acc[0:1] * 4.0 + acc[1:2] + UNITS * (1.0 - acc[2:3])
    for i in range(4):
        out_ref[UNIT + i:UNIT + i + 1, :] = units[:, i * 128:i * 128 + 128].astype(I32)
    out_ref[UNIT + 4:UNIT + 8, :] = jnp.zeros((4, 128), I32)
    listed = jnp.sum(found[3:4].astype(F32), axis=1, keepdims=True).astype(I32)
    active = jnp.sum(acc[2:3], axis=1, keepdims=True).astype(I32)
    lane = iota((1, 128), 1)
    out_ref[TOTALS:TOTALS + 1, :] = jnp.where(lane == 0, listed, active)
    out_ref[WIDTHS:WIDTHS + 2, :] = jnp.zeros((2, 128), I32)
    out_ref[PLACE:PLACE + 1, :] = jnp.where(lane == 0, z, c)
    out_ref[PLACE + 1:TALLY, :] = jnp.zeros((4, 128), I32)


def greet(r, c):
    y, z = r // SIDE, lax.rem(r, SIDE)
    peers = [(r, lax.rem(c + d, COLS)) for d in range(1, COLS)]
    peers += [(lax.rem(y + d, SIDE) * SIDE + z, c) for d in range(1, SIDE)]
    peers += [(y * SIDE + lax.rem(z + d, SIDE), c) for d in range(1, SIDE)]
    barrier = pltpu.get_barrier_semaphore()
    for peer in peers:
        pl.semaphore_signal(barrier, 1, device_id=peer, device_id_type=MESH)
    pl.semaphore_wait(barrier, len(peers))


def gather_kernel(coords, counts, lens_ref, pairs, inter, rows, cols, list_ref,
                  pairs_ref, inter_ref, stage_ref, tallies, send, recv, local):
    r, c = lax.axis_index("row"), lax.axis_index("col")
    y, z = r // SIDE, lax.rem(r, SIDE)
    taken = [pltpu.make_async_copy(pairs.at[y], pairs_ref, local.at[0]),
             pltpu.make_async_copy(inter, inter_ref, local.at[1])]
    kept = [pltpu.make_async_copy(coords.at[y], rows.at[c, y], local.at[2]),
            pltpu.make_async_copy(counts.at[y], tallies.at[c, y], local.at[3])]
    for copy in kept + taken:
        copy.start()
    greet(r, c)

    def push(source, target, n, peer):
        return pltpu.make_async_remote_copy(source, target, send.at[n], recv.at[n],
                                            device_id=peer, device_id_type=MESH)

    early = []
    for d in (1, 3, 2):
        to = lax.rem(y + d, SIDE)
        peer = (to * SIDE + z, c)
        early.append(push(coords.at[to], rows.at[c, y], d, peer))
        early.append(push(counts.at[to], tallies.at[c, y], SIDE + d, peer))
    for copy in early:
        copy.start()
    for copy in kept:
        copy.wait()
    for copy in early:
        copy.wait_recv()
    same = pltpu.make_async_copy(rows.at[c], cols.at[z], local.at[4])
    same.start()
    late = []
    for d in (1, 3, 2):
        late.append(push(rows.at[c], cols.at[z], 2 * SIDE + d, (y * SIDE + lax.rem(z + d, SIDE), c)))
    for d in (4, 2, 6, 1, 3, 5, 7):
        late.append(push(rows.at[c], rows.at[c], 3 * SIDE + d, (r, lax.rem(c + d, COLS))))
    talk = []
    for d in range(1, COLS):
        talk.append(push(tallies.at[c], tallies.at[c], 3 * SIDE + COLS + d, (r, lax.rem(c + d, COLS))))
    for copy in late + talk:
        copy.start()
    for copy in taken:
        copy.wait()
    make_list(y, z, c, lens_ref, pairs_ref, inter_ref, stage_ref, list_ref)
    for copy in talk:
        copy.wait_recv()
    for k in range(COLS):
        for yy in range(SIDE):
            for u in range(U):
                at = TALLY + k * 8 + yy * 2 + u // 4
                list_ref[at:at + 1, (u % 4) * 32:(u % 4) * 32 + 32] = tallies[k, yy, u]
    for copy in early + talk:
        copy.wait_send()
    for copy in late:
        copy.wait()
    same.wait()


def scatter_kernel(rows, cols, out, land, own, total, last, send, recv, local):
    r, c = lax.axis_index("row"), lax.axis_index("col")
    y, z = r // SIDE, lax.rem(r, SIDE)
    kept = [pltpu.make_async_copy(rows.at[c], own.at[0], local.at[0]),
            pltpu.make_async_copy(cols.at[z], own.at[1], local.at[1])]
    for copy in kept:
        copy.start()
    greet(r, c)
    copies = []

    def push(source, target, n, peer):
        return pltpu.make_async_remote_copy(source, target, send.at[n], recv.at[n],
                                            device_id=peer, device_id_type=MESH)

    for d in (1, 3, 2):
        to = lax.rem(z + d, SIDE)
        copies.append(push(cols.at[to], land.at[d - 1], d, (y * SIDE + to, c)))
    for d in (4, 2, 6, 1, 3, 5, 7):
        to = lax.rem(c + d, COLS)
        copies.append(push(rows.at[to], land.at[SIDE - 2 + d], SIDE + d, (r, to)))
    for copy in copies:
        copy.start()
    for copy in kept:
        copy.wait()
    for copy in copies:
        copy.wait_recv()
    for i in range(SIDE):
        sums = own[0, i] + own[1, i]
        for d in range(SIDE + COLS - 2):
            sums = sums + land[d, i]
        total[i] = sums
    second = []
    for d in (1, 3, 2):
        to = lax.rem(y + d, SIDE)
        second.append(push(total.at[to], last.at[d - 1], SIDE + COLS + d, (to * SIDE + z, c)))
    for copy in second:
        copy.start()
    out[y] = total[y]
    for d, copy in zip((1, 3, 2), second):
        copy.wait_recv()
        out[lax.rem(y + SIDE - d, SIDE)] = last[d - 1]
    for copy in copies + second:
        copy.wait_send()


def split3(x):
    a = x.astype(BF16).astype(F32)
    b = (x - a).astype(BF16).astype(F32)
    return a, b, (x - a) - b


def points_of(x, y, z):
    c = 0.75 - 0.25 * (x * x + y * y + z * z)
    return split3(x), split3(y), split3(z), split3(c)


def pair_kernel(list_ref, lens_ref, rows_ref, cols_ref, prow_ref, pcol_ref,
                tile_ref, left_ref, lrow_ref, same_ref, differ_ref, arow_ref, acol_ref):
    z, c = list_ref[PLACE, 0], list_ref[PLACE, 1]
    starts, ends = chrom_bounds(lens_ref)
    starts = jnp.broadcast_to(starts, (LABELS, BEADS))
    ends = jnp.broadcast_to(ends, (LABELS, BEADS))
    lanes = iota((LABELS, BEADS), 1)
    eye = flag(iota((128, 128), 0) == iota((128, 128), 1))
    one = jnp.ones((8, 128), F32)
    nil = jnp.zeros((8, 128), F32)

    def hot_of(block):
        bead = lanes + block * BEADS
        return (bead >= starts) & (bead < ends)

    for v in range(SIDE):
        for u in range(U):
            for q in range(3):
                tile_ref[v, u, 8 * q:8 * q + 8] = nil
    for v in range(SIDE):
        tile_ref[v, :, 4, :] = one

    @pl.loop(0, COLS)
    def _(k):
        for yy in range(SIDE):
            parts = points_of(rows_ref[k, yy, 0], rows_ref[k, yy, 1], rows_ref[k, yy, 2])
            for q in range(3):
                for w in range(4):
                    value = parts[w][q]
                    tile_ref[yy, :, 8 * q + w, :] = 0.5 * value if w < 3 else value
        for yy in range(SIDE):
            for u in range(0, U, 2):
                fulls = []
                for i in range(2):
                    at = (k * SIDE + yy) * U + u + i
                    tiles = [tile_ref[yy, u + i, 8 * q:8 * q + 8] for q in range(3)]
                    full = jnp.concatenate([tiles[j] for j in (0, 0, 1, 0, 2, 1)], axis=0).astype(BF16)
                    hot = hot_of((u + i) * 128 + (4 * yy + z) * 8 + k)
                    fulls += [full, jnp.where(hot, 1.0, 0.0).astype(BF16), jnp.zeros((32, 128), BF16)]
                    lrow_ref[at] = jnp.concatenate(tiles[:2], axis=0).astype(BF16)
                flipped = lax.dot_general(eye, jnp.concatenate(fulls, axis=0), NT, preferred_element_type=F32)
                for i in range(2):
                    left_ref[(k * SIDE + yy) * U + u + i] = flipped[:, i * 128:i * 128 + 128].astype(BF16)

    for v in range(SIDE):
        tile_ref[v, :, 3, :] = one
        tile_ref[v, :, 11, :] = nil
        tile_ref[v, :, 19, :] = nil

    @pl.loop(0, SIDE)
    def _(zz):
        for yy in range(SIDE):
            parts = points_of(cols_ref[zz, yy, 0], cols_ref[zz, yy, 1], cols_ref[zz, yy, 2])
            for q in range(3):
                for w in range(4):
                    tile_ref[yy, :, 8 * q + (w if w < 3 else 4), :] = parts[w][q]
        for yy in range(SIDE):
            for u in range(U):
                at = u * ROWS + 4 * yy + zz
                tiles = [tile_ref[yy, u, 8 * q:8 * q + 8] for q in range(3)]
                full = jnp.concatenate([tiles[i] for i in (0, 1, 0, 2, 0, 1)], axis=0).astype(BF16)
                hot = hot_of(at * 8 + c)
                same_ref[at, 0:LABELS] = full
                differ_ref[at, 0:LABELS] = full
                same_ref[at, LABELS:] = jnp.where(hot, 0.0, -BIG).astype(BF16)
                differ_ref[at, LABELS:] = jnp.where(hot, -BIG, 0.0).astype(BF16)

    apart = jnp.concatenate([jnp.zeros((LABELS, BEADS), BF16), jnp.full((LABELS, BEADS), -BIG, BF16)], axis=0)
    for p in range(PAD):
        same_ref[NC + p] = apart
    differ_ref[NC] = apart

    @pl.loop(0, (NC + PAD) // 4)
    def _(i):
        for j in range(4):
            acol_ref[i * 4 + j] = nil

    @pl.loop(0, NR // 8)
    def _(i):
        for j in range(8):
            arow_ref[i * 8 + j] = nil

    triangle = iota((128, 128), 0) < iota((128, 128), 1)
    empty = jnp.zeros((16, 128), BF16)

    def finish(z, diagonal=False):
        t = jnp.tanh(z)
        if diagonal:
            t = jnp.concatenate([jnp.where(triangle, t[:, :128], -1.0), t[:, 128:]], axis=1)
        return jnp.sum(t, axis=0, keepdims=True), (1.0 - t * t).astype(BF16)

    def weigh(sums, n):
        expect = 0.5 + (0.5 * (16384.0 + jnp.sum(sums, axis=1, keepdims=True))) / 128.0
        n = jnp.full((1, 128), n, I32).astype(F32)
        return jnp.broadcast_to(1.0 - n / jnp.broadcast_to(expect, (1, 128)), (8, 128))

    def unit_drain(g, sums, at, start, counts):
        far = [same_ref[start + m, 0:16] for m in range(2)]
        o = jnp.dot(lrow_ref[at], g, preferred_element_type=F32)
        spread = jnp.concatenate([jnp.concatenate([far[0], empty], axis=1),
                                  jnp.concatenate([empty, far[1]], axis=1)], axis=0)
        p = lax.dot_general(spread, g, NT, preferred_element_type=F32)
        w = [weigh(sums[:, m * 128:m * 128 + 128], counts[m]) for m in range(2)]
        arow_ref[at] += w[0] * (p[0:8] + p[8:16]) + w[1] * (p[16:24] + p[24:32])
        for m in range(2):
            lane = slice(m * 128, m * 128 + 128)
            acol_ref[start + m] += w[m] * (o[0:8, lane] + o[8:16, lane])

    def run(unit_at, trips, diagonal):
        def body(it, held):
            for q in range(2):
                zs, now = [], []
                for i in range(WIDE):
                    entry = unit_at(it * 2 * WIDE + q * WIDE + i)
                    at, half = entry & (NR - 1), entry >> 8
                    k, u = at >> 5, at & 7
                    start = u * ROWS + 4 * ((at >> 3) & 3) + z + jnp.where(k > c, 1, 0) + 2 * half
                    start = jnp.where(entry < UNITS, start, NC)
                    lane = (at & 3) * 32 + ((c - k) & 7) + 16 * half
                    counts = [list_ref[TALLY + (at >> 2), lane + 8 * m] for m in range(2)]
                    right = jnp.concatenate([same_ref[start], same_ref[start + 1]], axis=1)
                    zs.append(jnp.dot(left_ref[at, :, 0:2 * LABELS], right, preferred_element_type=F32))
                    now.append((at, start, counts))
                for entry in held:
                    unit_drain(*entry)
                done = [finish(v, diagonal) for v in zs]
                held = [(done[i][1], done[i][0]) + now[i] for i in range(WIDE)]
            return held

        zero = jnp.int32(0)
        first = [(jnp.zeros((128, 256), BF16), jnp.zeros((1, 256), F32), zero, zero, [zero, zero])
                 for _ in range(WIDE)]
        for entry in lax.fori_loop(0, trips, body, first):
            unit_drain(*entry)

    run(lambda i: c * (SIDE * U) + i, SIDE * U // (2 * WIDE), True)
    run(lambda i: list_ref[UNIT + (i >> 7), i & 127], (list_ref[TOTALS, 1] + 2 * WIDE - 1) // (2 * WIDE), False)

    def listed_drain(held):
        for lo in range(0, WIDE, 2):
            pair = held[lo:lo + 2]
            near = jnp.concatenate([lrow_ref[p[2]] for p in pair], axis=0)
            far = jnp.concatenate([differ_ref[p[3], 0:16] for p in pair], axis=0)
            o = jnp.dot(near, jnp.concatenate([p[0] for p in pair], axis=1), preferred_element_type=F32)
            v = lax.dot_general(far, jnp.concatenate([p[0] for p in pair], axis=0), NT,
                                preferred_element_type=F32)
            for m, p in enumerate(pair):
                lane, at = slice(m * 128, m * 128 + 128), m * 16
                w = weigh(p[1], p[4])
                arow_ref[p[2]] += w * (v[at:at + 8, lane] + v[at + 8:at + 16, lane])
                acol_ref[p[3]] += w * (o[at:at + 8, lane] + o[at + 8:at + 16, lane])

    def listed_body(it, held):
        for q in range(2):
            zs, now = [], []
            for i in range(WIDE):
                slot = it * 2 * WIDE + q * WIDE + i
                line, lane = LISTED + (slot >> 7) * 8, slot & 127
                at, to, n = [list_ref[line + f, lane] for f in range(3)]
                zs.append(jnp.dot(left_ref[at, :, 0:2 * LABELS], differ_ref[to], preferred_element_type=F32))
                now.append((at, to, n))
            listed_drain(held)
            done = [finish(v) for v in zs]
            held = [(done[i][1], done[i][0]) + now[i] for i in range(WIDE)]
        return held

    zero = jnp.int32(0)
    first = [(jnp.zeros((128, 128), BF16), jnp.zeros((1, 128), F32), zero, zero, zero) for _ in range(WIDE)]
    listed_drain(lax.fori_loop(0, (list_ref[TOTALS, 0] + 2 * WIDE - 1) // (2 * WIDE), listed_body, first))

    @pl.loop(0, COLS)
    def _(k):
        for yy in range(SIDE):
            here = pl.ds((k * SIDE + yy) * U, U)
            mass = arow_ref[here, 3, :]
            for w in range(3):
                pulled = rows_ref[k, yy, w] * mass - arow_ref[here, w, :]
                prow_ref[k, yy, w] = pulled * (-1.0 / 512.0)

    @pl.loop(0, SIDE)
    def _(zz):
        for yy in range(SIDE):
            here = pl.ds(4 * yy + zz, U, stride=ROWS)
            mass = acol_ref[here, 4, :]
            for w in range(3):
                pulled = cols_ref[zz, yy, w] * mass - 2.0 * acol_ref[here, w, :]
                pcol_ref[zz, yy, w] = pulled * (-1.0 / 512.0)


def pairs_call(listing, lens, rows, cols):
    return pl.pallas_call(
        pair_kernel,
        out_shape=[jax.ShapeDtypeStruct(rows.shape, F32), jax.ShapeDtypeStruct(cols.shape, F32)],
        in_specs=[SMEM] + [VMEM] * 3, out_specs=[VMEM] * 2,
        scratch_shapes=[
            pltpu.VMEM((SIDE, U, 24, BEADS), F32),
            pltpu.VMEM((NR, BEADS, 128), BF16),
            pltpu.VMEM((NR, 16, BEADS), BF16),
            pltpu.VMEM((NC + PAD + 2, 2 * LABELS, BEADS), BF16),
            pltpu.VMEM((NC + 1, 2 * LABELS, BEADS), BF16),
            pltpu.VMEM((NR, 8, BEADS), F32),
            pltpu.VMEM((NC + PAD + 2, 8, BEADS), F32),
        ],
        compiler_params=pltpu.CompilerParams(vmem_limit_bytes=60 << 20),
        name="pairs",
    )(listing, lens, rows, cols)


def on_device(coords, chrom_lengths, band_counts, inter_pairs, inter_counts):
    part = coords.shape[1:]
    lens = chrom_lengths.reshape(1, -1)
    flipped = jnp.transpose(inter_pairs, (0, 2, 1))
    sems = 3 * SIDE + 2 * COLS
    rows, cols, listing = pl.pallas_call(
        gather_kernel,
        out_shape=[jax.ShapeDtypeStruct((COLS, SIDE) + part, F32), jax.ShapeDtypeStruct((SIDE, SIDE) + part, F32),
                   jax.ShapeDtypeStruct((LINES, 128), I32)],
        in_specs=[ANY] * 2 + [VMEM] + [ANY] * 2, out_specs=[ANY] * 2 + [VMEM],
        scratch_shapes=[
            pltpu.VMEM(flipped.shape[1:], I32),
            pltpu.VMEM(inter_counts.shape, I32),
            pltpu.VMEM((3, 32, 128), I32),
            pltpu.VMEM((COLS,) + band_counts.shape, I32),
            pltpu.SemaphoreType.DMA((sems,)),
            pltpu.SemaphoreType.DMA((sems,)),
            pltpu.SemaphoreType.DMA((5,)),
        ],
        compiler_params=pltpu.CompilerParams(collective_id=0, has_side_effects=True),
        name="gather",
    )(coords, band_counts, lens, flipped, inter_counts)
    prow, pcol = pairs_call(listing, lens, rows, cols)
    return pl.pallas_call(
        scatter_kernel,
        out_shape=jax.ShapeDtypeStruct(coords.shape, F32),
        in_specs=[ANY] * 2, out_specs=VMEM,
        scratch_shapes=[
            pltpu.VMEM((SIDE + COLS - 2, SIDE) + part, F32),
            pltpu.VMEM((2, SIDE) + part, F32),
            pltpu.VMEM((SIDE,) + part, F32),
            pltpu.VMEM((SIDE - 1,) + part, F32),
            pltpu.SemaphoreType.DMA((2 * SIDE + COLS,)),
            pltpu.SemaphoreType.DMA((2 * SIDE + COLS,)),
            pltpu.SemaphoreType.DMA((2,)),
        ],
        compiler_params=pltpu.CompilerParams(collective_id=1, has_side_effects=True),
        name="scatter",
    )(prow, pcol)


def solution(mesh):
    placed = (P(None, None, None, ("row", "col")), P(), P(None, None, ("row", "col"), None), P(), P())
    return jax.shard_map(on_device, mesh=mesh, in_specs=placed,
                         out_specs=P(None, None, None, ("row", "col")), check_vma=False)
```

time: 700 us -> 77 us (0.11)
  other arithmetic: 409 us -> 0 us
  waiting for transfers between devices: 100 us -> 0 us
  local copies, waits for them, and re-layouts: 89.2 us -> 1.42 us
  Pallas kernels: 0 us -> 75.2 us
  blocking collectives: 55.8 us -> 0 us
  loops' own time: 21.3 us -> 0 us
  between operations: 13.4 us -> 0.02 us
  matrix products: 8.08 us -> 0 us
    reduce_sum x44 -> x0, other arithmetic: 335 us -> none  [the longest x9 160 us: pair_tiles(): return (jnp.sum(pair_force, axis=4), -jnp.sum(pair_force, axis=3))]
    unnamed x3 -> x0, waiting for transfers between devices: 76.8 us -> none
    pallas_call x0 -> x3, Pallas kernels: none -> 75.2 us  [the longest x1 37.7 us: pairs_call(): pl.pallas_call(pair_kernel, out_shape=[jax.ShapeDtypeStruct(rows.shape, F...]
    mul x43 -> x0, other arithmetic: 59.6 us -> none  [the longest x18 50 us: pair_tiles(): -2.0 * CONTACT_SLOPE / block_size * (masked * (1.0 - chance))]
    all_gather x3 -> x0, blocking collectives: 55.8 us -> none  [the longest x1 21.4 us: on_device(): column_points = lax.all_gather(local_points, 'row', axis=2, tiled=True)]
    gather x35 -> x0, local copies, waits for them, and re-layouts: 36.6 us -> none  [the longest x8 14.6 us: sweep(): second_points = jnp.take(column_flat, up_index, axis=2)]
    reduce_scatter x1 -> x0, waiting for transfers between devices: 23.4 us -> none  [on_device(): lax.psum_scatter(row_total, 'col', scatter_dimension=2, tiled=True)]
    dynamic_update_slice x16 -> x0, local copies, waits for them, and re-layouts: 22.6 us -> none  [on_device(): lax.scan(sweep, column_total, jnp.arange(sweeps, dtype=jnp.int32))]
  transfers between devices with their start and end apart: 2 -> 0, of which waited for: 2 -> 0; matrix products, arithmetic and copies ran while one was open for 0% -> 0% of each run, Pallas kernels for 0% -> 0%
where the time goes in v4:
time: 77 us; the launch traced here: 76.7 us
  Pallas kernels  75.2 us (98%)
  local copies, waits for them, and re-layouts  1.42 us (2%)
    pallas_call x1, Pallas kernels, pairs_call(): pl.pallas_call(pair_kernel, out_shape=[jax.ShapeDtypeStruct(rows.shape, F...  37.7 us
    pallas_call x1, Pallas kernels, on_device(): pl.pallas_call(gather_kernel, out_shape=[jax.ShapeDtypeStruct((COLS, SIDE...  21 us
    pallas_call x1, Pallas kernels, on_device(): pl.pallas_call(scatter_kernel, out_shape=jax.ShapeDtypeStruct(coords.shap...  16.6 us

profile of v4, /device:TPU:1, one launch (start us, length us, event | category | flops | bytes accessed | tf_op | source)
XLA Modules:
  0.0 76.7 jit_solution(9764148219554584040)
XLA Ops:
  0.0 21.0 %gather.1 = (f32[8,4,3,8,128]{4,3,2,1,0:T(8,128)}, f32[4,4,3,8,128]{4,3,2,1,0:T(8,128)}, s32[96,128]{1,0:T(8,128)}) custom-call(f32[4,3,8,128]{3,2,1,0:T(8,128)} %coords.1, s32[4,8,1,32]{3,2,1,0:T(1,128)} %counts.1, s32[1,46]{1,0:T(1,128)} %bitcast.3, s32[4,2,4096]{2,1,0:T(2,128)} %bitcast.2, s32[4,4096]{1,0:T(4,128)} %inter.1), custom_call_target="tpu_custom_call" | custom-call | tf_op jit(solution)/shard_map/gather/pallas_call | solution.py:444
  21.0 37.7 %pairs.1 = (f32[8,4,3,8,128]{4,3,2,1,0:T(8,128)}, f32[4,4,3,8,128]{4,3,2,1,0:T(8,128)}) custom-call(s32[96,128]{1,0:T(8,128)} %get-tuple-element.10.list_ref, s32[1,46]{1,0:T(1,128)} %bitcast.4, f32[8,4,3,8,128]{4,3,2,1,0:T(8,128)} %get-tuple-element.11.rows_ref, f32[4,4,3,8,128]{4,3,2,1,0:T(8,128)} %get-tuple-element.12.cols_ref), custom_call_target="tpu_custom_call" | custom-call | tf_op jit(solution)/shard_map/pairs/pallas_call | solution.py:421
  58.6 16.6 %scatter.1 = f32[4,3,8,128]{3,2,1,0:T(8,128)} custom-call(f32[8,4,3,8,128]{4,3,2,1,0:T(8,128)} %get-tuple-element.13.rows, f32[4,4,3,8,128]{4,3,2,1,0:T(8,128)} %get-tuple-element.14.cols), custom_call_target="tpu_custom_call" | custom-call | tf_op jit(solution)/shard_map/scatter/pallas_call | solution.py:462
  75.3 1.4 %copy.7 = f32[4,3,8,128]{3,2,1,0:T(8,128)} copy(f32[4,3,8,128]{3,2,1,0:T(8,128)} %scatter.1) | data formatting | bytes 98304

commit v5 on v4

--- a/solution.py
+++ b/solution.py
@@ -16,7 +16,7 @@
 WIDE = 4
 BIG = 64.0
 F32, BF16, I32 = jnp.float32, jnp.bfloat16, jnp.int32
-ANY = pl.BlockSpec(memory_space=pl.ANY)
+HBM = pl.BlockSpec(memory_space=pltpu.HBM)
 VMEM = pl.BlockSpec(memory_space=pltpu.VMEM)
 SMEM = pl.BlockSpec(memory_space=pltpu.SMEM)
 NT = (((1,), (1,)), ((), ()))
@@ -60,7 +60,7 @@
     return acc[0:8]
 
 
-def make_list(y, z, c, lens_ref, pairs_ref, count_ref, stage_ref, out_ref):
+def make_list(y, z, c, lens_ref, pairs_ref, count_ref, stage_ref, out_ref, bounds_ref):
     for t in range(32):
         lane = slice(t * 128, t * 128 + 128)
         stage_ref[0, t:t + 1, :] = pairs_ref[0:1, lane]
@@ -77,6 +77,8 @@
     out_ref[LISTED + 8:LISTED + 16, :] = found[:, 128:256]
 
     starts, ends = chrom_bounds(lens_ref)
+    bounds_ref[0] = jnp.broadcast_to(starts, (LABELS, BEADS))
+    bounds_ref[1] = jnp.broadcast_to(ends, (LABELS, BEADS))
     widths = []
     for i in range(2):
         at = iota((1, 128), 1) + i * 128
@@ -115,12 +117,13 @@
     pl.semaphore_wait(barrier, len(peers))
 
 
-def gather_kernel(coords, counts, lens_ref, pairs, inter, rows, cols, list_ref,
-                  pairs_ref, inter_ref, stage_ref, tallies, send, recv, local):
+def gather_kernel(coords, counts, lens, pairs, inter, rows, cols, list_ref, bounds_ref,
+                  lens_ref, pairs_ref, inter_ref, stage_ref, tallies, send, recv, local):
     r, c = lax.axis_index("row"), lax.axis_index("col")
     y, z = r // SIDE, lax.rem(r, SIDE)
     taken = [pltpu.make_async_copy(pairs.at[y], pairs_ref, local.at[0]),
-             pltpu.make_async_copy(inter, inter_ref, local.at[1])]
+             pltpu.make_async_copy(inter, inter_ref, local.at[1]),
+             pltpu.make_async_copy(lens, lens_ref, local.at[5])]
     kept = [pltpu.make_async_copy(coords.at[y], rows.at[c, y], local.at[2]),
             pltpu.make_async_copy(counts.at[y], tallies.at[c, y], local.at[3])]
     for copy in kept + taken:
@@ -157,7 +160,7 @@
         copy.start()
     for copy in taken:
         copy.wait()
-    make_list(y, z, c, lens_ref, pairs_ref, inter_ref, stage_ref, list_ref)
+    make_list(y, z, c, lens_ref, pairs_ref, inter_ref, stage_ref, list_ref, bounds_ref)
     for copy in talk:
         copy.wait_recv()
     for k in range(COLS):
@@ -228,12 +231,10 @@
     return split3(x), split3(y), split3(z), split3(c)
 
 
-def pair_kernel(list_ref, lens_ref, rows_ref, cols_ref, prow_ref, pcol_ref,
+def pair_kernel(list_ref, bounds_ref, rows_ref, cols_ref, prow_ref, pcol_ref,
                 tile_ref, left_ref, lrow_ref, same_ref, differ_ref, arow_ref, acol_ref):
     z, c = list_ref[PLACE, 0], list_ref[PLACE, 1]
-    starts, ends = chrom_bounds(lens_ref)
-    starts = jnp.broadcast_to(starts, (LABELS, BEADS))
-    ends = jnp.broadcast_to(ends, (LABELS, BEADS))
+    starts, ends = bounds_ref[0], bounds_ref[1]
     lanes = iota((LABELS, BEADS), 1)
     eye = flag(iota((128, 128), 0) == iota((128, 128), 1))
     one = jnp.ones((8, 128), F32)
@@ -417,7 +418,7 @@
                 pcol_ref[zz, yy, w] = pulled * (-1.0 / 512.0)
 
 
-def pairs_call(listing, lens, rows, cols):
+def pairs_call(listing, bounds, rows, cols):
     return pl.pallas_call(
         pair_kernel,
         out_shape=[jax.ShapeDtypeStruct(rows.shape, F32), jax.ShapeDtypeStruct(cols.shape, F32)],
@@ -431,9 +432,9 @@
             pltpu.VMEM((NR, 8, BEADS), F32),
             pltpu.VMEM((NC + PAD + 2, 8, BEADS), F32),
         ],
-        compiler_params=pltpu.CompilerParams(vmem_limit_bytes=60 << 20),
+        compiler_params=pltpu.CompilerParams(vmem_limit_bytes=32 << 20),
         name="pairs",
-    )(listing, lens, rows, cols)
+    )(listing, bounds, rows, cols)
 
 
 def on_device(coords, chrom_lengths, band_counts, inter_pairs, inter_counts):
@@ -441,28 +442,30 @@
     lens = chrom_lengths.reshape(1, -1)
     flipped = jnp.transpose(inter_pairs, (0, 2, 1))
     sems = 3 * SIDE + 2 * COLS
-    rows, cols, listing = pl.pallas_call(
+    rows, cols, listing, bounds = pl.pallas_call(
         gather_kernel,
         out_shape=[jax.ShapeDtypeStruct((COLS, SIDE) + part, F32), jax.ShapeDtypeStruct((SIDE, SIDE) + part, F32),
-                   jax.ShapeDtypeStruct((LINES, 128), I32)],
-        in_specs=[ANY] * 2 + [VMEM] + [ANY] * 2, out_specs=[ANY] * 2 + [VMEM],
+                   jax.ShapeDtypeStruct((LINES, 128), I32), jax.ShapeDtypeStruct((2, LABELS, BEADS), I32)],
+        in_specs=[HBM] * 5, out_specs=[VMEM] * 4,
         scratch_shapes=[
+            pltpu.VMEM(lens.shape, I32),
             pltpu.VMEM(flipped.shape[1:], I32),
             pltpu.VMEM(inter_counts.shape, I32),
             pltpu.VMEM((3, 32, 128), I32),
             pltpu.VMEM((COLS,) + band_counts.shape, I32),
             pltpu.SemaphoreType.DMA((sems,)),
             pltpu.SemaphoreType.DMA((sems,)),
-            pltpu.SemaphoreType.DMA((5,)),
+            pltpu.SemaphoreType.DMA((6,)),
         ],
-        compiler_params=pltpu.CompilerParams(collective_id=0, has_side_effects=True),
+        compiler_params=pltpu.CompilerParams(collective_id=0, has_side_effects=True, vmem_limit_bytes=24 << 20),
         name="gather",
-    )(coords, band_counts, lens, flipped, inter_counts)
-    prow, pcol = pairs_call(listing, lens, rows, cols)
+    )(*[pltpu.with_memory_space_constraint(v, pltpu.HBM)
+        for v in (coords, band_counts, lens, flipped, inter_counts)])
+    prow, pcol = pairs_call(listing, bounds, rows, cols)
     return pl.pallas_call(
         scatter_kernel,
         out_shape=jax.ShapeDtypeStruct(coords.shape, F32),
-        in_specs=[ANY] * 2, out_specs=VMEM,
+        in_specs=[VMEM] * 2, out_specs=VMEM,
         scratch_shapes=[
             pltpu.VMEM((SIDE + COLS - 2, SIDE) + part, F32),
             pltpu.VMEM((2, SIDE) + part, F32),
@@ -472,7 +475,7 @@
             pltpu.SemaphoreType.DMA((2 * SIDE + COLS,)),
             pltpu.SemaphoreType.DMA((2,)),
         ],
-        compiler_params=pltpu.CompilerParams(collective_id=1, has_side_effects=True),
+        compiler_params=pltpu.CompilerParams(collective_id=1, has_side_effects=True, vmem_limit_bytes=24 << 20),
         name="scatter",
     )(prow, pcol)
 

time: 77 us -> 71.6 us (0.930)
  Pallas kernels: 75.2 us -> 70.6 us
  local copies, waits for them, and re-layouts: 1.42 us -> 0.62 us
    pallas_call x1, Pallas kernels: 16.6 us -> 13.9 us  [on_device(): pl.pallas_call(scatter_kernel, out_shape=jax.ShapeDtypeStruct(coords.shap...]
    pallas_call x1, Pallas kernels: 21 us -> 19.4 us  [on_device(): pl.pallas_call(gather_kernel, out_shape=[jax.ShapeDtypeStruct((COLS, SIDE...]
    unnamed x1, local copies, waits for them, and re-layouts: 1.42 us -> 0.62 us
where the time goes in v5:
time: 71.6 us; the launch traced here: 71.2 us
  Pallas kernels  70.6 us (99%)
    pallas_call x1, Pallas kernels, pairs_call(): pl.pallas_call(pair_kernel, out_shape=[jax.ShapeDtypeStruct(rows.shape, F...  37.3 us
    pallas_call x1, Pallas kernels, on_device(): pl.pallas_call(gather_kernel, out_shape=[jax.ShapeDtypeStruct((COLS, SIDE...  19.4 us
    pallas_call x1, Pallas kernels, on_device(): pl.pallas_call(scatter_kernel, out_shape=jax.ShapeDtypeStruct(coords.shap...  13.9 us

profile of v5, /device:TPU:1, one launch (start us, length us, event | category | flops | bytes accessed | tf_op | source)
XLA Modules:
  0.0 71.2 jit_solution(2219221660837278027)
XLA Ops:
  0.0 19.4 %gather.1 = (f32[8,4,3,8,128]{4,3,2,1,0:T(8,128)S(1)}, f32[4,4,3,8,128]{4,3,2,1,0:T(8,128)S(1)}, s32[96,128]{1,0:T(8,128)S(1)}, s32[2,48,128]{2,1,0:T(8,128)S(1)}) custom-call(f32[4,3,8,128]{3,2,1,0:T(8,128)} %coords.1, s32[4,8,1,32]{3,2,1,0:T(1,128)} %counts.1, s32[1,46]{1,0:T(1,128)} %bitcast.3, s32[4,2,4096]{2,1,0:T(2,128)} %bitcast.2, s32[4,4096]{1,0:T(4,128)} %inter.1), custom_call_target="tpu_custom_call" | custom-call | tf_op jit(solution)/shard_map/gather/pallas_call | solution.py:445
  19.4 37.3 %pairs.1 = (f32[8,4,3,8,128]{4,3,2,1,0:T(8,128)S(1)}, f32[4,4,3,8,128]{4,3,2,1,0:T(8,128)S(1)}) custom-call(s32[96,128]{1,0:T(8,128)S(1)} %get-tuple-element.11.list_ref, s32[2,48,128]{2,1,0:T(8,128)S(1)} %get-tuple-element.12.bounds_ref, f32[8,4,3,8,128]{4,3,2,1,0:T(8,128)S(1)} %get-tuple-element.13.rows_ref, ...), custom_call_target="tpu_custom_call" | custom-call | tf_op jit(solution)/shard_map/pairs/pallas_call | solution.py:422
  56.7 13.9 %scatter.1 = f32[4,3,8,128]{3,2,1,0:T(8,128)S(1)} custom-call(f32[8,4,3,8,128]{4,3,2,1,0:T(8,128)S(1)} %get-tuple-element.15.rows, f32[4,4,3,8,128]{4,3,2,1,0:T(8,128)S(1)} %get-tuple-element.16.cols), custom_call_target="tpu_custom_call" | custom-call | tf_op jit(solution)/shard_map/scatter/pallas_call | solution.py:465
  70.6 0.6 copy.7

commit v6 on v5

--- a/solution.py
+++ b/solution.py
@@ -14,6 +14,7 @@
 UNITS = 2 * NR
 PAD = 4
 WIDE = 4
+LONG, SHORT = 12, 2
 BIG = 64.0
 F32, BF16, I32 = jnp.float32, jnp.bfloat16, jnp.int32
 HBM = pl.BlockSpec(memory_space=pltpu.HBM)
@@ -269,9 +270,9 @@
                     hot = hot_of((u + i) * 128 + (4 * yy + z) * 8 + k)
                     fulls += [full, jnp.where(hot, 1.0, 0.0).astype(BF16), jnp.zeros((32, 128), BF16)]
                     lrow_ref[at] = jnp.concatenate(tiles[:2], axis=0).astype(BF16)
-                flipped = lax.dot_general(eye, jnp.concatenate(fulls, axis=0), NT, preferred_element_type=F32)
+                flipped = [jnp.concatenate(fulls[i * 3:i * 3 + 3], axis=0).T for i in range(2)]
                 for i in range(2):
-                    left_ref[(k * SIDE + yy) * U + u + i] = flipped[:, i * 128:i * 128 + 128].astype(BF16)
+                    left_ref[(k * SIDE + yy) * U + u + i] = flipped[i]
 
     for v in range(SIDE):
         tile_ref[v, :, 3, :] = one
@@ -337,12 +338,12 @@
             lane = slice(m * 128, m * 128 + 128)
             acol_ref[start + m] += w[m] * (o[0:8, lane] + o[8:16, lane])
 
-    def run(unit_at, trips, diagonal):
+    def run(held, unit_at, trips, turns, diagonal):
         def body(it, held):
-            for q in range(2):
+            for q in range(turns):
                 zs, now = [], []
                 for i in range(WIDE):
-                    entry = unit_at(it * 2 * WIDE + q * WIDE + i)
+                    entry = unit_at((it * turns + q) * WIDE + i)
                     at, half = entry & (NR - 1), entry >> 8
                     k, u = at >> 5, at & 7
                     start = u * ROWS + 4 * ((at >> 3) & 3) + z + jnp.where(k > c, 1, 0) + 2 * half
@@ -358,14 +359,22 @@
                 held = [(done[i][1], done[i][0]) + now[i] for i in range(WIDE)]
             return held
 
-        zero = jnp.int32(0)
-        first = [(jnp.zeros((128, 256), BF16), jnp.zeros((1, 256), F32), zero, zero, [zero, zero])
-                 for _ in range(WIDE)]
-        for entry in lax.fori_loop(0, trips, body, first):
-            unit_drain(*entry)
-
-    run(lambda i: c * (SIDE * U) + i, SIDE * U // (2 * WIDE), True)
-    run(lambda i: list_ref[UNIT + (i >> 7), i & 127], (list_ref[TOTALS, 1] + 2 * WIDE - 1) // (2 * WIDE), False)
+        return lax.fori_loop(0, trips, body, held)
+
+    def split(count):
+        whole = count // (WIDE * LONG)
+        done = whole * (WIDE * LONG)
+        return whole, done, (count - done + WIDE * SHORT - 1) // (WIDE * SHORT)
+
+    zero = jnp.int32(0)
+    held = [(jnp.zeros((128, 256), BF16), jnp.zeros((1, 256), F32), zero, zero, [zero, zero])
+            for _ in range(WIDE)]
+    held = run(held, lambda i: c * (SIDE * U) + i, 1, SIDE * U // WIDE, True)
+    whole, done, rest = split(list_ref[TOTALS, 1])
+    held = run(held, lambda i: list_ref[UNIT + (i >> 7), i & 127], whole, LONG, False)
+    held = run(held, lambda i: list_ref[UNIT + ((i + done) >> 7), (i + done) & 127], rest, SHORT, False)
+    for entry in held:
+        unit_drain(*entry)
 
     def listed_drain(held):
         for lo in range(0, WIDE, 2):
@@ -381,23 +390,27 @@
                 arow_ref[p[2]] += w * (v[at:at + 8, lane] + v[at + 8:at + 16, lane])
                 acol_ref[p[3]] += w * (o[at:at + 8, lane] + o[at + 8:at + 16, lane])
 
-    def listed_body(it, held):
-        for q in range(2):
-            zs, now = [], []
-            for i in range(WIDE):
-                slot = it * 2 * WIDE + q * WIDE + i
-                line, lane = LISTED + (slot >> 7) * 8, slot & 127
-                at, to, n = [list_ref[line + f, lane] for f in range(3)]
-                zs.append(jnp.dot(left_ref[at, :, 0:2 * LABELS], differ_ref[to], preferred_element_type=F32))
-                now.append((at, to, n))
-            listed_drain(held)
-            done = [finish(v) for v in zs]
-            held = [(done[i][1], done[i][0]) + now[i] for i in range(WIDE)]
-        return held
-
-    zero = jnp.int32(0)
-    first = [(jnp.zeros((128, 128), BF16), jnp.zeros((1, 128), F32), zero, zero, zero) for _ in range(WIDE)]
-    listed_drain(lax.fori_loop(0, (list_ref[TOTALS, 0] + 2 * WIDE - 1) // (2 * WIDE), listed_body, first))
+    def listed_run(held, offset, trips, laps):
+        def body(it, held):
+            for q in range(laps):
+                zs, now = [], []
+                for i in range(WIDE):
+                    slot = offset + (it * laps + q) * WIDE + i
+                    line, lane = LISTED + (slot >> 7) * 8, slot & 127
+                    at, to, n = [list_ref[line + f, lane] for f in range(3)]
+                    zs.append(jnp.dot(left_ref[at, :, 0:2 * LABELS], differ_ref[to], preferred_element_type=F32))
+                    now.append((at, to, n))
+                listed_drain(held)
+                done = [finish(v) for v in zs]
+                held = [(done[i][1], done[i][0]) + now[i] for i in range(WIDE)]
+            return held
+
+        return lax.fori_loop(0, trips, body, held)
+
+    held = [(jnp.zeros((128, 128), BF16), jnp.zeros((1, 128), F32), zero, zero, zero) for _ in range(WIDE)]
+    whole, done, rest = split(list_ref[TOTALS, 0])
+    held = listed_run(held, 0, whole, LONG)
+    listed_drain(listed_run(held, done, rest, SHORT))
 
     @pl.loop(0, COLS)
     def _(k):

time: 71.6 us -> 62.3 us (0.87)
  Pallas kernels: 70.6 us -> 61.1 us
    pallas_call x1, Pallas kernels: 37.3 us -> 29.5 us  [pairs_call(): pl.pallas_call(pair_kernel, out_shape=[jax.ShapeDtypeStruct(rows.shape, F...]
    pallas_call x1, Pallas kernels: 13.9 us -> 12.2 us  [on_device(): pl.pallas_call(scatter_kernel, out_shape=jax.ShapeDtypeStruct(coords.shap...]
where the time goes in v6:
time: 62.3 us; the launch traced here: 61.8 us
  Pallas kernels  61.1 us (98%)
    pallas_call x1, Pallas kernels, pairs_call(): pl.pallas_call(pair_kernel, out_shape=[jax.ShapeDtypeStruct(rows.shape, F...  29.5 us
    pallas_call x1, Pallas kernels, on_device(): pl.pallas_call(gather_kernel, out_shape=[jax.ShapeDtypeStruct((COLS, SIDE...  19.4 us
    pallas_call x1, Pallas kernels, on_device(): pl.pallas_call(scatter_kernel, out_shape=jax.ShapeDtypeStruct(coords.shap...  12.2 us

profile of v6, /device:TPU:1, one launch (start us, length us, event | category | flops | bytes accessed | tf_op | source)
XLA Modules:
  0.0 61.8 jit_solution(14482616242358917259)
XLA Ops:
  0.0 19.4 %gather.1 = (f32[8,4,3,8,128]{4,3,2,1,0:T(8,128)S(1)}, f32[4,4,3,8,128]{4,3,2,1,0:T(8,128)S(1)}, s32[96,128]{1,0:T(8,128)S(1)}, s32[2,48,128]{2,1,0:T(8,128)S(1)}) custom-call(f32[4,3,8,128]{3,2,1,0:T(8,128)} %coords.1, s32[4,8,1,32]{3,2,1,0:T(1,128)} %counts.1, s32[1,46]{1,0:T(1,128)} %bitcast.3, s32[4,2,4096]{2,1,0:T(2,128)} %bitcast.2, s32[4,4096]{1,0:T(4,128)} %inter.1), custom_call_target="tpu_custom_call" | custom-call | tf_op jit(solution)/shard_map/gather/pallas_call | solution.py:458
  19.4 29.5 %pairs.1 = (f32[8,4,3,8,128]{4,3,2,1,0:T(8,128)S(1)}, f32[4,4,3,8,128]{4,3,2,1,0:T(8,128)S(1)}) custom-call(s32[96,128]{1,0:T(8,128)S(1)} %get-tuple-element.11.list_ref, s32[2,48,128]{2,1,0:T(8,128)S(1)} %get-tuple-element.12.bounds_ref, f32[8,4,3,8,128]{4,3,2,1,0:T(8,128)S(1)} %get-tuple-element.13.rows_ref, ...), custom_call_target="tpu_custom_call" | custom-call | tf_op jit(solution)/shard_map/pairs/pallas_call | solution.py:435
  48.9 12.2 %scatter.1 = f32[4,3,8,128]{3,2,1,0:T(8,128)S(1)} custom-call(f32[8,4,3,8,128]{4,3,2,1,0:T(8,128)S(1)} %get-tuple-element.15.rows, f32[4,4,3,8,128]{4,3,2,1,0:T(8,128)S(1)} %get-tuple-element.16.cols), custom_call_target="tpu_custom_call" | custom-call | tf_op jit(solution)/shard_map/scatter/pallas_call | solution.py:478
  61.1 0.6 %copy.7 = f32[4,3,8,128]{3,2,1,0:T(8,128)} copy(f32[4,3,8,128]{3,2,1,0:T(8,128)S(1)} %scatter.1) | data formatting | bytes 98304

commit v7 on v6

--- a/solution.py
+++ b/solution.py
@@ -135,29 +135,42 @@
         return pltpu.make_async_remote_copy(source, target, send.at[n], recv.at[n],
                                             device_id=peer, device_id_type=MESH)
 
-    early = []
+    early, talks = [], []
     for d in (1, 3, 2):
         to = lax.rem(y + d, SIDE)
         peer = (to * SIDE + z, c)
         early.append(push(coords.at[to], rows.at[c, y], d, peer))
-        early.append(push(counts.at[to], tallies.at[c, y], SIDE + d, peer))
+        talks.append(push(counts.at[to], tallies.at[c, y], SIDE + d, peer))
     for copy in early:
         copy.start()
+    late = []
+
+    def spread(step):
+        part = lax.rem(y + SIDE - step, SIDE)
+        source = rows.at[c, part] if step else coords.at[y]
+        base = 2 * SIDE + COLS + step * (SIDE + COLS)
+        copies = [push(source, rows.at[c, part], base + SIDE + d, (r, lax.rem(c + d, COLS)))
+                  for d in (4, 2, 6, 1, 3, 5, 7)]
+        copies += [push(source, cols.at[z, part], base + d, (y * SIDE + lax.rem(z + d, SIDE), c))
+                   for d in (1, 3, 2)]
+        for copy in copies:
+            copy.start()
+        late.extend(copies)
+
+    spread(0)
+    for copy in talks:
+        copy.start()
+    for step, copy in zip((1, 3, 2), early):
+        copy.wait_recv()
+        spread(step)
     for copy in kept:
         copy.wait()
-    for copy in early:
-        copy.wait_recv()
     same = pltpu.make_async_copy(rows.at[c], cols.at[z], local.at[4])
     same.start()
-    late = []
-    for d in (1, 3, 2):
-        late.append(push(rows.at[c], cols.at[z], 2 * SIDE + d, (y * SIDE + lax.rem(z + d, SIDE), c)))
-    for d in (4, 2, 6, 1, 3, 5, 7):
-        late.append(push(rows.at[c], rows.at[c], 3 * SIDE + d, (r, lax.rem(c + d, COLS))))
-    talk = []
-    for d in range(1, COLS):
-        talk.append(push(tallies.at[c], tallies.at[c], 3 * SIDE + COLS + d, (r, lax.rem(c + d, COLS))))
-    for copy in late + talk:
+    for copy in talks:
+        copy.wait_recv()
+    talk = [push(tallies.at[c], tallies.at[c], 2 * SIDE + d, (r, lax.rem(c + d, COLS))) for d in range(1, COLS)]
+    for copy in talk:
         copy.start()
     for copy in taken:
         copy.wait()
@@ -169,7 +182,7 @@
             for u in range(U):
                 at = TALLY + k * 8 + yy * 2 + u // 4
                 list_ref[at:at + 1, (u % 4) * 32:(u % 4) * 32 + 32] = tallies[k, yy, u]
-    for copy in early + talk:
+    for copy in early + talks + talk:
         copy.wait_send()
     for copy in late:
         copy.wait()
@@ -190,34 +203,40 @@
         return pltpu.make_async_remote_copy(source, target, send.at[n], recv.at[n],
                                             device_id=peer, device_id_type=MESH)
 
-    for d in (1, 3, 2):
-        to = lax.rem(z + d, SIDE)
-        copies.append(push(cols.at[to], land.at[d - 1], d, (y * SIDE + to, c)))
-    for d in (4, 2, 6, 1, 3, 5, 7):
-        to = lax.rem(c + d, COLS)
-        copies.append(push(rows.at[to], land.at[SIDE - 2 + d], SIDE + d, (r, to)))
-    for copy in copies:
-        copy.start()
+    order = (2, 1, 3, 0)
+    for turn in order:
+        part, base = lax.rem(y + turn, SIDE), turn * (SIDE + COLS)
+        group = []
+        for d in (4, 2, 6, 1, 3, 5, 7):
+            to = lax.rem(c + d, COLS)
+            group.append(push(rows.at[to, part], land.at[SIDE - 2 + d, part], base + SIDE + d, (r, to)))
+        for d in (1, 3, 2):
+            to = lax.rem(z + d, SIDE)
+            group.append(push(cols.at[to, part], land.at[d - 1, part], base + d, (y * SIDE + to, c)))
+        for copy in group:
+            copy.start()
+        copies.append(group)
     for copy in kept:
         copy.wait()
-    for copy in copies:
+    second = []
+    for turn, group in zip(order, copies):
+        part = lax.rem(y + turn, SIDE)
+        for copy in group:
+            copy.wait_recv()
+        sums = [own[0, part] + own[1, part]] + [land[d, part] for d in range(SIDE + COLS - 2)]
+        while len(sums) > 1:
+            sums = [a + b for a, b in zip(sums[::2], sums[1::2])] + sums[len(sums) - len(sums) % 2:]
+        if turn == 0:
+            out[y] = sums[0]
+        else:
+            total[turn - 1] = sums[0]
+            copy = push(total.at[turn - 1], last.at[turn - 1], SIDE * (SIDE + COLS) + turn, (part * SIDE + z, c))
+            copy.start()
+            second.append((turn, copy))
+    for turn, copy in second:
         copy.wait_recv()
-    for i in range(SIDE):
-        sums = own[0, i] + own[1, i]
-        for d in range(SIDE + COLS - 2):
-            sums = sums + land[d, i]
-        total[i] = sums
-    second = []
-    for d in (1, 3, 2):
-        to = lax.rem(y + d, SIDE)
-        second.append(push(total.at[to], last.at[d - 1], SIDE + COLS + d, (to * SIDE + z, c)))
-    for copy in second:
-        copy.start()
-    out[y] = total[y]
-    for d, copy in zip((1, 3, 2), second):
-        copy.wait_recv()
-        out[lax.rem(y + SIDE - d, SIDE)] = last[d - 1]
-    for copy in copies + second:
+        out[lax.rem(y + SIDE - turn, SIDE)] = last[turn - 1]
+    for copy in [copy for group in copies for copy in group] + [copy for _, copy in second]:
         copy.wait_send()
 
 
@@ -454,7 +473,7 @@
     part = coords.shape[1:]
     lens = chrom_lengths.reshape(1, -1)
     flipped = jnp.transpose(inter_pairs, (0, 2, 1))
-    sems = 3 * SIDE + 2 * COLS
+    sems = 2 * SIDE + COLS + SIDE * (SIDE + COLS)
     rows, cols, listing, bounds = pl.pallas_call(
         gather_kernel,
         out_shape=[jax.ShapeDtypeStruct((COLS, SIDE) + part, F32), jax.ShapeDtypeStruct((SIDE, SIDE) + part, F32),
@@ -482,10 +501,10 @@
         scratch_shapes=[
             pltpu.VMEM((SIDE + COLS - 2, SIDE) + part, F32),
             pltpu.VMEM((2, SIDE) + part, F32),
-            pltpu.VMEM((SIDE,) + part, F32),
             pltpu.VMEM((SIDE - 1,) + part, F32),
-            pltpu.SemaphoreType.DMA((2 * SIDE + COLS,)),
-            pltpu.SemaphoreType.DMA((2 * SIDE + COLS,)),
+            pltpu.VMEM((SIDE - 1,) + part, F32),
+            pltpu.SemaphoreType.DMA((SIDE * (SIDE + COLS) + SIDE,)),
+            pltpu.SemaphoreType.DMA((SIDE * (SIDE + COLS) + SIDE,)),
             pltpu.SemaphoreType.DMA((2,)),
         ],
         compiler_params=pltpu.CompilerParams(collective_id=1, has_side_effects=True, vmem_limit_bytes=24 << 20),

time: 62.3 us -> 60.3 us (0.968); the launches traced: 61.8 us -> 60.6 us
  Pallas kernels: 61.1 us -> 59.9 us
    pallas_call x1, Pallas kernels: 29.5 us -> 28.5 us  [pairs_call(): pl.pallas_call(pair_kernel, out_shape=[jax.ShapeDtypeStruct(rows.shape, F...]
    pallas_call x1, Pallas kernels: 19.4 us -> 18.7 us  [on_device(): pl.pallas_call(gather_kernel, out_shape=[jax.ShapeDtypeStruct((COLS, SIDE...]
where the time goes in v7:
time: 60.3 us; the launch traced here: 60.6 us
  Pallas kernels  59.9 us (99%)
  local copies, waits for them, and re-layouts  0.62 us (1%)
    pallas_call x1, Pallas kernels, pairs_call(): pl.pallas_call(pair_kernel, out_shape=[jax.ShapeDtypeStruct(rows.shape, F...  28.5 us
    pallas_call x1, Pallas kernels, on_device(): pl.pallas_call(gather_kernel, out_shape=[jax.ShapeDtypeStruct((COLS, SIDE...  18.7 us
    pallas_call x1, Pallas kernels, on_device(): pl.pallas_call(scatter_kernel, out_shape=jax.ShapeDtypeStruct(coords.shap...  12.8 us

profile of v7, /device:TPU:1, one launch (start us, length us, event | category | flops | bytes accessed | tf_op | source)
XLA Modules:
  0.0 60.6 jit_solution(8986694688305624803)
XLA Ops:
  0.0 18.7 %gather.1 = (f32[8,4,3,8,128]{4,3,2,1,0:T(8,128)S(1)}, f32[4,4,3,8,128]{4,3,2,1,0:T(8,128)S(1)}, s32[96,128]{1,0:T(8,128)S(1)}, s32[2,48,128]{2,1,0:T(8,128)S(1)}) custom-call(f32[4,3,8,128]{3,2,1,0:T(8,128)} %coords.1, s32[4,8,1,32]{3,2,1,0:T(1,128)} %counts.1, s32[1,46]{1,0:T(1,128)} %bitcast.3, s32[4,2,4096]{2,1,0:T(2,128)} %bitcast.2, s32[4,4096]{1,0:T(4,128)} %inter.1), custom_call_target="tpu_custom_call" | custom-call | tf_op jit(solution)/shard_map/gather/pallas_call | solution.py:477
  18.7 28.5 %pairs.1 = (f32[8,4,3,8,128]{4,3,2,1,0:T(8,128)S(1)}, f32[4,4,3,8,128]{4,3,2,1,0:T(8,128)S(1)}) custom-call(s32[96,128]{1,0:T(8,128)S(1)} %get-tuple-element.11.list_ref, s32[2,48,128]{2,1,0:T(8,128)S(1)} %get-tuple-element.12.bounds_ref, f32[8,4,3,8,128]{4,3,2,1,0:T(8,128)S(1)} %get-tuple-element.13.rows_ref, ...), custom_call_target="tpu_custom_call" | custom-call | tf_op jit(solution)/shard_map/pairs/pallas_call | solution.py:454
  47.2 12.8 %scatter.1 = f32[4,3,8,128]{3,2,1,0:T(8,128)S(1)} custom-call(f32[8,4,3,8,128]{4,3,2,1,0:T(8,128)S(1)} %get-tuple-element.15.rows, f32[4,4,3,8,128]{4,3,2,1,0:T(8,128)S(1)} %get-tuple-element.16.cols), custom_call_target="tpu_custom_call" | custom-call | tf_op jit(solution)/shard_map/scatter/pallas_call | solution.py:497
  59.9 0.6 %copy.7 = f32[4,3,8,128]{3,2,1,0:T(8,128)} copy(f32[4,3,8,128]{3,2,1,0:T(8,128)S(1)} %scatter.1) | data formatting | bytes 98304

commit v8 on v7

--- a/solution.py
+++ b/solution.py
@@ -118,8 +118,39 @@
     pl.semaphore_wait(barrier, len(peers))
 
 
-def gather_kernel(coords, counts, lens, pairs, inter, rows, cols, list_ref, bounds_ref,
-                  lens_ref, pairs_ref, inter_ref, stage_ref, tallies, send, recv, local):
+def split3(x):
+    a = x.astype(BF16).astype(F32)
+    b = (x - a).astype(BF16).astype(F32)
+    return a, b, (x - a) - b
+
+
+def points_of(x, y, z):
+    c = 0.75 - 0.25 * (x * x + y * y + z * z)
+    return split3(x), split3(y), split3(z), split3(c)
+
+
+def turn_rows(k, z, rows_ref, bounds_ref, tile_ref, left_ref, lrow_ref):
+    starts, ends = bounds_ref[0], bounds_ref[1]
+    lanes = iota((LABELS, BEADS), 1)
+    for yy in range(SIDE):
+        parts = points_of(rows_ref[k, yy, 0], rows_ref[k, yy, 1], rows_ref[k, yy, 2])
+        for q in range(3):
+            for w in range(4):
+                value = parts[w][q]
+                tile_ref[yy, :, 8 * q + w, :] = 0.5 * value if w < 3 else value
+    for yy in range(SIDE):
+        for u in range(U):
+            at = (k * SIDE + yy) * U + u
+            tiles = [tile_ref[yy, u, 8 * q:8 * q + 8] for q in range(3)]
+            full = jnp.concatenate([tiles[j] for j in (0, 0, 1, 0, 2, 1)], axis=0).astype(BF16)
+            bead = lanes + (u * 128 + (4 * yy + z) * 8 + k) * BEADS
+            hot = jnp.where((bead >= starts) & (bead < ends), 1.0, 0.0).astype(BF16)
+            lrow_ref[at] = jnp.concatenate(tiles[:2], axis=0).astype(BF16)
+            left_ref[at] = jnp.concatenate([full, hot, jnp.zeros((32, 128), BF16)], axis=0).T
+
+
+def gather_kernel(coords, counts, lens, pairs, inter, rows, cols, list_ref, bounds_ref, left_ref, lrow_ref,
+                  lens_ref, pairs_ref, inter_ref, stage_ref, tile_ref, tallies, send, recv, local):
     r, c = lax.axis_index("row"), lax.axis_index("col")
     y, z = r // SIDE, lax.rem(r, SIDE)
     taken = [pltpu.make_async_copy(pairs.at[y], pairs_ref, local.at[0]),
@@ -143,7 +174,7 @@
         talks.append(push(counts.at[to], tallies.at[c, y], SIDE + d, peer))
     for copy in early:
         copy.start()
-    late = []
+    late, across = [], []
 
     def spread(step):
         part = lax.rem(y + SIDE - step, SIDE)
@@ -155,7 +186,8 @@
                    for d in (1, 3, 2)]
         for copy in copies:
             copy.start()
-        late.extend(copies)
+        across.extend(copies[:COLS - 1])
+        late.extend(copies[COLS - 1:])
 
     spread(0)
     for copy in talks:
@@ -182,7 +214,24 @@
             for u in range(U):
                 at = TALLY + k * 8 + yy * 2 + u // 4
                 list_ref[at:at + 1, (u % 4) * 32:(u % 4) * 32 + 32] = tallies[k, yy, u]
-    for copy in early + talks + talk:
+    for v in range(SIDE):
+        for u in range(U):
+            for q in range(3):
+                tile_ref[v, u, 8 * q:8 * q + 8] = jnp.zeros((8, 128), F32)
+    for v in range(SIDE):
+        tile_ref[v, :, 4, :] = jnp.ones((8, 128), F32)
+    turn_rows(c, z, rows, bounds_ref, tile_ref, left_ref, lrow_ref)
+
+    def land(d, carry):
+        k = lax.rem(c + COLS - d, COLS)
+        for step in range(SIDE):
+            n = 2 * SIDE + COLS + step * (SIDE + COLS) + SIDE + d
+            push(coords.at[0], rows.at[k, lax.rem(y + SIDE - step, SIDE)], n, (r, lax.rem(c + d, COLS))).wait_recv()
+        turn_rows(k, z, rows, bounds_ref, tile_ref, left_ref, lrow_ref)
+        return carry
+
+    lax.fori_loop(1, COLS, land, 0)
+    for copy in early + talks + talk + across:
         copy.wait_send()
     for copy in late:
         copy.wait()
@@ -240,23 +289,11 @@
         copy.wait_send()
 
 
-def split3(x):
-    a = x.astype(BF16).astype(F32)
-    b = (x - a).astype(BF16).astype(F32)
-    return a, b, (x - a) - b
-
-
-def points_of(x, y, z):
-    c = 0.75 - 0.25 * (x * x + y * y + z * z)
-    return split3(x), split3(y), split3(z), split3(c)
-
-
-def pair_kernel(list_ref, bounds_ref, rows_ref, cols_ref, prow_ref, pcol_ref,
-                tile_ref, left_ref, lrow_ref, same_ref, differ_ref, arow_ref, acol_ref):
+def pair_kernel(list_ref, bounds_ref, rows_ref, cols_ref, left_ref, lrow_ref, prow_ref, pcol_ref,
+                tile_ref, same_ref, differ_ref, arow_ref, acol_ref):
     z, c = list_ref[PLACE, 0], list_ref[PLACE, 1]
     starts, ends = bounds_ref[0], bounds_ref[1]
     lanes = iota((LABELS, BEADS), 1)
-    eye = flag(iota((128, 128), 0) == iota((128, 128), 1))
     one = jnp.ones((8, 128), F32)
     nil = jnp.zeros((8, 128), F32)
 
@@ -268,35 +305,9 @@
         for u in range(U):
             for q in range(3):
                 tile_ref[v, u, 8 * q:8 * q + 8] = nil
-    for v in range(SIDE):
-        tile_ref[v, :, 4, :] = one
-
-    @pl.loop(0, COLS)
-    def _(k):
-        for yy in range(SIDE):
-            parts = points_of(rows_ref[k, yy, 0], rows_ref[k, yy, 1], rows_ref[k, yy, 2])
-            for q in range(3):
-                for w in range(4):
-                    value = parts[w][q]
-                    tile_ref[yy, :, 8 * q + w, :] = 0.5 * value if w < 3 else value
-        for yy in range(SIDE):
-            for u in range(0, U, 2):
-                fulls = []
-                for i in range(2):
-                    at = (k * SIDE + yy) * U + u + i
-                    tiles = [tile_ref[yy, u + i, 8 * q:8 * q + 8] for q in range(3)]
-                    full = jnp.concatenate([tiles[j] for j in (0, 0, 1, 0, 2, 1)], axis=0).astype(BF16)
-                    hot = hot_of((u + i) * 128 + (4 * yy + z) * 8 + k)
-                    fulls += [full, jnp.where(hot, 1.0, 0.0).astype(BF16), jnp.zeros((32, 128), BF16)]
-                    lrow_ref[at] = jnp.concatenate(tiles[:2], axis=0).astype(BF16)
-                flipped = [jnp.concatenate(fulls[i * 3:i * 3 + 3], axis=0).T for i in range(2)]
-                for i in range(2):
-                    left_ref[(k * SIDE + yy) * U + u + i] = flipped[i]
 
     for v in range(SIDE):
         tile_ref[v, :, 3, :] = one
-        tile_ref[v, :, 11, :] = nil
-        tile_ref[v, :, 19, :] = nil
 
     @pl.loop(0, SIDE)
     def _(zz):
@@ -450,15 +461,13 @@
                 pcol_ref[zz, yy, w] = pulled * (-1.0 / 512.0)
 
 
-def pairs_call(listing, bounds, rows, cols):
+def pairs_call(listing, bounds, rows, cols, left, lrow):
     return pl.pallas_call(
         pair_kernel,
         out_shape=[jax.ShapeDtypeStruct(rows.shape, F32), jax.ShapeDtypeStruct(cols.shape, F32)],
-        in_specs=[SMEM] + [VMEM] * 3, out_specs=[VMEM] * 2,
+        in_specs=[SMEM] + [VMEM] * 5, out_specs=[VMEM] * 2,
         scratch_shapes=[
             pltpu.VMEM((SIDE, U, 24, BEADS), F32),
-            pltpu.VMEM((NR, BEADS, 128), BF16),
-            pltpu.VMEM((NR, 16, BEADS), BF16),
             pltpu.VMEM((NC + PAD + 2, 2 * LABELS, BEADS), BF16),
             pltpu.VMEM((NC + 1, 2 * LABELS, BEADS), BF16),
             pltpu.VMEM((NR, 8, BEADS), F32),
@@ -466,7 +475,7 @@
         ],
         compiler_params=pltpu.CompilerParams(vmem_limit_bytes=32 << 20),
         name="pairs",
-    )(listing, bounds, rows, cols)
+    )(listing, bounds, rows, cols, left, lrow)
 
 
 def on_device(coords, chrom_lengths, band_counts, inter_pairs, inter_counts):
@@ -474,16 +483,18 @@
     lens = chrom_lengths.reshape(1, -1)
     flipped = jnp.transpose(inter_pairs, (0, 2, 1))
     sems = 2 * SIDE + COLS + SIDE * (SIDE + COLS)
-    rows, cols, listing, bounds = pl.pallas_call(
+    rows, cols, listing, bounds, left, lrow = pl.pallas_call(
         gather_kernel,
         out_shape=[jax.ShapeDtypeStruct((COLS, SIDE) + part, F32), jax.ShapeDtypeStruct((SIDE, SIDE) + part, F32),
-                   jax.ShapeDtypeStruct((LINES, 128), I32), jax.ShapeDtypeStruct((2, LABELS, BEADS), I32)],
-        in_specs=[HBM] * 5, out_specs=[VMEM] * 4,
+                   jax.ShapeDtypeStruct((LINES, 128), I32), jax.ShapeDtypeStruct((2, LABELS, BEADS), I32),
+                   jax.ShapeDtypeStruct((NR, BEADS, 128), BF16), jax.ShapeDtypeStruct((NR, 16, BEADS), BF16)],
+        in_specs=[HBM] * 5, out_specs=[VMEM] * 6,
         scratch_shapes=[
             pltpu.VMEM(lens.shape, I32),
             pltpu.VMEM(flipped.shape[1:], I32),
             pltpu.VMEM(inter_counts.shape, I32),
             pltpu.VMEM((3, 32, 128), I32),
+            pltpu.VMEM((SIDE, U, 24, BEADS), F32),
             pltpu.VMEM((COLS,) + band_counts.shape, I32),
             pltpu.SemaphoreType.DMA((sems,)),
             pltpu.SemaphoreType.DMA((sems,)),
@@ -493,7 +504,7 @@
         name="gather",
     )(*[pltpu.with_memory_space_constraint(v, pltpu.HBM)
         for v in (coords, band_counts, lens, flipped, inter_counts)])
-    prow, pcol = pairs_call(listing, bounds, rows, cols)
+    prow, pcol = pairs_call(listing, bounds, rows, cols, left, lrow)
     return pl.pallas_call(
         scatter_kernel,
         out_shape=jax.ShapeDtypeStruct(coords.shape, F32),

time: 60.3 us -> 60.8 us (level)
    pallas_call x1, Pallas kernels: 18.7 us -> 22.4 us  [on_device(): pl.pallas_call(gather_kernel, out_shape=[jax.ShapeDtypeStruct((COLS, SIDE...]
    pallas_call x1, Pallas kernels: 28.5 us -> 26.2 us  [pairs_call(): pl.pallas_call(pair_kernel, out_shape=[jax.ShapeDtypeStruct(rows.shape, F...]
    pallas_call x1, Pallas kernels: 12.8 us -> 11.8 us  [on_device(): pl.pallas_call(scatter_kernel, out_shape=jax.ShapeDtypeStruct(coords.shap...]
where the time goes in v8:
time: 60.8 us; the launch traced here: 61.1 us
  Pallas kernels  60.4 us (99%)
  local copies, waits for them, and re-layouts  0.62 us (1%)
    pallas_call x1, Pallas kernels, pairs_call(): pl.pallas_call(pair_kernel, out_shape=[jax.ShapeDtypeStruct(rows.shape, F...  26.2 us
    pallas_call x1, Pallas kernels, on_device(): pl.pallas_call(gather_kernel, out_shape=[jax.ShapeDtypeStruct((COLS, SIDE...  22.4 us
    pallas_call x1, Pallas kernels, on_device(): pl.pallas_call(scatter_kernel, out_shape=jax.ShapeDtypeStruct(coords.shap...  11.8 us

profile of v8, /device:TPU:1, one launch (start us, length us, event | category | flops | bytes accessed | tf_op | source)
XLA Modules:
  0.0 61.1 jit_solution(10951093492870960594)
XLA Ops:
  0.0 22.4 %gather.1 = (f32[8,4,3,8,128]{4,3,2,1,0:T(8,128)S(1)}, f32[4,4,3,8,128]{4,3,2,1,0:T(8,128)S(1)}, s32[96,128]{1,0:T(8,128)S(1)}, s32[2,48,128]{2,1,0:T(8,128)S(1)...) custom-call(f32[4,3,8,128]{3,2,1,0:T(8,128)} %coords.1, s32[4,8,1,32]{3,2,1,0:T(1,128)} %counts.1, ...), custom_call_target="tpu_custom_call" | custom-call | tf_op jit(solution)/shard_map/gather/pallas_call | solution.py:486
  22.4 26.2 %pairs.1 = (f32[8,4,3,8,128]{4,3,2,1,0:T(8,128)S(1)}, f32[4,4,3,8,128]{4,3,2,1,0:T(8,128)S(1)}) custom-call(s32[96,128]{1,0:T(8,128)S(1)} %get-tuple-element.13.list_ref, s32[2,48,128]{2,1,0:T(8,128)S(1)} %get-tuple-element.14.bounds_ref, f32[8,4,3,8,128]{4,3,2,1,0:T(8,128)S(1)} %get-tuple-element.15.rows_ref, ...), custom_call_target="tpu_custom_call" | custom-call | tf_op jit(solution)/shard_map/pairs/pallas_call | solution.py:465
  48.6 11.8 %scatter.1 = f32[4,3,8,128]{3,2,1,0:T(8,128)S(1)} custom-call(f32[8,4,3,8,128]{4,3,2,1,0:T(8,128)S(1)} %get-tuple-element.19.rows, f32[4,4,3,8,128]{4,3,2,1,0:T(8,128)S(1)} %get-tuple-element.20.cols), custom_call_target="tpu_custom_call" | custom-call | tf_op jit(solution)/shard_map/scatter/pallas_call | solution.py:508
  60.5 0.6 %copy.7 = f32[4,3,8,128]{3,2,1,0:T(8,128)} copy(f32[4,3,8,128]{3,2,1,0:T(8,128)S(1)} %scatter.1) | data formatting | bytes 98304

commit v9 on v8

--- a/solution.py
+++ b/solution.py
@@ -61,7 +61,7 @@
     return acc[0:8]
 
 
-def make_list(y, z, c, lens_ref, pairs_ref, count_ref, stage_ref, out_ref, bounds_ref):
+def make_list(y, z, c, pairs_ref, count_ref, stage_ref, out_ref):
     for t in range(32):
         lane = slice(t * 128, t * 128 + 128)
         stage_ref[0, t:t + 1, :] = pairs_ref[0:1, lane]
@@ -76,7 +76,11 @@
     found = (acc + spare).astype(I32)
     out_ref[LISTED:LISTED + 8, :] = found[:, 0:128]
     out_ref[LISTED + 8:LISTED + 16, :] = found[:, 128:256]
-
+    listed = jnp.sum(found[3:4].astype(F32), axis=1, keepdims=True).astype(I32)
+    out_ref[TOTALS:TOTALS + 1, :] = jnp.where(iota((1, 128), 1) == 0, listed, out_ref[TOTALS:TOTALS + 1, :])
+
+
+def make_units(z, c, lens_ref, out_ref, bounds_ref):
     starts, ends = chrom_bounds(lens_ref)
     bounds_ref[0] = jnp.broadcast_to(starts, (LABELS, BEADS))
     bounds_ref[1] = jnp.broadcast_to(ends, (LABELS, BEADS))
@@ -98,10 +102,9 @@
     for i in range(4):
         out_ref[UNIT + i:UNIT + i + 1, :] = units[:, i * 128:i * 128 + 128].astype(I32)
     out_ref[UNIT + 4:UNIT + 8, :] = jnp.zeros((4, 128), I32)
-    listed = jnp.sum(found[3:4].astype(F32), axis=1, keepdims=True).astype(I32)
     active = jnp.sum(acc[2:3], axis=1, keepdims=True).astype(I32)
     lane = iota((1, 128), 1)
-    out_ref[TOTALS:TOTALS + 1, :] = jnp.where(lane == 0, listed, active)
+    out_ref[TOTALS:TOTALS + 1, :] = jnp.broadcast_to(active, (1, 128))
     out_ref[WIDTHS:WIDTHS + 2, :] = jnp.zeros((2, 128), I32)
     out_ref[PLACE:PLACE + 1, :] = jnp.where(lane == 0, z, c)
     out_ref[PLACE + 1:TALLY, :] = jnp.zeros((4, 128), I32)
@@ -192,6 +195,14 @@
     spread(0)
     for copy in talks:
         copy.start()
+    taken[2].wait()
+    make_units(z, c, lens_ref, list_ref, bounds_ref)
+    for v in range(SIDE):
+        for u in range(U):
+            for q in range(3):
+                tile_ref[v, u, 8 * q:8 * q + 8] = jnp.zeros((8, 128), F32)
+    for v in range(SIDE):
+        tile_ref[v, :, 4, :] = jnp.ones((8, 128), F32)
     for step, copy in zip((1, 3, 2), early):
         copy.wait_recv()
         spread(step)
@@ -204,9 +215,20 @@
     talk = [push(tallies.at[c], tallies.at[c], 2 * SIDE + d, (r, lax.rem(c + d, COLS))) for d in range(1, COLS)]
     for copy in talk:
         copy.start()
-    for copy in taken:
+    for copy in taken[:2]:
         copy.wait()
-    make_list(y, z, c, lens_ref, pairs_ref, inter_ref, stage_ref, list_ref, bounds_ref)
+    make_list(y, z, c, pairs_ref, inter_ref, stage_ref, list_ref)
+    turn_rows(c, z, rows, bounds_ref, tile_ref, left_ref, lrow_ref)
+
+    def land(d, carry):
+        k = lax.rem(c + COLS - d, COLS)
+        for step in range(SIDE):
+            n = 2 * SIDE + COLS + step * (SIDE + COLS) + SIDE + d
+            push(coords.at[0], rows.at[k, lax.rem(y + SIDE - step, SIDE)], n, (r, lax.rem(c + d, COLS))).wait_recv()
+        turn_rows(k, z, rows, bounds_ref, tile_ref, left_ref, lrow_ref)
+        return carry
+
+    lax.fori_loop(1, COLS, land, 0)
     for copy in talk:
         copy.wait_recv()
     for k in range(COLS):
@@ -214,23 +236,6 @@
             for u in range(U):
                 at = TALLY + k * 8 + yy * 2 + u // 4
                 list_ref[at:at + 1, (u % 4) * 32:(u % 4) * 32 + 32] = tallies[k, yy, u]
-    for v in range(SIDE):
-        for u in range(U):
-            for q in range(3):
-                tile_ref[v, u, 8 * q:8 * q + 8] = jnp.zeros((8, 128), F32)
-    for v in range(SIDE):
-        tile_ref[v, :, 4, :] = jnp.ones((8, 128), F32)
-    turn_rows(c, z, rows, bounds_ref, tile_ref, left_ref, lrow_ref)
-
-    def land(d, carry):
-        k = lax.rem(c + COLS - d, COLS)
-        for step in range(SIDE):
-            n = 2 * SIDE + COLS + step * (SIDE + COLS) + SIDE + d
-            push(coords.at[0], rows.at[k, lax.rem(y + SIDE - step, SIDE)], n, (r, lax.rem(c + d, COLS))).wait_recv()
-        turn_rows(k, z, rows, bounds_ref, tile_ref, left_ref, lrow_ref)
-        return carry
-
-    lax.fori_loop(1, COLS, land, 0)
     for copy in early + talks + talk + across:
         copy.wait_send()
     for copy in late:

time: 60.8 us -> 57.8 us (0.951); the launches traced: 61.1 us -> 56.7 us
  Pallas kernels: 60.4 us -> 56 us
    pallas_call x1, Pallas kernels: 22.4 us -> 20.1 us  [on_device(): pl.pallas_call(gather_kernel, out_shape=[jax.ShapeDtypeStruct((COLS, SIDE...]
    pallas_call x1, Pallas kernels: 26.2 us -> 24.8 us  [pairs_call(): pl.pallas_call(pair_kernel, out_shape=[jax.ShapeDtypeStruct(rows.shape, F...]
    pallas_call x1, Pallas kernels: 11.8 us -> 11.1 us  [on_device(): pl.pallas_call(scatter_kernel, out_shape=jax.ShapeDtypeStruct(coords.shap...]
where the time goes in v9:
time: 57.8 us; the launch traced here: 56.7 us
  Pallas kernels  56 us (97%)
  local copies, waits for them, and re-layouts  0.62 us (1%)
    pallas_call x1, Pallas kernels, pairs_call(): pl.pallas_call(pair_kernel, out_shape=[jax.ShapeDtypeStruct(rows.shape, F...  24.8 us
    pallas_call x1, Pallas kernels, on_device(): pl.pallas_call(gather_kernel, out_shape=[jax.ShapeDtypeStruct((COLS, SIDE...  20.1 us
    pallas_call x1, Pallas kernels, on_device(): pl.pallas_call(scatter_kernel, out_shape=jax.ShapeDtypeStruct(coords.shap...  11.1 us

profile of v9, /device:TPU:1, one launch (start us, length us, event | category | flops | bytes accessed | tf_op | source)
XLA Modules:
  0.0 56.7 jit_solution(12957076243059012894)
XLA Ops:
  0.0 20.1 %gather.1 = (f32[8,4,3,8,128]{4,3,2,1,0:T(8,128)S(1)}, f32[4,4,3,8,128]{4,3,2,1,0:T(8,128)S(1)}, s32[96,128]{1,0:T(8,128)S(1)}, s32[2,48,128]{2,1,0:T(8,128)S(1)...) custom-call(f32[4,3,8,128]{3,2,1,0:T(8,128)} %coords.1, s32[4,8,1,32]{3,2,1,0:T(1,128)} %counts.1, ...), custom_call_target="tpu_custom_call" | custom-call | tf_op jit(solution)/shard_map/gather/pallas_call | solution.py:491
  20.1 24.8 %pairs.1 = (f32[8,4,3,8,128]{4,3,2,1,0:T(8,128)S(1)}, f32[4,4,3,8,128]{4,3,2,1,0:T(8,128)S(1)}) custom-call(s32[96,128]{1,0:T(8,128)S(1)} %get-tuple-element.13.list_ref, s32[2,48,128]{2,1,0:T(8,128)S(1)} %get-tuple-element.14.bounds_ref, f32[8,4,3,8,128]{4,3,2,1,0:T(8,128)S(1)} %get-tuple-element.15.rows_ref, ...), custom_call_target="tpu_custom_call" | custom-call | tf_op jit(solution)/shard_map/pairs/pallas_call | solution.py:470
  44.9 11.1 %scatter.1 = f32[4,3,8,128]{3,2,1,0:T(8,128)S(1)} custom-call(f32[8,4,3,8,128]{4,3,2,1,0:T(8,128)S(1)} %get-tuple-element.19.rows, f32[4,4,3,8,128]{4,3,2,1,0:T(8,128)S(1)} %get-tuple-element.20.cols), custom_call_target="tpu_custom_call" | custom-call | tf_op jit(solution)/shard_map/scatter/pallas_call | solution.py:513
  56.1 0.6 %copy.7 = f32[4,3,8,128]{3,2,1,0:T(8,128)} copy(f32[4,3,8,128]{3,2,1,0:T(8,128)S(1)} %scatter.1) | data formatting | bytes 98304

commit v10 on v9

--- a/solution.py
+++ b/solution.py
@@ -14,7 +14,7 @@
 UNITS = 2 * NR
 PAD = 4
 WIDE = 4
-LONG, SHORT = 12, 2
+LONG, SHORT = 16, 2
 BIG = 64.0
 F32, BF16, I32 = jnp.float32, jnp.bfloat16, jnp.int32
 HBM = pl.BlockSpec(memory_space=pltpu.HBM)

time: 57.8 us -> 58.1 us (level)
  Pallas kernels: 56 us -> 56.9 us
    pallas_call x1, Pallas kernels: 24.8 us -> 26 us  [pairs_call(): pl.pallas_call(pair_kernel, out_shape=[jax.ShapeDtypeStruct(rows.shape, F...]
where the time goes in v10:
time: 58.1 us; the launch traced here: 57.6 us
  Pallas kernels  56.9 us (98%)
  local copies, waits for them, and re-layouts  0.62 us (1%)
    pallas_call x1, Pallas kernels, pairs_call(): pl.pallas_call(pair_kernel, out_shape=[jax.ShapeDtypeStruct(rows.shape, F...  26 us
    pallas_call x1, Pallas kernels, on_device(): pl.pallas_call(gather_kernel, out_shape=[jax.ShapeDtypeStruct((COLS, SIDE...  20.1 us
    pallas_call x1, Pallas kernels, on_device(): pl.pallas_call(scatter_kernel, out_shape=jax.ShapeDtypeStruct(coords.shap...  10.8 us

profile of v10, /device:TPU:1, one launch (start us, length us, event | category | flops | bytes accessed | tf_op | source)
XLA Modules:
  0.0 57.6 jit_solution(12664548251695784403)
XLA Ops:
  0.0 20.1 %gather.1 = (f32[8,4,3,8,128]{4,3,2,1,0:T(8,128)S(1)}, f32[4,4,3,8,128]{4,3,2,1,0:T(8,128)S(1)}, s32[96,128]{1,0:T(8,128)S(1)}, s32[2,48,128]{2,1,0:T(8,128)S(1)...) custom-call(f32[4,3,8,128]{3,2,1,0:T(8,128)} %coords.1, s32[4,8,1,32]{3,2,1,0:T(1,128)} %counts.1, ...), custom_call_target="tpu_custom_call" | custom-call | tf_op jit(solution)/shard_map/gather/pallas_call | solution.py:491
  20.1 26.0 %pairs.1 = (f32[8,4,3,8,128]{4,3,2,1,0:T(8,128)S(1)}, f32[4,4,3,8,128]{4,3,2,1,0:T(8,128)S(1)}) custom-call(s32[96,128]{1,0:T(8,128)S(1)} %get-tuple-element.13.list_ref, s32[2,48,128]{2,1,0:T(8,128)S(1)} %get-tuple-element.14.bounds_ref, f32[8,4,3,8,128]{4,3,2,1,0:T(8,128)S(1)} %get-tuple-element.15.rows_ref, ...), custom_call_target="tpu_custom_call" | custom-call | tf_op jit(solution)/shard_map/pairs/pallas_call | solution.py:470
  46.1 10.8 %scatter.1 = f32[4,3,8,128]{3,2,1,0:T(8,128)S(1)} custom-call(f32[8,4,3,8,128]{4,3,2,1,0:T(8,128)S(1)} %get-tuple-element.19.rows, f32[4,4,3,8,128]{4,3,2,1,0:T(8,128)S(1)} %get-tuple-element.20.cols), custom_call_target="tpu_custom_call" | custom-call | tf_op jit(solution)/shard_map/scatter/pallas_call | solution.py:513
  56.9 0.6 %copy.7 = f32[4,3,8,128]{3,2,1,0:T(8,128)} copy(f32[4,3,8,128]{3,2,1,0:T(8,128)S(1)} %scatter.1) | data formatting | bytes 98304

commit v11 on v10

--- a/solution.py
+++ b/solution.py
@@ -14,7 +14,7 @@
 UNITS = 2 * NR
 PAD = 4
 WIDE = 4
-LONG, SHORT = 16, 2
+LONG, SHORT = 16, 4
 BIG = 64.0
 F32, BF16, I32 = jnp.float32, jnp.bfloat16, jnp.int32
 HBM = pl.BlockSpec(memory_space=pltpu.HBM)

time: 58.1 us -> 57.6 us (level)
  no operation moved by 1% of the time
where the time goes in v11:
time: 57.6 us; the launch traced here: 57.2 us
  Pallas kernels  56.6 us (98%)
  local copies, waits for them, and re-layouts  0.62 us (1%)
    pallas_call x1, Pallas kernels, pairs_call(): pl.pallas_call(pair_kernel, out_shape=[jax.ShapeDtypeStruct(rows.shape, F...  25.9 us
    pallas_call x1, Pallas kernels, on_device(): pl.pallas_call(gather_kernel, out_shape=[jax.ShapeDtypeStruct((COLS, SIDE...  20.1 us
    pallas_call x1, Pallas kernels, on_device(): pl.pallas_call(scatter_kernel, out_shape=jax.ShapeDtypeStruct(coords.shap...  10.5 us

profile of v11, /device:TPU:1, one launch (start us, length us, event | category | flops | bytes accessed | tf_op | source)
XLA Modules:
  0.0 57.2 jit_solution(17474031577152821333)
XLA Ops:
  0.0 20.1 %gather.1 = (f32[8,4,3,8,128]{4,3,2,1,0:T(8,128)S(1)}, f32[4,4,3,8,128]{4,3,2,1,0:T(8,128)S(1)}, s32[96,128]{1,0:T(8,128)S(1)}, s32[2,48,128]{2,1,0:T(8,128)S(1)...) custom-call(f32[4,3,8,128]{3,2,1,0:T(8,128)} %coords.1, s32[4,8,1,32]{3,2,1,0:T(1,128)} %counts.1, ...), custom_call_target="tpu_custom_call" | custom-call | tf_op jit(solution)/shard_map/gather/pallas_call | solution.py:491
  20.1 25.9 %pairs.1 = (f32[8,4,3,8,128]{4,3,2,1,0:T(8,128)S(1)}, f32[4,4,3,8,128]{4,3,2,1,0:T(8,128)S(1)}) custom-call(s32[96,128]{1,0:T(8,128)S(1)} %get-tuple-element.13.list_ref, s32[2,48,128]{2,1,0:T(8,128)S(1)} %get-tuple-element.14.bounds_ref, f32[8,4,3,8,128]{4,3,2,1,0:T(8,128)S(1)} %get-tuple-element.15.rows_ref, ...), custom_call_target="tpu_custom_call" | custom-call | tf_op jit(solution)/shard_map/pairs/pallas_call | solution.py:470
  46.0 10.5 %scatter.1 = f32[4,3,8,128]{3,2,1,0:T(8,128)S(1)} custom-call(f32[8,4,3,8,128]{4,3,2,1,0:T(8,128)S(1)} %get-tuple-element.19.rows, f32[4,4,3,8,128]{4,3,2,1,0:T(8,128)S(1)} %get-tuple-element.20.cols), custom_call_target="tpu_custom_call" | custom-call | tf_op jit(solution)/shard_map/scatter/pallas_call | solution.py:513
  56.6 0.6 %copy.7 = f32[4,3,8,128]{3,2,1,0:T(8,128)} copy(f32[4,3,8,128]{3,2,1,0:T(8,128)S(1)} %scatter.1) | data formatting | bytes 98304
